TPU v7x, 32 devices: a whole 2x2x4 slice. The times are simulated.
32 devices in a mesh: azim: 8 (over y, x, core), radax: 4 (over z).
Axes of the slice: x: 2, y: 2, z: 4, core: 2. Of those that a mesh axis runs over, the one named last changes fastest.
Arguments:
- gas: float32 [14, 32, 128, 128], P(None, 'azim', 'radax'), may hold values from -6 to 6
- transport: float32 [3, 14], replicated, may hold values from 0.02 to 0.12
- chemistry: float32 [14, 14], replicated, may hold values from -1.2 to 1.2
- evap_weight: float32 [14], replicated, may hold values from -1.5 to 1.5
- source_map: float32 [14, 8], replicated, may hold values from -2 to 2
- parcel_mass: float32 [8, 4, 2048], P('azim', 'radax'), may hold values from 0.2 to 2
- parcel_state: float32 [7, 8, 4, 2048], P(None, 'azim', 'radax'), may hold values from -6 to 6
- parcel_host: int32 [8, 4, 2048], P('azim', 'radax'), may hold values from 0 to 16383
- parcel_count: int32 [8, 4], P('azim', 'radax'), may hold values from 384 to 1536, as said below
- crossing: int32 [8, 4, 2, 2, 128], P('azim', 'radax'), may hold values from 0 to 2048, as said below
Outputs:
- gas_next: float32 [14, 32, 128, 128], P(None, 'azim', 'radax')
- mass_next: float32 [8, 4, 2048], P('azim', 'radax')
- state_next: float32 [7, 8, 4, 2048], P(None, 'azim', 'radax')
- host_next: int32 [8, 4, 2048], P('azim', 'radax')
- count_next: int32 [8, 4], P('azim', 'radax')
Inputs may be any that keep to these rules, and one draw needn't show every extreme that they name: `parcel_count`: every device's count lies in 1536 halved zero, one or two times; some device holds exactly 1536. `crossing`: each list holds 64 to 128 distinct ascending slots below 2048, then the value 2048; the four lists of a device are disjoint. In every draw a list of each section and direction is full on some device, and some device with the largest count receives full lists from both neighbours in both sections.
All inputs are finite; a program needn't handle non-finite values.
Results may differ from a plain program's by a relative error of at most 0.0009.
Values sent between devices are 32-bit elements; how exact they have to be, the bound alone decides.
No kernel may reach another device: no remote copies, remote signals or barrier semaphores. Data moves between devices by JAX's collectives and lax.ppermute only.
A program may use at most 64 MiB of HBM per device.

v0:
```python
import jax
import jax.numpy as jnp
from jax import lax
from jax.sharding import PartitionSpec as P

HIGH = lax.Precision.HIGHEST
DT = 0.5
RELAX = 0.3
EVAP = 0.5
LANES = 128


def padded(array, sides, width, wrap):
    for axis, dim in sides:
        size, length = (lax.axis_size(axis), array.shape[dim])
        up = [(i, (i + 1) % size) for i in range(size if wrap else size - 1)]
        down = [(j, i) for i, j in up]
        last = lax.slice_in_dim(array, length - width, length, axis=dim)
        first = lax.slice_in_dim(array, 0, width, axis=dim)
        before = lax.ppermute(last, axis, up)
        after = lax.ppermute(first, axis, down)
        array = jnp.concatenate([before, array, after], axis=dim)
    return array


def passed_along(array, axis, by):
    size = lax.axis_size(axis)
    return lax.ppermute(array, axis, [(i, (i + by) % size) for i in range(size)])


def spatial_rhs(field, sector_pad, block_pad, transport, chemistry):
    east = sector_pad[:, 2:]
    west = sector_pad[:, :-2]
    north = block_pad[:, :, 2:]
    south = block_pad[:, :, :-2]
    axial_pad = jnp.pad(field, ((0, 0), (0, 0), (0, 0), (1, 1)))
    upper = axial_pad[..., 2:]
    lower = axial_pad[..., :-2]
    lap = east + west + north + south + upper + lower - 6.0 * field
    diffuse = transport[0][:, None, None, None]
    swirl = transport[1][:, None, None, None]
    axial = transport[2][:, None, None, None]
    chem = jnp.einsum("fg,gabz->fabz", chemistry, jnp.tanh(field), precision=HIGH)
    return diffuse * lap - swirl * 0.5 * (east - west) - axial * 0.5 * (upper - lower) + chem


def split_three(values):
    first = values.astype(jnp.bfloat16)
    rest = values - lax.optimization_barrier(first).astype(jnp.float32)
    second = rest.astype(jnp.bfloat16)
    third = (rest - lax.optimization_barrier(second).astype(jnp.float32)).astype(jnp.bfloat16)
    return jnp.stack([first, second, third], axis=0)


def block_tables(host_block, upper_rows):
    upper_ids = host_block // LANES
    lower_ids = host_block % LANES
    upper_hot = (jnp.arange(upper_rows, dtype=jnp.int32)[:, None] == upper_ids[None, :]).astype(
        jnp.bfloat16
    )
    lower_hot = jnp.arange(LANES, dtype=jnp.int32)[:, None] == lower_ids[None, :]
    return (upper_hot, lower_hot)


def parcel_physics(field, mass, state, host, live, evap_weight, source_map):
    fields = field.shape[0]
    slots = mass.shape[0]
    width = min(slots, 512)
    nblocks = slots // width
    cells = field.shape[1] * field.shape[2] * field.shape[3]
    upper_rows = cells // LANES
    pieces = split_three(field.reshape(fields, upper_rows, LANES))
    host_blocks = host.reshape(nblocks, width)

    def probe_block(carry, host_block):
        upper_hot, lower_hot = block_tables(host_block, upper_rows)
        spread = jnp.einsum("sfhl,hp->flp", pieces, upper_hot, preferred_element_type=jnp.float32)
        picked = jnp.sum(jnp.where(lower_hot[None], spread, 0.0), axis=1)
        return (carry, picked)

    unused, probe_blocks = lax.scan(probe_block, jnp.zeros((), jnp.float32), host_blocks)
    probe = jnp.moveaxis(probe_blocks, 0, 1).reshape(fields, slots)
    sig = jax.nn.sigmoid(jnp.dot(evap_weight, probe, precision=HIGH) + state[0])
    mdot = EVAP * mass * sig * live
    attr = jnp.concatenate([mass[None], state], axis=0)
    source = jnp.dot(source_map, attr, precision=HIGH) * mdot
    source_blocks = jnp.moveaxis(source.reshape(fields, nblocks, width), 1, 0)

    def deposit_block(total, inputs):
        host_block, source_block = inputs
        upper_hot, lower_hot = block_tables(host_block, upper_rows)
        parts = split_three(source_block)
        laid = parts[:, :, None, :] * lower_hot.astype(jnp.bfloat16)[None, None]
        return (
            total + jnp.einsum("sflp,hp->fhl", laid, upper_hot, preferred_element_type=jnp.float32),
            None,
        )

    empty = jnp.zeros((fields, upper_rows, LANES), jnp.float32)
    deposit, unused = lax.scan(deposit_block, empty, (host_blocks, source_blocks))
    deposit = deposit.reshape(field.shape)
    new_mass = mass - DT * mdot
    temper = state[0:1] + DT * RELAX * (probe[4:5] - state[0:1])
    speeds = state[1:4] + DT * RELAX * (probe[1:4] - state[1:4])
    new_state = jnp.concatenate([temper, speeds, state[4:]], axis=0)
    return (deposit, new_mass, new_state)


def depart(mass, state, host, live, lists, span):
    slots = mass.shape[0]
    valid = lists < slots
    safe = jnp.where(valid, lists, 0)
    attr = jnp.concatenate([mass[None], state], axis=0)
    block = jnp.take(attr, safe, axis=1) * valid.astype(jnp.float32)
    host_row = jnp.where(valid, jnp.take(host, safe) % span, -1).astype(jnp.float32)
    packed = jnp.concatenate([block, host_row[None]], axis=0)
    slot_ids = jnp.arange(slots, dtype=jnp.int32)
    leaving = jnp.any(slot_ids[:, None] == lists.reshape(1, -1), axis=1)
    live = jnp.where(leaving, 0.0, live)
    return (packed[:, 1], packed[:, 0], live)


def place(attr, host, live, packed, start, offset):
    length = packed.shape[1]
    cells = packed[-1].astype(jnp.int32)
    valid = cells >= 0
    old_attr = lax.dynamic_slice_in_dim(attr, start, length, 1)
    old_host = lax.dynamic_slice_in_dim(host, start, length, 0)
    old_live = lax.dynamic_slice_in_dim(live, start, length, 0)
    attr = lax.dynamic_update_slice_in_dim(
        attr, jnp.where(valid[None], packed[:-1], old_attr), start, 1
    )
    host = lax.dynamic_update_slice_in_dim(
        host, jnp.where(valid, cells + offset, old_host), start, 0
    )
    live = lax.dynamic_update_slice_in_dim(live, jnp.where(valid, 1.0, old_live), start, 0)
    return (attr, host, live, jnp.sum(valid.astype(jnp.int32)))


def arrive(mass, state, host, live, count, from_left, from_right, far_offset):
    attr = jnp.concatenate([mass[None], state], axis=0)
    attr, host, live, left_count = place(attr, host, live, from_left, count, 0)
    attr, host, live, right_count = place(
        attr, host, live, from_right, count + left_count, far_offset
    )
    return (attr[0], attr[1:], host, live, count + left_count + right_count)


def sector_halo(field):
    return padded(field, (("azim", 1),), 1, True)


def block_halo(field):
    return padded(field, (("radax", 2),), 1, False)


def send_parcels(right_going, left_going):
    from_left = passed_along(right_going, "azim", 1)
    from_right = passed_along(left_going, "azim", -1)
    return (from_left, from_right)


def on_device(
    gas,
    transport,
    chemistry,
    evap_weight,
    source_map,
    parcel_mass,
    parcel_state,
    parcel_host,
    parcel_count,
    crossing,
):
    slots = parcel_mass.shape[-1]
    span = gas.shape[2] * gas.shape[3]
    far_offset = (gas.shape[1] - 1) * span
    mass = parcel_mass.reshape(slots)
    state = parcel_state.reshape(parcel_state.shape[0], slots)
    host = parcel_host.reshape(slots)
    count = parcel_count.reshape(())
    lists = crossing.reshape(crossing.shape[2], crossing.shape[3], crossing.shape[4])
    live = (jnp.arange(slots, dtype=jnp.int32) < count).astype(jnp.float32)
    sector_pad = sector_halo(gas)
    block_pad = block_halo(gas)
    deposit, mass, state = parcel_physics(gas, mass, state, host, live, evap_weight, source_map)
    section_one = gas + DT * (
        spatial_rhs(gas, sector_pad, block_pad, transport, chemistry) + deposit
    )
    right_going, left_going, live = depart(mass, state, host, live, lists[0], span)
    from_left, from_right = send_parcels(right_going, left_going)
    sector_pad = sector_halo(section_one)
    mass, state, host, live, count = arrive(
        mass, state, host, live, count, from_left, from_right, far_offset
    )
    block_pad = block_halo(section_one)
    deposit, mass, state = parcel_physics(
        section_one, mass, state, host, live, evap_weight, source_map
    )
    gas_next = 0.5 * (
        gas
        + section_one
        + DT * (spatial_rhs(section_one, sector_pad, block_pad, transport, chemistry) + deposit)
    )
    right_going, left_going, live = depart(mass, state, host, live, lists[1], span)
    from_left, from_right = send_parcels(right_going, left_going)
    mass, state, host, live, count = arrive(
        mass, state, host, live, count, from_left, from_right, far_offset
    )
    mass_next = (mass * live).reshape(parcel_mass.shape)
    state_next = (state * live[None]).reshape(parcel_state.shape)
    host_next = jnp.where(live > 0.5, host, -1).reshape(parcel_host.shape)
    count_next = count.reshape(parcel_count.shape)
    return (gas_next, mass_next, state_next, host_next, count_next)


def solution(mesh):
    in_specs = (
        P(None, "azim", "radax", None),
        P(),
        P(),
        P(),
        P(),
        P("azim", "radax", None),
        P(None, "azim", "radax", None),
        P("azim", "radax", None),
        P("azim", "radax"),
        P("azim", "radax", None, None, None),
    )
    out_specs = (
        P(None, "azim", "radax", None),
        P("azim", "radax", None),
        P(None, "azim", "radax", None),
        P("azim", "radax", None),
        P("azim", "radax"),
    )
    return jax.shard_map(
        on_device, mesh=mesh, in_specs=in_specs, out_specs=out_specs, check_vma=False
    )
```

profile of v0, /device:TPU:0, one launch (start us, length us, event | category | flops | bytes accessed | tf_op | source)
XLA Modules:
  0.0 101.2 jit_solution(10960177631570975006)
XLA Ops:
  0.7 2.8 %fusion.91 = (f32[14,4,32,128]{3,2,1,0:T(8,128)}, bf16[14,4,32,128]{3,2,1,0:T(8,128)(2,1)S(1)}, bf16[14,128,128]{2,1,0:T(8,128)(2,1)S(1)}) fusion(f32[14,4,32,128]{3,2,1,0:T(8,128)} %param.22), kind=kLoop, calls=%fused_computation.247 | loop fusion | flops 458752 | bytes 2752512 | tf_op jit(solution)/shard_map/tanh | solution.py:43
  3.6 1.0 subtract_convert_fusion.3
  5.7 1.2 %pad_maximum_fusion.2 = bf16[3,14,128,128]{3,2,1,0:T(8,128)(2,1)S(1)} fusion(bf16[1,14,128,128]{3,2,1,0:T(8,128)(2,1)} %bitcast.357, bf16[1,14,128,128]{3,2,1,0:T(8,128)(2,1)S(1)} %bitcast.350, bf16[1,14,128,128]{3,2,1,0:T(8,128)(2,1)S(1)} %bitcast.356), kind=kLoop, calls=%fused_computation.80 | loop fusion | flops 1376256 | bytes 2752512 | tf_op jit(solution)/shard_map/stack | solution.py:52
  7.0 4.1 %while.50 = (s32[]{:T(128)}, f32[4,14,512]{2,1,0:T(8,128)S(1)}, s32[4,512]{1,0:T(4,128)S(1)}, bf16[3,14,128,128]{3,2,1,0:T(8,128)(2,1)S(1)}, s32[]{:T(128)}) while((s32[]{:T(128)}, f32[4,14,512]{2,1,0:T(8,128)S(1)}, s32[4,512]{1,0:T(4,128)S(1)}, bf16[3,14,128,128]{3,2,1,0:T(8,128)(2,1)S(1)}, s32[]{:T(128)}) %tuple.156), condition=%wide.region_3.4_spmd, body=%wide.region_0.3_spmd.sunk | while | flops 237997056 | bytes 2533445 | solution.py:81
  14.1 1.7 %gather_fusion.1 = s32[256]{0:T(256)S(1)} fusion(s32[2048]{0:T(1024)S(1)} %bitcast.345, s32[1024]{0:T(1024)S(1)} %pad_clamp_fusion.1), kind=kCustom, calls=%fused_computation.1.clone | custom fusion | bytes 3072 | tf_op jit(solution)/shard_map/jit(_take)/gather | solution.py:115
  16.5 3.0 %collective-permute-start.9 = (f32[9,128]{1,0:T(8,128)S(1)}, f32[9,128]{1,0:T(8,128)S(1)}, u32[]{:S(2)}, u32[]{:S(2)}) collective-permute-start(f32[9,128]{1,0:T(8,128)S(1)} %bitcast.399), channel_id=1, source_target_pairs={{0,28},{4,0},{8,4},{12,8},{16,12},{20,16},{24,20},{28,24},{1,29},{... | collective-permute-start | bytes 13832 | tf_op jit(solution)/shard_map/ppermute | solution.py:28
  20.0 0.8 fusion.89
  21.5 1.3 %collective-permute-start.2 = (f32[14,4,1,128]{3,0,2,1:T(8,128)S(1)}, f32[14,4,1,128]{3,0,2,1:T(8,128)S(1)}, u32[]{:S(2)}, u32[]{:S(2)}) collective-permute-start(f32[14,4,1,128]{3,0,2,1:T(8,128)S(1)} %get-tuple-element.352), channel_id=1, source_target_pairs={{1,0},{2,1},{3,2},{5,4},{6,5},{7,6},{9,8},{10,9},{11,10},{13,12},{... | collective-permute-start | bytes 86024 | tf_op jit(solution)/shard_map/ppermute | solution.py:21
  23.3 8.0 %while.52 = (s32[]{:T(128)}, f32[14,128,128]{2,1,0:T(8,128)S(1)}, s32[4,512]{1,0:T(4,128)S(1)}, f32[4,14,512]{2,1,0:T(8,128)S(1)}, s32[]{:T(128)}, /*index=5*/s32[]{:T(128)}) while((s32[]{:T(128)}, f32[14,128,128]{2,1,0:T(8,128)S(1)}, s32[4,512]{1,0:T(4,128)S(1)}, f32[4,14,512]{2,1,0:T(8,128)S(1)}, s32[]{:T(128)}, ...), condition=%wide.region_6.7_spmd.clone, body=%wide.region_4.6_spmd.clone.sunk | while | flops 248492032 | bytes 6082655 | solution.py:100
  23.5 0.9 convert_reduce_fusion.12
  24.4 0.9 fusion.128
  25.5 0.9 convert_reduce_fusion.12
  26.4 0.9 fusion.128
  27.4 0.9 convert_reduce_fusion.12
  28.4 0.9 fusion.128
  29.4 0.9 convert_reduce_fusion.12
  30.3 0.9 fusion.128
  31.7 1.0 fusion.23
  32.7 2.7 %copy.164 = f32[14,128,128]{2,0,1:T(8,128)} copy(f32[14,128,128]{2,1,0:T(8,128)} %copy-done.2) | data formatting | bytes 1835008 | tf_op jit(solution)/shard_map/while | solution.py:100
  35.4 4.6 %collective-permute-start.3 = (f32[14,4,1,128]{3,0,2,1:T(8,128)S(1)}, f32[14,4,1,128]{3,0,2,1:T(8,128)S(1)}, u32[]{:S(2)}, u32[]{:S(2)}) collective-permute-start(f32[14,4,1,128]{3,0,2,1:T(8,128)S(1)} %get-tuple-element.353), channel_id=1, source_target_pairs={{0,1},{1,2},{2,3},{4,5},{5,6},{6,7},{8,9},{9,10},{10,11},{12,13},{... | collective-permute-start | bytes 86024 | tf_op jit(solution)/shard_map/ppermute | solution.py:20
  40.1 0.8 fusion.70
  42.0 0.8 convert_reduce_fusion.5
  43.1 1.7 %gather_fusion.3 = s32[256]{0:T(256)S(1)} fusion(s32[2048]{0:T(1024)S(1)} %get-tuple-element.374, s32[1024]{0:T(1024)S(1)} %pad_clamp_fusion), kind=kCustom, calls=%fused_computation.3.clone | custom fusion | bytes 3072 | tf_op jit(solution)/shard_map/jit(_take)/gather | solution.py:115
  46.9 3.7 %fusion.93 = (bf16[14,4,32,128]{3,0,2,1:T(8,128)(2,1)S(1)}, f32[14,4,32,128]{3,0,2,1:T(8,128)S(1)}) fusion(f32[14,4,32,128]{3,0,2,1:T(8,128)S(1)} %copy-done.8, f32[14,4,32,128]{3,0,2,1:T(8,128)} %bitcast.359, f32[14,4,32,128]{3,2,1,0:T(8,128)} %get-tuple-element.354, f32[14,14]{1,0:T(8,128)S(1)} %copy-done, f32[14]{0:T(128)S(1)} %get-tuple-element.383, ...), kind=kOutput, calls=%fused_computation.249 | convolution fusion | flops 43810816 | bytes 4645816 | tf_op jit(solution)/shard_map/fg,gabz->fabz/dot_general | solution.py:43
  51.9 6.9 %while.51 = (s32[]{:T(128)}, f32[4,14,512]{2,1,0:T(8,128)S(1)}, s32[4,512]{1,0:T(4,128)}, bf16[3,14,128,128]{3,2,1,0:T(8,128)(2,1)S(1)}, s32[]{:T(128)}) while((s32[]{:T(128)}, f32[4,14,512]{2,1,0:T(8,128)S(1)}, s32[4,512]{1,0:T(4,128)}, bf16[3,14,128,128]{3,2,1,0:T(8,128)(2,1)S(1)}, s32[]{:T(128)}) %tuple.162), condition=%wide.region_11.14_spmd, body=%wide.region_8.13_spmd.sunk | while | flops 237997056 | bytes 2533445 | solution.py:81
  59.1 0.8 fusion.87
  61.3 0.9 gather_fusion.2
  62.5 2.5 %collective-permute-start.11 = (f32[9,128]{1,0:T(8,128)S(1)}, f32[9,128]{1,0:T(8,128)}, u32[]{:S(2)}, u32[]{:S(2)}) collective-permute-start(f32[9,128]{1,0:T(8,128)S(1)} %bitcast.401), channel_id=1, source_target_pairs={{0,28},{4,0},{8,4},{12,8},{16,12},{20,16},{24,20},{28,24},{1,29},{... | collective-permute-start | bytes 13832 | tf_op jit(solution)/shard_map/ppermute | solution.py:28
  65.4 10.8 %while.53 = (s32[]{:T(128)}, f32[14,128,128]{2,1,0:T(8,128)S(1)}, s32[4,512]{1,0:T(4,128)}, f32[4,14,512]{2,1,0:T(8,128)S(1)}, s32[]{:T(128)}, /*index=5*/s32[]{:T(128)}) while((s32[]{:T(128)}, f32[14,128,128]{2,1,0:T(8,128)S(1)}, s32[4,512]{1,0:T(4,128)}, f32[4,14,512]{2,1,0:T(8,128)S(1)}, s32[]{:T(128)}, ...), condition=%wide.region_15.18_spmd.clone, body=%wide.region_13.17_spmd.clone.sunk | while | flops 248492032 | bytes 6082655 | solution.py:100
  65.5 0.8 and_select_fusion.24
  66.3 0.9 convert_reduce_fusion.13
  67.3 0.9 fusion.134
  69.0 0.9 convert_reduce_fusion.13
  69.9 0.9 fusion.134
  71.7 0.9 convert_reduce_fusion.13
  72.6 0.9 fusion.134
  74.4 0.9 convert_reduce_fusion.13
  75.3 0.9 fusion.134
  76.3 1.5 %copy.178 = f32[14,128,128]{2,0,1:T(8,128)} copy(f32[14,128,128]{2,1,0:T(8,128)S(1)} %get-tuple-element.234) | data formatting | bytes 1835008 | tf_op jit(solution)/shard_map/while | solution.py:100
  78.3 1.3 %collective-permute-start.6 = (f32[14,4,1,128]{3,0,2,1:T(8,128)}, f32[14,4,1,128]{3,0,2,1:T(8,128)S(1)}, u32[]{:S(2)}, u32[]{:S(2)}) collective-permute-start(f32[14,4,1,128]{3,0,2,1:T(8,128)} %get-tuple-element.348), channel_id=1, source_target_pairs={{1,0},{2,1},{3,2},{5,4},{6,5},{7,6},{9,8},{10,9},{11,10},{13,12},{... | collective-permute-start | bytes 86024 | tf_op jit(solution)/shard_map/ppermute | solution.py:21
  79.6 4.6 %collective-permute-start.7 = (f32[14,4,1,128]{3,0,2,1:T(8,128)S(1)}, f32[14,4,1,128]{3,0,2,1:T(8,128)S(1)}, u32[]{:S(2)}, u32[]{:S(2)}) collective-permute-start(f32[14,4,1,128]{3,0,2,1:T(8,128)S(1)} %get-tuple-element.349), channel_id=1, source_target_pairs={{0,1},{1,2},{2,3},{4,5},{5,6},{6,7},{8,9},{9,10},{10,11},{12,13},{... | collective-permute-start | bytes 86024 | tf_op jit(solution)/shard_map/ppermute | solution.py:20
  85.6 1.5 %fusion.74 = (s32[2048]{0:T(1024)S(1)}, s32[]{:T(128)}) fusion(s32[2048]{0:T(1024)S(1)} %get-tuple-element.374, s32[]{:T(128)S(6)} %select_n.227, f32[9,128]{1,0:T(8,128)} %collective-permute-done.10), kind=kLoop, calls=%fused_computation.217 | loop fusion | flops 639 | bytes 1544 | tf_op jit(solution)/shard_map/dynamic_update_slice | solution.py:133
  88.7 0.8 slice_select_fusion
  89.5 0.9 fusion.73
  90.4 0.8 select_dynamic-update-slice_fusion
  91.2 1.6 %convert_reduce_fusion.4 = (s32[]{:T(128)}, s32[2048]{0:T(1024)S(1)}) fusion(f32[9,128]{1,0:T(8,128)} %collective-permute-done.11, s32[2048]{0:T(1024)S(1)} %get-tuple-element.370, s32[]{:T(128)S(6)} %select_n.229), kind=kLoop, calls=%fused_computation.231 | loop fusion | flops 767 | bytes 1544 | tf_op jit(solution)/shard_map/reduce_sum | solution.py:137
  95.4 3.5 %fusion.28 = f32[14,4,32,128]{3,0,2,1:T(8,128)S(1)} fusion(f32[14,4,32,128]{3,0,2,1:T(8,128)} %bitcast.358, f32[14,4,32,128]{3,0,2,1:T(8,128)S(1)} %copy-done.6, f32[14,4,1,128]{3,0,2,1:T(8,128)S(1)} %collective-permute-done.7, f32[14,4,1,128]{3,0,2,1:T(8,128)S(1)} %collective-permute-done.6, f32[14,1,32,128]{3,0,2,1:T(8,128)S(1)} %collective-permute-done.4, ...), kind=kOutput, calls=%fused_computation.87 | convolution fusion | flops 44040192 | bytes 5448304 | tf_op jit(solution)/shard_map/fg,gabz->fabz/dot_general | solution.py:43
  98.9 1.2 %copy.183 = f32[14,4,32,128]{3,2,1,0:T(8,128)} copy(f32[14,4,32,128]{3,0,2,1:T(8,128)S(1)} %fusion.28) | data formatting | bytes 1835008
  (271 shorter events, 30.2 us)
Async XLA Ops:
  0.6 46.3 %copy-start = (f32[14,14]{1,0:T(8,128)S(1)}, f32[14,14]{1,0:T(8,128)}, u32[]{:S(2)}) copy-start(f32[14,14]{1,0:T(8,128)} %param.24) | copy-start | bytes 2356
  0.6 2.8 %copy-start.3 = (f32[14,4,32,128]{3,2,1,0:T(8,128)S(1)}, f32[14,4,32,128]{3,2,1,0:T(8,128)}, u32[]{:S(2)}) copy-start(f32[14,4,32,128]{3,2,1,0:T(8,128)} %param.22) | copy-start | bytes 2752516
  3.5 1.6 %copy-start.1 = (s32[1,1,2048]{2,1,0:T(1,128)S(1)}, s32[1,1,2048]{2,1,0:T(1,128)}, u32[]{:S(2)}) copy-start(s32[1,1,2048]{2,1,0:T(1,128)} %param.29) | copy-start | bytes 24580
  6.9 4.3 %copy-start.9 = (f32[7,1,1,2048]{3,2,1,0:T(1,128)S(1)}, f32[7,1,1,2048]{3,2,1,0:T(1,128)}, u32[]{:S(2)}) copy-start(f32[7,1,1,2048]{3,2,1,0:T(1,128)} %param.28) | copy-start | bytes 172036
  6.9 5.1 %copy-start.21 = (f32[14]{0:T(128)S(1)}, f32[14]{0:T(128)}, u32[]{:S(2)}) copy-start(f32[14]{0:T(128)} %param.25) | copy-start | bytes 172
  7.0 5.4 %slice-start = ((f32[7,1,1,2048]{3,2,1,0:T(1,128)}), f32[1,1,1,2048]{3,2,1,0:T(1,128)S(1)}, s32[]{:S(2)}) async-start(f32[7,1,1,2048]{3,2,1,0:T(1,128)} %param.28), calls=%async_computation | async-start | bytes 16384 | tf_op jit(solution)/shard_map/slice | solution.py:83
  7.0 5.4 %copy-start.15 = (f32[1,1,2048]{2,1,0:T(1,128)S(1)}, f32[1,1,2048]{2,1,0:T(1,128)}, u32[]{:S(2)}) copy-start(f32[1,1,2048]{2,1,0:T(1,128)} %param.27) | copy-start | bytes 24580
  11.1 1.6 %copy-start.14 = (s32[1,1,2,2,128]{4,3,2,1,0:T(2,128)S(1)}, s32[1,1,2,2,128]{4,3,2,1,0:T(2,128)}, u32[]{:S(2)}) copy-start(s32[1,1,2,2,128]{4,3,2,1,0:T(2,128)} %param.31) | copy-start | bytes 6148
  15.9 6.9 %copy-start.16 = (f32[14,8]{0,1:T(8,128)S(1)}, f32[14,8]{0,1:T(8,128)}, u32[]{:S(2)}) copy-start(f32[14,8]{0,1:T(8,128)} %param.26) | copy-start | bytes 1348
  15.9 19.5 %collective-permute-start.8 = (f32[9,128]{1,0:T(8,128)S(1)}, f32[9,128]{1,0:T(8,128)S(1)}, u32[]{:S(2)}, u32[]{:S(2)}) collective-permute-start(f32[9,128]{1,0:T(8,128)S(1)} %bitcast.400), channel_id=1, source_target_pairs={{0,4},{4,8},{8,12},{12,16},{16,20},{20,24},{24,28},{28,0},{1,5},{5... | collective-permute-start | bytes 13832 | tf_op jit(solution)/shard_map/ppermute | solution.py:28
  16.5 25.4 %collective-permute-start.9 = (f32[9,128]{1,0:T(8,128)S(1)}, f32[9,128]{1,0:T(8,128)S(1)}, u32[]{:S(2)}, u32[]{:S(2)}) collective-permute-start(f32[9,128]{1,0:T(8,128)S(1)} %bitcast.399), channel_id=1, source_target_pairs={{0,28},{4,0},{8,4},{12,8},{16,12},{20,16},{24,20},{28,24},{1,29},{... | collective-permute-start | bytes 13832 | tf_op jit(solution)/shard_map/ppermute | solution.py:28
  20.0 2.8 %copy-start.7 = (f32[14,4,32,128]{3,0,2,1:T(8,128)}, f32[14,4,32,128]{3,0,2,1:T(8,128)S(1)}, u32[]{:S(2)}) copy-start(f32[14,4,32,128]{3,0,2,1:T(8,128)S(1)} %copy.166) | copy-start | bytes 2752516
  20.8 26.1 %collective-permute-start = (f32[14,1,32,128]{3,0,2,1:T(8,128)}, f32[14,1,32,128]{3,0,2,1:T(8,128)}, u32[]{:S(2)}, u32[]{:S(2)}) collective-permute-start(f32[14,1,32,128]{3,0,2,1:T(8,128)} %get-tuple-element.351), channel_id=1, source_target_pairs={{4,0},{8,4},{12,8},{16,12},{20,16},{24,20},{28,24},{0,28},{5,1},{9... | collective-permute-start | bytes 688136 | tf_op jit(solution)/shard_map/ppermute | solution.py:21
  21.4 25.4 %collective-permute-start.1 = (f32[14,1,32,128]{3,0,2,1:T(8,128)S(1)}, f32[14,1,32,128]{3,0,2,1:T(8,128)}, u32[]{:S(2)}, u32[]{:S(2)}) collective-permute-start(f32[14,1,32,128]{3,0,2,1:T(8,128)S(1)} %get-tuple-element.350), channel_id=1, source_target_pairs={{0,4},{4,8},{8,12},{12,16},{16,20},{20,24},{24,28},{28,0},{1,5},{5... | collective-permute-start | bytes 688136 | tf_op jit(solution)/shard_map/ppermute | solution.py:20
  21.5 25.4 %collective-permute-start.2 = (f32[14,4,1,128]{3,0,2,1:T(8,128)S(1)}, f32[14,4,1,128]{3,0,2,1:T(8,128)S(1)}, u32[]{:S(2)}, u32[]{:S(2)}) collective-permute-start(f32[14,4,1,128]{3,0,2,1:T(8,128)S(1)} %get-tuple-element.352), channel_id=1, source_target_pairs={{1,0},{2,1},{3,2},{5,4},{6,5},{7,6},{9,8},{10,9},{11,10},{13,12},{... | collective-permute-start | bytes 86024 | tf_op jit(solution)/shard_map/ppermute | solution.py:21
  23.3 8.0 %copy-start.25 = (f32[3,14]{1,0:T(4,128)S(1)}, f32[3,14]{1,0:T(4,128)}, u32[]{:S(2)}) copy-start(f32[3,14]{1,0:T(4,128)} %param.23) | copy-start | bytes 508
  31.3 1.4 %copy-start.2 = (f32[14,128,128]{2,1,0:T(8,128)}, f32[14,128,128]{2,1,0:T(8,128)S(1)}, u32[]{:S(2)}) copy-start(f32[14,128,128]{2,1,0:T(8,128)S(1)} %get-tuple-element.232) | copy-start | bytes 2752516
  31.3 15.6 %copy-start.8 = (f32[14,4,32,128]{3,0,2,1:T(8,128)S(1)}, f32[14,4,32,128]{3,0,2,1:T(8,128)}, u32[]{:S(2)}) copy-start(f32[14,4,32,128]{3,0,2,1:T(8,128)} %copy-done.7) | copy-start | bytes 2752516
  31.3 19.3 %copy-start.26 = (f32[14]{0:T(128)}, f32[14]{0:T(128)S(1)}, u32[]{:S(2)}) copy-start(f32[14]{0:T(128)S(1)} %get-tuple-element.382) | copy-start | bytes 172
  31.3 19.3 %copy-start.28 = (f32[14]{0:T(128)}, f32[14]{0:T(128)S(1)}, u32[]{:S(2)}) copy-start(f32[14]{0:T(128)S(1)} %get-tuple-element.383) | copy-start | bytes 172
  31.3 19.3 %copy-start.29 = (f32[14]{0:T(128)}, f32[14]{0:T(128)S(1)}, u32[]{:S(2)}) copy-start(f32[14]{0:T(128)S(1)} %get-tuple-element.384) | copy-start | bytes 172
  32.7 14.2 %copy-start.18 = (s32[1024]{0:T(1024)}, s32[1024]{0:T(1024)S(1)}, u32[]{:S(2)}) copy-start(s32[1024]{0:T(1024)S(1)} %pad_clamp_fusion) | copy-start | bytes 12292
  35.4 11.4 %collective-permute-start.3 = (f32[14,4,1,128]{3,0,2,1:T(8,128)S(1)}, f32[14,4,1,128]{3,0,2,1:T(8,128)S(1)}, u32[]{:S(2)}, u32[]{:S(2)}) collective-permute-start(f32[14,4,1,128]{3,0,2,1:T(8,128)S(1)} %get-tuple-element.353), channel_id=1, source_target_pairs={{0,1},{1,2},{2,3},{4,5},{5,6},{6,7},{8,9},{9,10},{10,11},{12,13},{... | collective-permute-start | bytes 86024 | tf_op jit(solution)/shard_map/ppermute | solution.py:20
  43.1 3.8 %copy-start.12 = (f32[2048]{0:T(1024)}, f32[2048]{0:T(1024)S(1)}, u32[]{:S(2)}) copy-start(f32[2048]{0:T(1024)S(1)} %select_dynamic-update-slice_fusion.1) | copy-start | bytes 24580
  50.6 9.3 %copy-start.5 = (f32[14,4,32,128]{3,0,2,1:T(8,128)}, f32[14,4,32,128]{3,0,2,1:T(8,128)S(1)}, u32[]{:S(2)}) copy-start(f32[14,4,32,128]{3,0,2,1:T(8,128)S(1)} %get-tuple-element.386) | copy-start | bytes 2752516
  58.9 1.7 %copy-start.22 = (f32[14]{0:T(128)S(1)}, f32[14]{0:T(128)}, u32[]{:S(2)}) copy-start(f32[14]{0:T(128)} %param.25) | copy-start | bytes 172
  58.9 2.0 %copy-start.13 = (f32[2048]{0:T(1024)S(1)}, f32[2048]{0:T(1024)}, u32[]{:S(2)}) copy-start(f32[2048]{0:T(1024)} %copy-done.12) | copy-start | bytes 24580
  58.9 2.0 %copy-start.24 = (pred[2048]{0:T(1024)(128)(4,1)S(1)}, pred[2048]{0:T(1024)(128)(4,1)}, u32[]{:S(2)}) copy-start(pred[2048]{0:T(1024)(128)(4,1)} %fusion.23) | copy-start | bytes 6148
  59.0 3.2 %copy-start.19 = (f32[2,128]{1,0:T(2,128)S(1)}, f32[2,128]{1,0:T(2,128)}, u32[]{:S(2)}) copy-start(f32[2,128]{1,0:T(2,128)} %get-tuple-element.332) | copy-start | bytes 3076
  59.0 3.2 %copy-start.23 = (pred[2,128]{1,0:T(4,128)(4,1)S(1)}, pred[2,128]{1,0:T(4,128)(4,1)}, u32[]{:S(2)}) copy-start(pred[2,128]{1,0:T(4,128)(4,1)} %get-tuple-element.331) | copy-start | bytes 772
  59.0 3.2 %copy-start.20 = (f32[1,2,128]{2,1,0:T(2,128)S(1)}, f32[1,2,128]{2,1,0:T(2,128)}, u32[]{:S(2)}) copy-start(f32[1,2,128]{2,1,0:T(2,128)} %get-tuple-element.330) | copy-start | bytes 3076
  59.0 5.9 %copy-start.17 = (f32[14,8]{0,1:T(8,128)S(1)}, f32[14,8]{0,1:T(8,128)}, u32[]{:S(2)}) copy-start(f32[14,8]{0,1:T(8,128)} %param.26) | copy-start | bytes 1348
  62.3 17.3 %collective-permute-start.10 = (f32[9,128]{1,0:T(8,128)S(1)}, f32[9,128]{1,0:T(8,128)}, u32[]{:S(2)}, u32[]{:S(2)}) collective-permute-start(f32[9,128]{1,0:T(8,128)S(1)} %bitcast.402), channel_id=1, source_target_pairs={{0,4},{4,8},{8,12},{12,16},{16,20},{20,24},{24,28},{28,0},{1,5},{5... | collective-permute-start | bytes 13832 | tf_op jit(solution)/shard_map/ppermute | solution.py:28
  62.5 25.5 %collective-permute-start.11 = (f32[9,128]{1,0:T(8,128)S(1)}, f32[9,128]{1,0:T(8,128)}, u32[]{:S(2)}, u32[]{:S(2)}) collective-permute-start(f32[9,128]{1,0:T(8,128)S(1)} %bitcast.401), channel_id=1, source_target_pairs={{0,28},{4,0},{8,4},{12,8},{16,12},{20,16},{24,20},{28,24},{1,29},{... | collective-permute-start | bytes 13832 | tf_op jit(solution)/shard_map/ppermute | solution.py:28
  65.4 12.4 %copy-start.11 = (f32[14,1,32,128]{3,0,2,1:T(8,128)S(1)}, f32[14,1,32,128]{3,0,2,1:T(8,128)}, u32[]{:S(2)}) copy-start(f32[14,1,32,128]{3,0,2,1:T(8,128)} %get-tuple-element.347) | copy-start | bytes 688132
  65.4 12.4 %copy-start.10 = (f32[14,1,32,128]{3,0,2,1:T(8,128)S(1)}, f32[14,1,32,128]{3,0,2,1:T(8,128)}, u32[]{:S(2)}) copy-start(f32[14,1,32,128]{3,0,2,1:T(8,128)} %get-tuple-element.346) | copy-start | bytes 688132
  76.2 19.1 %copy-start.4 = (f32[14,4,32,128]{3,2,1,0:T(8,128)S(1)}, f32[14,4,32,128]{3,2,1,0:T(8,128)}, u32[]{:S(2)}) copy-start(f32[14,4,32,128]{3,2,1,0:T(8,128)} %param.22) | copy-start | bytes 2752516
  76.2 19.1 %copy-start.6 = (f32[14,4,32,128]{3,0,2,1:T(8,128)S(1)}, f32[14,4,32,128]{3,0,2,1:T(8,128)}, u32[]{:S(2)}) copy-start(f32[14,4,32,128]{3,0,2,1:T(8,128)} %copy-done.5) | copy-start | bytes 2752516
  76.3 19.1 %copy-start.27 = (f32[14]{0:T(128)S(1)}, f32[14]{0:T(128)}, u32[]{:S(2)}) copy-start(f32[14]{0:T(128)} %copy-done.26) | copy-start | bytes 172
  77.8 17.6 %collective-permute-start.4 = (f32[14,1,32,128]{3,0,2,1:T(8,128)S(1)}, f32[14,1,32,128]{3,0,2,1:T(8,128)S(1)}, u32[]{:S(2)}, u32[]{:S(2)}) collective-permute-start(f32[14,1,32,128]{3,0,2,1:T(8,128)S(1)} %copy-done.11), channel_id=1, source_target_pairs={{4,0},{8,4},{12,8},{16,12},{20,16},{24,20},{28,24},{0,28},{5,1},{9... | collective-permute-start | bytes 688136 | tf_op jit(solution)/shard_map/ppermute | solution.py:21
  77.8 17.6 %collective-permute-start.5 = (f32[14,1,32,128]{3,0,2,1:T(8,128)S(1)}, f32[14,1,32,128]{3,0,2,1:T(8,128)S(1)}, u32[]{:S(2)}, u32[]{:S(2)}) collective-permute-start(f32[14,1,32,128]{3,0,2,1:T(8,128)S(1)} %copy-done.10), channel_id=1, source_target_pairs={{0,4},{4,8},{8,12},{12,16},{16,20},{20,24},{24,28},{28,0},{1,5},{5... | collective-permute-start | bytes 688136 | tf_op jit(solution)/shard_map/ppermute | solution.py:20
  78.3 17.1 %collective-permute-start.6 = (f32[14,4,1,128]{3,0,2,1:T(8,128)}, f32[14,4,1,128]{3,0,2,1:T(8,128)S(1)}, u32[]{:S(2)}, u32[]{:S(2)}) collective-permute-start(f32[14,4,1,128]{3,0,2,1:T(8,128)} %get-tuple-element.348), channel_id=1, source_target_pairs={{1,0},{2,1},{3,2},{5,4},{6,5},{7,6},{9,8},{10,9},{11,10},{13,12},{... | collective-permute-start | bytes 86024 | tf_op jit(solution)/shard_map/ppermute | solution.py:21
  79.6 15.8 %collective-permute-start.7 = (f32[14,4,1,128]{3,0,2,1:T(8,128)S(1)}, f32[14,4,1,128]{3,0,2,1:T(8,128)S(1)}, u32[]{:S(2)}, u32[]{:S(2)}) collective-permute-start(f32[14,4,1,128]{3,0,2,1:T(8,128)S(1)} %get-tuple-element.349), channel_id=1, source_target_pairs={{0,1},{1,2},{2,3},{4,5},{5,6},{6,7},{8,9},{9,10},{10,11},{12,13},{... | collective-permute-start | bytes 86024 | tf_op jit(solution)/shard_map/ppermute | solution.py:20
where the time goes:
time: 102 us; the launch traced here: 101 us
  other arithmetic  36.1 us (35%)
  matrix products  20.8 us (20%)
  starting transfers between devices  19.1 us (19%)
  local copies, waits for them, and re-layouts  17.9 us (18%)
  between operations  6.1 us (6%)
  loops' own time  1.13 us (1%)
    ppermute x4, starting transfers between devices, padded(): before = lax.ppermute(last, axis, up)  9.7 us
    dot_general x8, matrix products, deposit_block(): jnp.einsum('sflp,hp->fhl', laid, upper_hot, preferred_element_type=jnp.fl...  7.22 us
    reduce_sum x8, other arithmetic, deposit_block(): jnp.einsum('sflp,hp->fhl', laid, upper_hot, preferred_element_type=jnp.fl...  7.16 us
    dot_general x2, matrix products, spatial_rhs(): jnp.einsum('fg,gabz->fabz', chemistry, jnp.tanh(field), precision=HIGH)  7.12 us
    ppermute x4, starting transfers between devices, passed_along(): lax.ppermute(array, axis, [(i, (i + by) % size) for i in range(size)])  6.16 us
    select_n x16, other arithmetic, block_tables(): upper_ids = host_block // LANES  5.94 us
    dot_general x8, matrix products, probe_block(): jnp.einsum('sfhl,hp->flp', pieces, upper_hot, preferred_element_type=jnp....  5.42 us
    while x2, local copies, waits for them, and re-layouts, parcel_physics(): lax.scan(deposit_block, empty, (host_blocks, source_blocks))  4.2 us
  transfers between devices with their start and end apart: 12, of which 0 were waited for; matrix products, arithmetic and copies ran while one was open for 41% of the time, Pallas kernels for 0%

commit v1 on v0

v1 whole, which is shorter than its diff:
```python
import functools

import jax
import jax.numpy as jnp
from jax import lax
from jax.experimental import pallas as pl
from jax.experimental.pallas import tpu as pltpu
from jax.sharding import PartitionSpec as P

DT = 0.5
RELAX = 0.3
EVAP = 0.5
F32 = jnp.float32
BF16 = jnp.bfloat16
ROWS = 16
HOST = 8
LIVE = 9
LANES = 128
LIMIT = 40 << 20

VMEM = pl.BlockSpec(memory_space=pltpu.VMEM)
SMEM = pl.BlockSpec(memory_space=pltpu.SMEM)
ANY = pl.BlockSpec(memory_space=pl.ANY)


def iota(shape, dim, dtype=jnp.int32):
    return lax.broadcasted_iota(dtype, shape, dim)


def parts_of(values, count):
    parts = []
    for _ in range(count - 1):
        part = values.astype(BF16)
        parts.append(part)
        values = values - part.astype(F32)
    return parts + [values.astype(BF16)]


def hot(mask):
    return mask.astype(F32).astype(BF16)


def across(left, right):
    return lax.dot_general(left, right, (((1,), (1,)), ((), ())), preferred_element_type=F32)


def call(kernel, outs, ins, out_specs, args, scratch=(), aliases=None, flops=0, moved=0, trans=0):
    return pl.pallas_call(
        kernel,
        out_shape=outs,
        in_specs=ins,
        out_specs=out_specs,
        scratch_shapes=list(scratch),
        input_output_aliases=aliases or {},
        compiler_params=pltpu.CompilerParams(vmem_limit_bytes=LIMIT),
        cost_estimate=pl.CostEstimate(flops=flops, bytes_accessed=moved, transcendentals=trans),
    )(*args)


def shape(dims, dtype=F32):
    return jax.ShapeDtypeStruct(dims, dtype)


def pack_kernel(par, gas, on, off, near, far, sems):
    ca, cr = gas.shape[1], gas.shape[2]
    odd_a, odd_r = par[0], par[1]
    copies = [
        pltpu.make_async_copy(gas.at[:, (ca - 1) * (1 - odd_a)], on, sems.at[0]),
        pltpu.make_async_copy(gas.at[:, (ca - 1) * odd_a], off, sems.at[1]),
        pltpu.make_async_copy(gas.at[:, :, (cr - 1) * (1 - odd_r)], near, sems.at[2]),
        pltpu.make_async_copy(gas.at[:, :, (cr - 1) * odd_r], far, sems.at[3]),
    ]
    for copy in copies:
        copy.start()
    for copy in copies:
        copy.wait()


def inner_terms(gas, transport, chemistry, tanh, a):
    nf, ca, cr, cz = gas.shape
    lane = iota((cr, cz), 1)
    row = iota((cr, cz), 0)
    for f in range(nf):
        nu, swirl, axial = transport[0, f], transport[1, f], transport[2, f]
        here = gas[f, a]
        total = -6.0 * nu * here
        total += (nu - 0.5 * axial) * jnp.where(lane == cz - 1, 0.0, pltpu.roll(here, cz - 1, 1))
        total += (nu + 0.5 * axial) * jnp.where(lane == 0, 0.0, pltpu.roll(here, 1, 1))
        radial = jnp.where(row == cr - 1, 0.0, pltpu.roll(here, cr - 1, 0))
        radial += jnp.where(row == 0, 0.0, pltpu.roll(here, 1, 0))
        total += nu * radial
        if a < ca - 1:
            total += (nu - 0.5 * swirl) * gas[f, a + 1]
        if a > 0:
            total += (nu + 0.5 * swirl) * gas[f, a - 1]
        for g in range(nf):
            total += chemistry[f, g] * tanh[g, a]
        yield f, total


def probe_all(gas, host, table, hots, probed):
    nf, ca, cr, cz = gas.shape
    slots = host.shape[1]
    width = ca * cz
    for f in range(nf):
        for a in range(ca):
            upper, lower = parts_of(gas[f, a], 2)
            table[f * cr : (f + 1) * cr, a * cz : (a + 1) * cz] = upper
            table[f * cr : (f + 1) * cr, width + a * cz : width + (a + 1) * cz] = lower
    span = cr * cz
    block = 256
    for b in range(slots // block):
        cells = host[:, b * block : (b + 1) * block]
        column = (cells // span) * cz + cells % cz
        row = (cells // cz) % cr
        hots[:, b * block : (b + 1) * block] = hot(iota((width, block), 0) == column)
        ahot = hots[:, b * block : (b + 1) * block]
        found = jnp.dot(table[:, :width], ahot, preferred_element_type=F32)
        found += jnp.dot(table[:, width:], ahot, preferred_element_type=F32)
        mask = iota((cr, block), 0) == row
        found = jnp.where(mask[None], found.reshape(nf, cr, block), 0.0)
        probed[:nf, b * block : (b + 1) * block] = jnp.sum(found, axis=1)


def react(probed, attr, live, evap, source_map):
    nf = source_map.shape[0]
    pull = evap[0] * probed[0:1]
    for f in range(1, nf):
        pull += evap[f] * probed[f : f + 1]
    sig = jax.nn.sigmoid(pull + attr[1:2])
    mdot = EVAP * attr[0:1] * sig * live
    source = source_map[:, 0:1] * attr[0:1]
    for k in range(1, source_map.shape[1]):
        source += source_map[:, k : k + 1] * attr[k : k + 1]
    source = source * mdot
    rows = [attr[0:1] - DT * mdot]
    rows.append(attr[1:2] + DT * RELAX * (probed[4:5] - attr[1:2]))
    rows.append(attr[2:5] + DT * RELAX * (probed[1:4] - attr[2:5]))
    rows.append(attr[5:8])
    return rows, source


def deposit_all(source, host, hots, shapes, reach, total):
    nf, ca, cr, cz = shapes
    width = ca * cz
    block = 512 if reach % 512 == 0 else 128
    for b in range(reach // block):
        cells = host[:, b * block : (b + 1) * block]
        row = (cells // cz) % cr
        mask = iota((cr, block), 0) == row
        spread = jnp.where(mask[None], source[:nf, b * block : (b + 1) * block][:, None, :], 0.0)
        upper, lower = parts_of(spread.reshape(nf * cr, block), 2)
        ahot = hots[:, b * block : (b + 1) * block]
        part = across(upper, ahot) + across(lower, ahot)
        if b == 0:
            total[...] = part
        else:
            total[...] += part


def list_hots(lists, section, slots, lhot):
    width = lists.shape[-1]
    for d in range(2):
        names = lists[0, 0, section, d : d + 1, :].astype(F32)
        column = jnp.broadcast_to(names, (width, width)).T
        for b in range(slots // width):
            at = iota((width, width), 1).astype(F32) + float(b * width)
            lhot[d * width : (d + 1) * width, b * width : (b + 1) * width] = hot(column == at)


def leave(parcels, lists, section, lhot, odd_a, span, slots):
    width = lists.shape[-1]
    parts = jnp.concatenate(parts_of(parcels[:, :slots], 3), axis=0)
    taken = across(parts, lhot[...])
    taken = taken[:ROWS] + taken[ROWS : 2 * ROWS] + taken[2 * ROWS :]
    gone = jnp.dot(jnp.ones((8, 2 * width), BF16), lhot[...], preferred_element_type=F32)
    live = jnp.where(gone[0:1] > 0.5, 0.0, parcels[LIVE : LIVE + 1, :slots])
    packs = []
    for d in range(2):
        valid = lists[0, 0, section, d : d + 1, :] < slots
        pack = taken[:, d * width : (d + 1) * width]
        cell = pack[HOST : HOST + 1].astype(jnp.int32) % span
        cell = jnp.where(valid, cell.astype(F32), -1.0)
        row = iota(pack.shape, 0)
        pack = jnp.where(row == HOST, cell, jnp.where(valid & (row < HOST), pack, 0.0))
        packs.append(pack)
    left, right = packs
    return jnp.where(odd_a == 1, left, right), jnp.where(odd_a == 1, right, left), live


def section_kernel(
    first, par, count, gas, transport, chemistry, evap, source_map, lists, *refs
):
    if first:
        mass, state, host_in, out, parcels, on, off = refs[:7]
        table, hots, probed, total, tanh, lhot = refs[7:]
    else:
        old_gas, old, out, parcels = refs[:4]
        table, hots, probed, total, tanh = refs[4:]
    nf, ca, cr, cz = gas.shape
    slots = probed.shape[1]
    reach = slots - 4 * lists.shape[-1]
    if first:
        host = host_in[0]
        live = (iota((1, slots), 1) < count[0, 0]).astype(F32)
        attr = jnp.concatenate([mass[0]] + [state[k, 0] for k in range(state.shape[0])], axis=0)
    else:
        host = old[HOST : HOST + 1, :slots].astype(jnp.int32)
        live = old[LIVE : LIVE + 1, :slots]
        attr = old[0:HOST, :slots]
    probe_all(gas, host, table, hots, probed)
    rows, source = react(probed[...], attr, live, evap, source_map)
    parcels[...] = jnp.zeros_like(parcels)
    parcels[0:ROWS, :slots] = jnp.concatenate(
        rows + [host.astype(F32), live, jnp.zeros((ROWS - LIVE - 1, slots), F32)], axis=0
    )
    if first:
        list_hots(lists, 0, slots, lhot)
        going_on, going_off, live_left = leave(parcels, lists, 0, lhot, par[0], cr * cz, slots)
        parcels[LIVE : LIVE + 1, :slots] = live_left
        on[...] = going_on
        off[...] = going_off
    for g in range(nf):
        tanh[g] = jnp.tanh(gas[g])
    deposit_all(source, host, hots, gas.shape, reach, total)
    for a in range(ca):
        for f, terms in inner_terms(gas, transport, chemistry, tanh, a):
            terms += total[f * cr : (f + 1) * cr, a * cz : (a + 1) * cz]
            here = gas[f, a] + DT * terms
            if not first:
                here = 0.5 * (old_gas[f, a] + here)
            out[f, a] = here


def edge_terms(scale, par, transport, out, on, off, near, far):
    nf, ca, cr, cz = out.shape
    odd_a, odd_r = par[0] == 1, par[1] == 1
    for f in range(nf):
        nu, swirl = transport[0, f], transport[1, f]
        got_on, got_off = on[f * cr : (f + 1) * cr], off[f * cr : (f + 1) * cr]
        east = jnp.where(odd_a, got_off, got_on)
        west = jnp.where(odd_a, got_on, got_off)
        out[f, 0] += (scale * (nu + 0.5 * swirl)) * west
        out[f, ca - 1] += (scale * (nu - 0.5 * swirl)) * east
        north = jnp.where(odd_r, far[f], near[f])
        south = jnp.where(odd_r, near[f], far[f])
        out[f, :, 0, :] += (scale * nu) * south
        out[f, :, cr - 1, :] += (scale * nu) * north


def edge_kernel(par, transport, base, on, off, near, far, pack_on, pack_off, out, *sends):
    send_on, send_off, send_near, send_far = sends
    nf, ca, cr, cz = out.shape
    out[...] = base[...]
    edge_terms(DT, par, transport, out, on, off, near, far)
    odd_a, odd_r = par[0] == 1, par[1] == 1
    for f in range(nf):
        low, high = out[f, 0], out[f, ca - 1]
        send_on[f * cr : (f + 1) * cr] = jnp.where(odd_a, low, high)
        send_off[f * cr : (f + 1) * cr] = jnp.where(odd_a, high, low)
        low, high = out[f, :, 0, :], out[f, :, cr - 1, :]
        send_near[f] = jnp.where(odd_r, low, high)
        send_far[f] = jnp.where(odd_r, high, low)
    send_on[nf * cr :] = pack_on[...]
    send_off[nf * cr :] = pack_off[...]


def put(parcels, pack, start, live):
    width = pack.shape[1]
    row = iota(pack.shape, 0)
    pack = jnp.where(row == LIVE, live, pack)
    shift = start % width
    first = pl.multiple_of((start // width) * width, width)
    pack = pltpu.roll(pack, shift, 1)
    lane = iota(pack.shape, 1)
    taken = pack[LIVE : LIVE + 1] > 0.5
    here = parcels[:, pl.ds(first, width)]
    parcels[:, pl.ds(first, width)] = jnp.where(taken & (lane >= shift), pack, here)
    second = pl.multiple_of(first + width, width)
    here = parcels[:, pl.ds(second, width)]
    parcels[:, pl.ds(second, width)] = jnp.where(taken & (lane < shift), pack, here)


def arrive_kernel(
    par, count, gas, evap, source_map, lists, on, off, old, parcels, send_on, send_off, sources,
    used, table, lhot,
):
    nf, ca, cr, cz = gas.shape
    slots = lhot.shape[1]
    odd_a = par[0] == 1
    base = nf * cr
    got_on, got_off = on[base:], off[base:]
    packs = [jnp.where(odd_a, got_on, got_off), jnp.where(odd_a, got_off, got_on)]
    parcels[...] = old[...]
    start = count[0, 0]
    for side in range(2):
        layer = side * (ca - 1)
        pack = packs[side]
        cell = pack[HOST : HOST + 1].astype(jnp.int32)
        live = (cell >= 0).astype(F32)
        for f in range(nf):
            upper, lower = parts_of(gas[f, layer], 2)
            table[f * cr : (f + 1) * cr, :cz] = upper
            table[f * cr : (f + 1) * cr, cz:] = lower
        zhot = hot(iota((cz, cell.shape[1]), 0) == cell % cz)
        found = jnp.dot(table[:, :cz], zhot, preferred_element_type=F32)
        found += jnp.dot(table[:, cz:], zhot, preferred_element_type=F32)
        mask = iota((cr, cell.shape[1]), 0) == cell // cz
        found = jnp.where(mask[None], found.reshape(nf, cr, cell.shape[1]), 0.0)
        probed = jnp.sum(found, axis=1)
        rows, source = react(probed, pack[0:HOST], live, evap, source_map)
        sources[side, :nf] = source
        sources[side, nf : nf + 1] = pack[HOST : HOST + 1]
        home = (cell + layer * cr * cz).astype(F32)
        moved = jnp.concatenate(rows + [home, live, jnp.zeros((ROWS - LIVE - 1, cell.shape[1]), F32)], 0)
        put(parcels, moved, start, live)
        start = start + jnp.sum(live).astype(jnp.int32)
    used[0, 0] = start
    list_hots(lists, 1, slots, lhot)
    going_on, going_off, live = leave(parcels, lists, 1, lhot, par[0], cr * cz, slots)
    parcels[LIVE : LIVE + 1, :slots] = live
    send_on[...] = going_on
    send_off[...] = going_off


def finish_kernel(par, transport, base, on, off, near, far, sources, out):
    nf, ca, cr, cz = out.shape
    out[...] = base[...]
    edge_terms(0.5 * DT, par, transport, out, on, off, near, far)
    for side in range(2):
        layer = side * (ca - 1)
        cell = sources[side, nf : nf + 1].astype(jnp.int32)
        mask = iota((cr, cell.shape[1]), 0) == cell // cz
        spread = jnp.where(mask[None], sources[side, :nf][:, None, :], 0.0)
        upper, lower = parts_of(spread.reshape(nf * cr, cell.shape[1]), 2)
        zhot = hot(iota((cz, cell.shape[1]), 0) == cell % cz)
        total = across(upper, zhot) + across(lower, zhot)
        for f in range(nf):
            out[f, layer] += (0.5 * DT) * total[f * cr : (f + 1) * cr]


def place_kernel(far_offset, par, count, on, off, old, mass, state, host, used, parcels):
    odd_a = par[0] == 1
    slots = mass.shape[-1]
    parcels[...] = old[...]
    got_on, got_off = on[...], off[...]
    packs = [jnp.where(odd_a, got_on, got_off), jnp.where(odd_a, got_off, got_on)]
    start = count[0, 0]
    for side in range(2):
        pack = packs[side]
        live = (pack[HOST : HOST + 1] >= 0.0).astype(F32)
        row = iota(pack.shape, 0)
        pack = jnp.where(row == HOST, pack + float(side * far_offset), pack)
        put(parcels, pack, start, live)
        start = start + jnp.sum(live).astype(jnp.int32)
    used[0, 0] = start
    live = parcels[LIVE : LIVE + 1, :slots] > 0.5
    mass[0] = jnp.where(live, parcels[0:1, :slots], 0.0)
    for k in range(state.shape[0]):
        state[k, 0] = jnp.where(live, parcels[k + 1 : k + 2, :slots], 0.0)
    host[0] = jnp.where(live, parcels[HOST : HOST + 1, :slots].astype(jnp.int32), -1)


def swap(array, axis, phase, wrap):
    size = lax.axis_size(axis)
    pairs = []
    for i in range(phase, size if wrap else size - 1, 2):
        j = (i + 1) % size
        pairs += [(i, j), (j, i)]
    return lax.ppermute(array, axis, pairs)


def on_device(
    gas, transport, chemistry, evap, source_map, mass, state, host, count, crossing
):
    nf, ca, cr, cz = gas.shape
    slots = mass.shape[-1]
    width = crossing.shape[-1]
    padded = slots + 2 * width
    par = jnp.stack([lax.axis_index("azim") % 2, lax.axis_index("radax") % 2]).astype(jnp.int32)
    layer, ring = shape((nf * cr, cz)), shape((nf, ca, cz))
    pack = shape((ROWS, width))
    on, off, near, far = call(
        pack_kernel,
        [shape((nf, cr, cz)), shape((nf, cr, cz)), ring, ring],
        [SMEM, ANY],
        [ANY] * 4,
        (par, gas),
        scratch=[pltpu.SemaphoreType.DMA((4,))],
        moved=2_000_000,
    )
    on = swap(on.reshape(nf * cr, cz), "azim", 0, True)
    off = swap(off.reshape(nf * cr, cz), "azim", 1, True)
    near = swap(near, "radax", 0, False)
    far = swap(far, "radax", 1, False)

    section_scratch = [
        pltpu.VMEM((nf * cr, 2 * ca * cz), BF16),
        pltpu.VMEM((ca * cz, slots), BF16),
        pltpu.VMEM((ROWS, slots), F32),
        pltpu.VMEM((nf * cr, ca * cz), F32),
        pltpu.VMEM(gas.shape, F32),
    ]
    list_scratch = pltpu.VMEM((2 * width, slots), BF16)
    heavy = dict(flops=6_000_000_000, moved=4_000_000, trans=300_000)
    params = [SMEM, SMEM, VMEM, SMEM, SMEM, SMEM, VMEM, VMEM]
    base, parcels, pack_on, pack_off = call(
        functools.partial(section_kernel, True),
        [shape(gas.shape), shape((ROWS, padded)), pack, pack],
        params + [VMEM] * 3,
        [VMEM] * 4,
        (par, count, gas, transport, chemistry, evap, source_map, crossing, mass, state, host),
        scratch=section_scratch + [list_scratch],
        **heavy,
    )
    longer = shape((nf * cr + ROWS, cz))
    section_one, on, off, near, far = call(
        edge_kernel,
        [shape(gas.shape), longer, longer, ring, ring],
        [SMEM, SMEM] + [VMEM] * 7,
        [VMEM] * 5,
        (par, transport, base, on, off, near, far, pack_on, pack_off),
        aliases={2: 0},
        moved=3_000_000,
    )
    on = swap(on, "azim", 0, True)
    off = swap(off, "azim", 1, True)
    near = swap(near, "radax", 0, False)
    far = swap(far, "radax", 1, False)
    base, parcels = call(
        functools.partial(section_kernel, False),
        [shape(gas.shape), shape((ROWS, padded))],
        params + [VMEM] * 2,
        [VMEM] * 2,
        (par, count, section_one, transport, chemistry, evap, source_map, crossing, gas, parcels),
        scratch=section_scratch,
        **heavy,
    )
    parcels, pack_on, pack_off, sources, count = call(
        arrive_kernel,
        [shape((ROWS, padded)), pack, pack, shape((2, ROWS, width)), shape((1, 1), jnp.int32)],
        [SMEM, SMEM, VMEM, SMEM] + [VMEM] * 5,
        [VMEM] * 4 + [SMEM],
        (par, count, section_one, evap, source_map, crossing, on, off, parcels),
        scratch=[pltpu.VMEM((nf * cr, 2 * cz), BF16), list_scratch],
        flops=100_000_000,
        moved=2_000_000,
    )
    pack_on = swap(pack_on, "azim", 0, True)
    pack_off = swap(pack_off, "azim", 1, True)
    gas_next = call(
        finish_kernel,
        shape(gas.shape),
        [SMEM, SMEM] + [VMEM] * 6,
        VMEM,
        (par, transport, base, on, off, near, far, sources),
        flops=100_000_000,
        moved=3_000_000,
    )
    mass_next, state_next, host_next, count_next = call(
        functools.partial(place_kernel, (ca - 1) * cr * cz),
        [shape(mass.shape), shape(state.shape), shape(host.shape, jnp.int32), shape((1, 1), jnp.int32)],
        [SMEM, SMEM] + [VMEM] * 3,
        [VMEM] * 3 + [SMEM],
        (par, count, pack_on, pack_off, parcels),
        scratch=[pltpu.VMEM((ROWS, padded), F32)],
        moved=500_000,
    )
    return gas_next, mass_next, state_next, host_next, count_next


def solution(mesh):
    in_specs = (
        P(None, "azim", "radax", None),
        P(),
        P(),
        P(),
        P(),
        P("azim", "radax", None),
        P(None, "azim", "radax", None),
        P("azim", "radax", None),
        P("azim", "radax"),
        P("azim", "radax", None, None, None),
    )
    out_specs = (
        P(None, "azim", "radax", None),
        P("azim", "radax", None),
        P(None, "azim", "radax", None),
        P("azim", "radax", None),
        P("azim", "radax"),
    )
    return jax.shard_map(
        on_device, mesh=mesh, in_specs=in_specs, out_specs=out_specs, check_vma=False
    )
```

time: 102 us -> 39.2 us (0.38)
  other arithmetic: 36.1 us -> 0.08 us
  matrix products: 20.8 us -> 0 us
  Pallas kernels: 0 us -> 19 us
  local copies, waits for them, and re-layouts: 17.9 us -> 2.57 us
  starting transfers between devices: 19.1 us -> 14 us
  between operations: 6.1 us -> 1.64 us
  waiting for transfers between devices: 0.03 us -> 1.67 us
  loops' own time: 1.13 us -> 0 us
    dot_general x22 -> x0, matrix products: 20.8 us -> none  [the longest x8 7.22 us: deposit_block(): jnp.einsum('sflp,hp->fhl', laid, upper_hot, preferred_element_type=jnp.fl...]
    pallas_call x0 -> x7, Pallas kernels: none -> 19 us  [call(): pl.pallas_call(kernel, out_shape=outs, in_specs=ins, out_specs=out_specs,...]
    reduce_sum x19 -> x0, other arithmetic: 12.1 us -> none  [the longest x8 7.16 us: deposit_block(): jnp.einsum('sflp,hp->fhl', laid, upper_hot, preferred_element_type=jnp.fl...]
    select_n x38 -> x0, other arithmetic: 8.3 us -> none  [the longest x16 5.94 us: block_tables(): upper_ids = host_block // LANES]
    gather x6 -> x0, local copies, waits for them, and re-layouts: 5.18 us -> none  [the longest x2 3.46 us: depart(): jnp.take(host, safe) % span]
    ppermute x12 -> x10, starting transfers between devices: 19.1 us -> 14 us  [swap(): return lax.ppermute(array, axis, pairs)]
    while x2 -> x0, local copies, waits for them, and re-layouts: 4.2 us -> none  [parcel_physics(): lax.scan(deposit_block, empty, (host_blocks, source_blocks))]
    dynamic_update_slice x5 -> x0, other arithmetic: 3.56 us -> none  [the longest x4 2.1 us: place(): lax.dynamic_update_slice_in_dim(live, jnp.where(valid, 1.0, old_live), st...]
  transfers between devices with their start and end apart: 12 -> 10, of which waited for: 0 -> 2; matrix products, arithmetic and copies ran while one was open for 41% -> 0% of each run, Pallas kernels for 0% -> 40%
where the time goes in v1:
time: 39.2 us; the launch traced here: 38.9 us
  Pallas kernels  19 us (48%)
  starting transfers between devices  14 us (36%)
  local copies, waits for them, and re-layouts  2.57 us (7%)
  waiting for transfers between devices  1.67 us (4%)
  between operations  1.64 us (4%)
    pallas_call x7, Pallas kernels, call(): pl.pallas_call(kernel, out_shape=outs, in_specs=ins, out_specs=out_specs,...  19 us
    ppermute x10, starting transfers between devices, swap(): return lax.ppermute(array, axis, pairs)  14 us
    unnamed x23, local copies, waits for them, and re-layouts  2.57 us
    ppermute x10, waiting for transfers between devices, swap(): return lax.ppermute(array, axis, pairs)  1.67 us
  transfers between devices with their start and end apart: 10, of which 2 were waited for; matrix products, arithmetic and copies ran while one was open for 0% of the time, Pallas kernels for 40%

profile of v1, /device:TPU:0, one launch (start us, length us, event | category | flops | bytes accessed | tf_op | source)
XLA Modules:
  0.0 38.9 jit_solution(11648258752153116811)
XLA Ops:
  0.6 0.0 copy-start.5
  0.7 0.1 pad_add_fusion.par
  0.7 0.0 copy-start
  0.7 1.2 %copy-done = f32[14,4,32,128]{3,2,1,0:T(8,128)S(1)} copy-done((f32[14,4,32,128]{3,2,1,0:T(8,128)S(1)}, f32[14,4,32,128]{3,2,1,0:T(8,128)}, u32[]{:S(2)}) %copy-start) | copy-done | bytes 917528
  1.9 0.0 copy-start.1
  1.9 0.7 %shard_map.138 = (f32[14,32,128]{2,1,0:T(8,128)S(1)}, f32[14,32,128]{2,1,0:T(8,128)S(1)}, f32[14,4,128]{2,1,0:T(4,128)S(1)}, f32[14,4,128]{2,1,0:T(4,128)S(1)}) custom-call(s32[2]{0:T(128)S(1)} %pad_add_fusion.par, f32[14,4,32,128]{3,2,1,0:T(8,128)S(1)} %copy-done), custom_call_target="tpu_custom_call" | custom-call | bytes 2000000 | tf_op jit(solution)/shard_map/pallas_call | solution.py:48
  2.6 3.1 %collective-permute-start.2 = (f32[14,4,128]{2,1,0:T(4,128)S(1)}, f32[14,4,128]{2,1,0:T(4,128)S(1)}, u32[]{:S(2)}, u32[]{:S(2)}) collective-permute-start(f32[14,4,128]{2,1,0:T(4,128)S(1)} %get-tuple-element.32), channel_id=1, source_target_pairs={{0,1},{1,0},{2,3},{3,2},{4,5},{5,4},{6,7},{7,6},{8,9},{9,8},{10,11... | collective-permute-start | bytes 86024 | tf_op jit(solution)/shard_map/ppermute | solution.py:370
  5.7 0.7 %collective-permute-start.3 = (f32[14,4,128]{2,1,0:T(4,128)S(1)}, f32[14,4,128]{2,1,0:T(4,128)S(1)}, u32[]{:S(2)}, u32[]{:S(2)}) collective-permute-start(f32[14,4,128]{2,1,0:T(4,128)S(1)} %get-tuple-element.33), channel_id=1, source_target_pairs={{1,2},{2,1},{5,6},{6,5},{9,10},{10,9},{13,14},{14,13},{17,18},{18,... | collective-permute-start | bytes 86024 | tf_op jit(solution)/shard_map/ppermute | solution.py:370
  6.4 0.0 copy-start.10
  6.4 1.7 %collective-permute-start.1 = (f32[448,128]{1,0:T(8,128)S(1)}, f32[448,128]{1,0:T(8,128)S(1)}, u32[]{:S(2)}, u32[]{:S(2)}) collective-permute-start(f32[448,128]{1,0:T(8,128)S(1)} %bitcast.5), channel_id=1, source_target_pairs={{4,8},{8,4},{12,16},{16,12},{20,24},{24,20},{28,0},{0,28},{5,9},{9... | collective-permute-start | bytes 688136 | tf_op jit(solution)/shard_map/ppermute | solution.py:370
  8.1 0.0 collective-permute-start
  8.7 0.0 copy-done.10
  8.8 0.0 copy-start.2
  8.8 0.0 copy-start.3
  8.8 0.0 copy-start.4
  8.8 0.1 copy.16.source_map
  8.9 0.0 copy-done.5
  8.9 0.0 copy-done.1
  8.9 0.0 copy-done.7
  8.9 0.0 copy-done.6
  8.9 0.5 %copy-done.2 = f32[3,14]{1,0:T(4,128)S(1)} copy-done((f32[3,14]{1,0:T(4,128)S(1)}, f32[3,14]{1,0:T(4,128)}, u32[]{:S(2)}) %copy-start.2) | copy-done | bytes 192
  9.4 0.0 copy-done.3
  9.5 0.0 copy-done.4
  9.5 0.7 %copy-done.8 = f32[14,14]{1,0:T(8,128)S(1)} copy-done((f32[14,14]{1,0:T(8,128)S(1)}, f32[14,14]{1,0:T(8,128)}, u32[]{:S(2)}) %copy-start.8) | copy-done | bytes 808
  10.2 6.1 %shard_map.137 = (f32[14,4,32,128]{3,2,1,0:T(8,128)S(1)}, f32[16,2304]{1,0:T(8,128)S(1)}, f32[16,128]{1,0:T(8,128)S(1)}, f32[16,128]{1,0:T(8,128)S(1)}) custom-call(s32[2]{0:T(128)S(1)} %pad_add_fusion.par, s32[1,1]{1,0:T(1,128)S(6)} %copy.20.count, f32[14,4,32,128]{3,2,1,0:T(8,128)S(1)} %copy-done.1, f32[3,14]{1,0:T(4,128)S(1)} %copy-done.2, ...), custom_call_target="tpu_custom_call" | custom-call | flops 6000000000 | bytes 4000000 | tf_op jit(solution)/shard_map/pallas_call | solution.py:48
  16.3 0.0 collective-permute-done.2.near
  16.3 0.0 collective-permute-done.3.far
  16.3 0.0 collective-permute-done.1.off
  16.3 0.0 collective-permute-done.on
  16.3 0.9 %shard_map.139 = (f32[14,4,32,128]{3,2,1,0:T(8,128)S(1)}, f32[464,128]{1,0:T(8,128)S(1)}, f32[464,128]{1,0:T(8,128)S(1)}, f32[14,4,128]{2,1,0:T(4,128)S(1)}, f32[14,4,128]{2,1,0:T(4,128)S(1)}) custom-call(s32[2]{0:T(128)S(1)} %pad_add_fusion.par, f32[3,14]{1,0:T(4,128)S(1)} %copy-done.2, ...), custom_call_target="tpu_custom_call", output_to_operand_aliasing={{0}: (2, {})} | custom-call | bytes 3000000 | tf_op jit(solution)/shard_map/pallas_call | solution.py:48
  17.2 0.0 copy-start.9
  17.3 4.4 %collective-permute-start.6 = (f32[14,4,128]{2,1,0:T(4,128)S(1)}, f32[14,4,128]{2,1,0:T(4,128)S(1)}, u32[]{:S(2)}, u32[]{:S(2)}) collective-permute-start(f32[14,4,128]{2,1,0:T(4,128)S(1)} %get-tuple-element.41), channel_id=1, source_target_pairs={{0,1},{1,0},{2,3},{3,2},{4,5},{5,4},{6,7},{7,6},{8,9},{9,8},{10,11... | collective-permute-start | bytes 86024 | tf_op jit(solution)/shard_map/ppermute | solution.py:370
  21.7 0.8 %collective-permute-start.7 = (f32[14,4,128]{2,1,0:T(4,128)S(1)}, f32[14,4,128]{2,1,0:T(4,128)S(1)}, u32[]{:S(2)}, u32[]{:S(2)}) collective-permute-start(f32[14,4,128]{2,1,0:T(4,128)S(1)} %get-tuple-element.42), channel_id=1, source_target_pairs={{1,2},{2,1},{5,6},{6,5},{9,10},{10,9},{13,14},{14,13},{17,18},{18,... | collective-permute-start | bytes 86024 | tf_op jit(solution)/shard_map/ppermute | solution.py:370
  22.5 0.1 collective-permute-start.4
  22.6 1.5 %collective-permute-start.5 = (f32[464,128]{1,0:T(8,128)S(1)}, f32[464,128]{1,0:T(8,128)S(1)}, u32[]{:S(2)}, u32[]{:S(2)}) collective-permute-start(f32[464,128]{1,0:T(8,128)S(1)} %get-tuple-element.40), channel_id=1, source_target_pairs={{4,8},{8,4},{12,16},{16,12},{20,24},{24,20},{28,0},{0,28},{5,9},{9... | collective-permute-start | bytes 712712 | tf_op jit(solution)/shard_map/ppermute | solution.py:370
  24.2 0.0 copy-done.9
  24.2 5.8 %shard_map.140 = (f32[14,4,32,128]{3,2,1,0:T(8,128)S(1)}, f32[16,2304]{1,0:T(8,128)S(1)}) custom-call(s32[2]{0:T(128)S(1)} %pad_add_fusion.par, s32[1,1]{1,0:T(1,128)S(6)} %copy.20.count, f32[14,4,32,128]{3,2,1,0:T(8,128)S(1)} %get-tuple-element.36.gas, f32[3,14]{1,0:T(4,128)S(1)} %copy-done.2, f32[14,14]{1,0:T(8,128)S(1)} %copy-done.9, f32[14]{0:T(128)S(1)} %copy-done.4, ...), custom_call_target="tpu_custom_call" | custom-call | flops 6000000000 | bytes 4000000 | tf_op jit(solution)/shard_map/pallas_call | solution.py:48
  30.0 0.0 collective-permute-done.4.on
  30.0 1.1 %collective-permute-done.5.off = f32[464,128]{1,0:T(8,128)S(1)} collective-permute-done((f32[464,128]{1,0:T(8,128)S(1)}, f32[464,128]{1,0:T(8,128)S(1)}, u32[]{:S(2)}, u32[]{:S(2)}) %collective-permute-start.5) | collective-permute-done | bytes 237600 | tf_op jit(solution)/shard_map/ppermute | solution.py:370
  31.0 1.6 %shard_map.141 = (f32[16,2304]{1,0:T(8,128)S(1)}, f32[16,128]{1,0:T(8,128)S(1)}, f32[16,128]{1,0:T(8,128)S(1)}, f32[2,16,128]{2,1,0:T(8,128)S(1)}, s32[1,1]{1,0:T(1,128)}) custom-call(s32[2]{0:T(128)S(1)} %pad_add_fusion.par, s32[1,1]{1,0:T(1,128)S(6)} %copy.20.count, f32[14,4,32,128]{3,2,1,0:T(8,128)S(1)} %get-tuple-element.36.gas, f32[14]{0:T(128)S(1)} %copy-done.4, ...), custom_call_target="tpu_custom_call" | custom-call | flops 100000000 | bytes 2000000 | tf_op jit(solution)/shard_map/pallas_call | solution.py:48
  32.7 0.2 collective-permute-start.8
  32.8 1.5 %collective-permute-start.9 = (f32[16,128]{1,0:T(8,128)S(1)}, f32[16,128]{1,0:T(8,128)S(1)}, u32[]{:S(2)}, u32[]{:S(2)}) collective-permute-start(f32[16,128]{1,0:T(8,128)S(1)} %get-tuple-element.47), channel_id=1, source_target_pairs={{4,8},{8,4},{12,16},{16,12},{20,24},{24,20},{28,0},{0,28},{5,9},{9... | collective-permute-start | bytes 24584 | tf_op jit(solution)/shard_map/ppermute | solution.py:370
  34.4 0.0 collective-permute-done.6.near
  34.4 0.0 collective-permute-done.7.far
  34.4 1.9 %shard_map.142 = f32[14,4,32,128]{3,2,1,0:T(8,128)} custom-call(s32[2]{0:T(128)S(1)} %pad_add_fusion.par, f32[3,14]{1,0:T(4,128)S(1)} %copy-done.2, f32[14,4,32,128]{3,2,1,0:T(8,128)S(1)} %get-tuple-element.38.base, f32[464,128]{1,0:T(8,128)S(1)} %collective-permute-done.4.on, f32[464,128]{1,0:T(8,128)S(1)} %collective-permute-done.5.off, ...), custom_call_target="tpu_custom_call" | custom-call | flops 100000000 | bytes 3000000 | tf_op jit(solution)/shard_map/pallas_call | solution.py:48
  36.2 0.0 collective-permute-done.8.on
  36.2 0.6 %collective-permute-done.9.off = f32[16,128]{1,0:T(8,128)S(1)} collective-permute-done((f32[16,128]{1,0:T(8,128)S(1)}, f32[16,128]{1,0:T(8,128)S(1)}, u32[]{:S(2)}, u32[]{:S(2)}) %collective-permute-start.9) | collective-permute-done | bytes 8224 | tf_op jit(solution)/shard_map/ppermute | solution.py:370
  36.8 2.0 %shard_map.143 = (f32[1,1,2048]{2,1,0:T(1,128)}, f32[7,1,1,2048]{3,2,1,0:T(1,128)}, s32[1,1,2048]{2,1,0:T(1,128)}, s32[1,1]{1,0:T(1,128)}) custom-call(s32[2]{0:T(128)S(1)} %pad_add_fusion.par, s32[1,1]{1,0:T(1,128)} %get-tuple-element.45.count, f32[16,128]{1,0:T(8,128)S(1)} %collective-permute-done.8.on, f32[16,128]{1,0:T(8,128)S(1)} %collective-permute-done.9.off, ...), custom_call_target="tpu_custom_call" | custom-call | bytes 500000 | tf_op jit(solution)/shard_map/pallas_call | solution.py:48
  (3 shorter events, 0.0 us)
Async XLA Ops:
  0.6 8.2 %copy-start.5 = (f32[7,1,1,2048]{3,2,1,0:T(1,128)S(1)}, f32[7,1,1,2048]{3,2,1,0:T(1,128)}, u32[]{:S(2)}) copy-start(f32[7,1,1,2048]{3,2,1,0:T(1,128)} %refs_1_.1) | copy-start | bytes 172036
  0.7 1.2 %copy-start = (f32[14,4,32,128]{3,2,1,0:T(8,128)S(1)}, f32[14,4,32,128]{3,2,1,0:T(8,128)}, u32[]{:S(2)}) copy-start(f32[14,4,32,128]{3,2,1,0:T(8,128)} %refs_0_.3) | copy-start | bytes 2752516
  1.9 7.0 %copy-start.1 = (f32[14,4,32,128]{3,2,1,0:T(8,128)S(1)}, f32[14,4,32,128]{3,2,1,0:T(8,128)}, u32[]{:S(2)}) copy-start(f32[14,4,32,128]{3,2,1,0:T(8,128)} %refs_0_.3) | copy-start | bytes 2752516
  1.9 7.0 %copy-start.7 = (s32[1,1,2048]{2,1,0:T(1,128)S(1)}, s32[1,1,2048]{2,1,0:T(1,128)}, u32[]{:S(2)}) copy-start(s32[1,1,2048]{2,1,0:T(1,128)} %refs_2_.1) | copy-start | bytes 24580
  2.6 13.6 %collective-permute-start.2 = (f32[14,4,128]{2,1,0:T(4,128)S(1)}, f32[14,4,128]{2,1,0:T(4,128)S(1)}, u32[]{:S(2)}, u32[]{:S(2)}) collective-permute-start(f32[14,4,128]{2,1,0:T(4,128)S(1)} %get-tuple-element.32), channel_id=1, source_target_pairs={{0,1},{1,0},{2,3},{3,2},{4,5},{5,4},{6,7},{7,6},{8,9},{9,8},{10,11... | collective-permute-start | bytes 86024 | tf_op jit(solution)/shard_map/ppermute | solution.py:370
  5.7 10.6 %collective-permute-start.3 = (f32[14,4,128]{2,1,0:T(4,128)S(1)}, f32[14,4,128]{2,1,0:T(4,128)S(1)}, u32[]{:S(2)}, u32[]{:S(2)}) collective-permute-start(f32[14,4,128]{2,1,0:T(4,128)S(1)} %get-tuple-element.33), channel_id=1, source_target_pairs={{1,2},{2,1},{5,6},{6,5},{9,10},{10,9},{13,14},{14,13},{17,18},{18,... | collective-permute-start | bytes 86024 | tf_op jit(solution)/shard_map/ppermute | solution.py:370
  6.4 2.4 %copy-start.10 = (f32[14,8]{0,1:T(8,128)S(1)}, f32[14,8]{0,1:T(8,128)}, u32[]{:S(2)}) copy-start(f32[14,8]{0,1:T(8,128)} %param.14) | copy-start | bytes 1348
  6.4 9.9 %collective-permute-start.1 = (f32[448,128]{1,0:T(8,128)S(1)}, f32[448,128]{1,0:T(8,128)S(1)}, u32[]{:S(2)}, u32[]{:S(2)}) collective-permute-start(f32[448,128]{1,0:T(8,128)S(1)} %bitcast.5), channel_id=1, source_target_pairs={{4,8},{8,4},{12,16},{16,12},{20,24},{24,20},{28,0},{0,28},{5,9},{9... | collective-permute-start | bytes 688136 | tf_op jit(solution)/shard_map/ppermute | solution.py:370
  8.1 0.8 %copy-start.6 = (f32[1,1,2048]{2,1,0:T(1,128)S(1)}, f32[1,1,2048]{2,1,0:T(1,128)}, u32[]{:S(2)}) copy-start(f32[1,1,2048]{2,1,0:T(1,128)} %refs_0_.2) | copy-start | bytes 24580
  8.1 8.2 %collective-permute-start = (f32[448,128]{1,0:T(8,128)S(1)}, f32[448,128]{1,0:T(8,128)S(1)}, u32[]{:S(2)}, u32[]{:S(2)}) collective-permute-start(f32[448,128]{1,0:T(8,128)S(1)} %bitcast.4), channel_id=1, source_target_pairs={{0,4},{4,0},{8,12},{12,8},{16,20},{20,16},{24,28},{28,24},{1,5},{5... | collective-permute-start | bytes 688136 | tf_op jit(solution)/shard_map/ppermute | solution.py:370
  8.8 0.7 %copy-start.2 = (f32[3,14]{1,0:T(4,128)S(1)}, f32[3,14]{1,0:T(4,128)}, u32[]{:S(2)}) copy-start(f32[3,14]{1,0:T(4,128)} %transport.7) | copy-start | bytes 508
  8.8 0.7 %copy-start.3 = (s32[1,1,2,2,128]{4,3,2,1,0:T(2,128)S(1)}, s32[1,1,2,2,128]{4,3,2,1,0:T(2,128)}, u32[]{:S(2)}) copy-start(s32[1,1,2,2,128]{4,3,2,1,0:T(2,128)} %lists.5) | copy-start | bytes 6148
  8.8 0.7 %copy-start.4 = (f32[14]{0:T(128)S(1)}, f32[14]{0:T(128)}, u32[]{:S(2)}) copy-start(f32[14]{0:T(128)} %evap.5) | copy-start | bytes 172
  9.5 0.7 %copy-start.8 = (f32[14,14]{1,0:T(8,128)S(1)}, f32[14,14]{1,0:T(8,128)}, u32[]{:S(2)}) copy-start(f32[14,14]{1,0:T(8,128)} %chemistry.3) | copy-start | bytes 2356
  17.2 6.9 %copy-start.9 = (f32[14,14]{1,0:T(8,128)S(1)}, f32[14,14]{1,0:T(8,128)}, u32[]{:S(2)}) copy-start(f32[14,14]{1,0:T(8,128)} %chemistry.3) | copy-start | bytes 2356
  17.3 17.1 %collective-permute-start.6 = (f32[14,4,128]{2,1,0:T(4,128)S(1)}, f32[14,4,128]{2,1,0:T(4,128)S(1)}, u32[]{:S(2)}, u32[]{:S(2)}) collective-permute-start(f32[14,4,128]{2,1,0:T(4,128)S(1)} %get-tuple-element.41), channel_id=1, source_target_pairs={{0,1},{1,0},{2,3},{3,2},{4,5},{5,4},{6,7},{7,6},{8,9},{9,8},{10,11... | collective-permute-start | bytes 86024 | tf_op jit(solution)/shard_map/ppermute | solution.py:370
  21.7 12.7 %collective-permute-start.7 = (f32[14,4,128]{2,1,0:T(4,128)S(1)}, f32[14,4,128]{2,1,0:T(4,128)S(1)}, u32[]{:S(2)}, u32[]{:S(2)}) collective-permute-start(f32[14,4,128]{2,1,0:T(4,128)S(1)} %get-tuple-element.42), channel_id=1, source_target_pairs={{1,2},{2,1},{5,6},{6,5},{9,10},{10,9},{13,14},{14,13},{17,18},{18,... | collective-permute-start | bytes 86024 | tf_op jit(solution)/shard_map/ppermute | solution.py:370
  22.5 7.4 %collective-permute-start.4 = (f32[464,128]{1,0:T(8,128)S(1)}, f32[464,128]{1,0:T(8,128)S(1)}, u32[]{:S(2)}, u32[]{:S(2)}) collective-permute-start(f32[464,128]{1,0:T(8,128)S(1)} %get-tuple-element.39), channel_id=1, source_target_pairs={{0,4},{4,0},{8,12},{12,8},{16,20},{20,16},{24,28},{28,24},{1,5},{5... | collective-permute-start | bytes 712712 | tf_op jit(solution)/shard_map/ppermute | solution.py:370
  22.6 8.4 %collective-permute-start.5 = (f32[464,128]{1,0:T(8,128)S(1)}, f32[464,128]{1,0:T(8,128)S(1)}, u32[]{:S(2)}, u32[]{:S(2)}) collective-permute-start(f32[464,128]{1,0:T(8,128)S(1)} %get-tuple-element.40), channel_id=1, source_target_pairs={{4,8},{8,4},{12,16},{16,12},{20,24},{24,20},{28,0},{0,28},{5,9},{9... | collective-permute-start | bytes 712712 | tf_op jit(solution)/shard_map/ppermute | solution.py:370
  32.7 3.5 %collective-permute-start.8 = (f32[16,128]{1,0:T(8,128)S(1)}, f32[16,128]{1,0:T(8,128)S(1)}, u32[]{:S(2)}, u32[]{:S(2)}) collective-permute-start(f32[16,128]{1,0:T(8,128)S(1)} %get-tuple-element.46), channel_id=1, source_target_pairs={{0,4},{4,0},{8,12},{12,8},{16,20},{20,16},{24,28},{28,24},{1,5},{5... | collective-permute-start | bytes 24584 | tf_op jit(solution)/shard_map/ppermute | solution.py:370
  32.8 4.0 %collective-permute-start.9 = (f32[16,128]{1,0:T(8,128)S(1)}, f32[16,128]{1,0:T(8,128)S(1)}, u32[]{:S(2)}, u32[]{:S(2)}) collective-permute-start(f32[16,128]{1,0:T(8,128)S(1)} %get-tuple-element.47), channel_id=1, source_target_pairs={{4,8},{8,4},{12,16},{16,12},{20,24},{24,20},{28,0},{0,28},{5,9},{9... | collective-permute-start | bytes 24584 | tf_op jit(solution)/shard_map/ppermute | solution.py:370

commit v2 on v1

v2 whole, which is shorter than its diff:
```python
import functools

import jax
import jax.numpy as jnp
from jax import lax
from jax.experimental import pallas as pl
from jax.experimental.pallas import tpu as pltpu
from jax.sharding import PartitionSpec as P

DT = 0.5
RELAX = 0.3
EVAP = 0.5
F32 = jnp.float32
BF16 = jnp.bfloat16
ROWS = 16
HOST = 8
LIVE = 9
GONE = 10
LANES = 128
LIMIT = 40 << 20

VMEM = pl.BlockSpec(memory_space=pltpu.VMEM)
HBM = pl.BlockSpec(memory_space=pltpu.HBM)


def iota(shape, dim, dtype=jnp.int32):
    return lax.broadcasted_iota(dtype, shape, dim)


def parts_of(values, count):
    parts = []
    for _ in range(count - 1):
        part = values.astype(BF16)
        parts.append(part)
        values = values - part.astype(F32)
    return parts + [values.astype(BF16)]


def hot(mask):
    return mask.astype(F32).astype(BF16)


def across(left, right):
    return lax.dot_general(left, right, (((1,), (1,)), ((), ())), preferred_element_type=F32)


def call(kernel, outs, ins, out_specs, args, scratch=(), aliases=None, flops=0, moved=0, trans=0):
    return pl.pallas_call(
        kernel,
        out_shape=outs,
        in_specs=ins,
        out_specs=out_specs,
        scratch_shapes=list(scratch),
        input_output_aliases=aliases or {},
        compiler_params=pltpu.CompilerParams(vmem_limit_bytes=LIMIT),
        cost_estimate=pl.CostEstimate(flops=flops, bytes_accessed=moved, transcendentals=trans),
    )(*args)


def shape(dims, dtype=F32):
    return jax.ShapeDtypeStruct(dims, dtype)


def odd(axis):
    return lax.axis_index(axis) % 2


def pack_kernel(gas, *refs):
    small = (len(refs) - 3) // 2
    sources, (on, off), targets = refs[:small], refs[small : small + 2], refs[small + 2 : -1]
    sems = refs[-1]
    last = gas.shape[1] - 1
    flip = odd("azim")
    pairs = [(gas.at[:, last * flip], off), (gas.at[:, last * (1 - flip)], on)]
    pairs += list(zip(sources, targets))
    copies = [pltpu.make_async_copy(src, dst, sems.at[k]) for k, (src, dst) in enumerate(pairs)]
    for copy in copies:
        copy.start()
    for copy in copies:
        copy.wait()


def column_of(row):
    n = row.shape[1]
    square = jnp.broadcast_to(row, (n, n))
    return jnp.sum(jnp.where(iota((n, n), 0) == iota((n, n), 1), square, 0.0), axis=1, keepdims=True)


NU, UPPER, LOWER, EAST, WEST, PULL, SOURCE = range(7)


def fill_table(table, transport, chemistry, evap, source_map):
    nf = chemistry.shape[0]
    nu, swirl, axial = (column_of(transport[k : k + 1]) for k in range(3))
    columns = [nu, nu - 0.5 * axial, nu + 0.5 * axial, nu - 0.5 * swirl, nu + 0.5 * swirl]
    columns.append(column_of(evap[...]))
    columns += [column_of(source_map[k : k + 1]) for k in range(source_map.shape[0])]
    columns += [chemistry[:, g : g + 1] for g in range(nf)]
    for k, column in enumerate(columns):
        table[k, :nf] = jnp.broadcast_to(column, (nf, LANES))


def spread(table, k, f, rows):
    return jnp.broadcast_to(table[k, f : f + 1], (rows, LANES))


def inner_terms(gas, table, tanh):
    nf, ca, cr, cz = gas.shape
    lane = iota((cr, cz), 1)
    row = iota((cr, cz), 0)
    chem = table.shape[0] - nf
    for f in range(nf):
        nu, upper, lower, east, west = (spread(table, k, f, cr) for k in (NU, UPPER, LOWER, EAST, WEST))
        totals = []
        for a in range(ca):
            here = gas[f, a]
            total = nu * (
                jnp.where(row == cr - 1, 0.0, pltpu.roll(here, cr - 1, 0))
                + jnp.where(row == 0, 0.0, pltpu.roll(here, 1, 0))
                - 6.0 * here
            )
            total += upper * jnp.where(lane == cz - 1, 0.0, pltpu.roll(here, cz - 1, 1))
            total += lower * jnp.where(lane == 0, 0.0, pltpu.roll(here, 1, 1))
            if a < ca - 1:
                total += east * gas[f, a + 1]
            if a > 0:
                total += west * gas[f, a - 1]
            totals.append(total)
        for g in range(nf):
            rate = spread(table, chem + g, f, cr)
            for a in range(ca):
                totals[a] += rate * tanh[g, a]
        for a in range(ca):
            yield f, a, totals[a]


def probe_all(gas, host, table, hots, probed):
    nf, ca, cr, cz = gas.shape
    slots = host.shape[1]
    width = ca * cz
    for f in range(nf):
        for a in range(ca):
            upper, lower = parts_of(gas[f, a], 2)
            table[f * cr : (f + 1) * cr, a * cz : (a + 1) * cz] = upper
            table[f * cr : (f + 1) * cr, width + a * cz : width + (a + 1) * cz] = lower
    span = cr * cz
    block = 256
    for b in range(slots // block):
        cells = host[:, b * block : (b + 1) * block]
        column = (cells // span) * cz + cells % cz
        row = (cells // cz) % cr
        hots[:, b * block : (b + 1) * block] = hot(iota((width, block), 0) == column)
        ahot = hots[:, b * block : (b + 1) * block]
        found = jnp.dot(table[:, :width], ahot, preferred_element_type=F32)
        found += jnp.dot(table[:, width:], ahot, preferred_element_type=F32)
        mask = iota((cr, block), 0) == row
        found = jnp.where(mask[None], found.reshape(nf, cr, block), 0.0)
        probed[:nf, b * block : (b + 1) * block] = jnp.sum(found, axis=1)


def react(probed, attr, live, table, nf):
    pull = jnp.sum(table[PULL, :nf, 0:1] * probed[:nf], axis=0, keepdims=True)
    sig = jax.nn.sigmoid(pull + attr[1:2])
    mdot = EVAP * attr[0:1] * sig * live
    source = table[SOURCE, :nf, 0:1] * attr[0:1]
    for k in range(1, attr.shape[0]):
        source += table[SOURCE + k, :nf, 0:1] * attr[k : k + 1]
    source = source * mdot
    rows = [attr[0:1] - DT * mdot]
    rows.append(attr[1:2] + DT * RELAX * (probed[4:5] - attr[1:2]))
    rows.append(attr[2:5] + DT * RELAX * (probed[1:4] - attr[2:5]))
    rows.append(attr[5:8])
    return rows, source


def deposit_all(source, host, hots, shapes, reach, total):
    nf, ca, cr, cz = shapes
    width = ca * cz
    block = 512 if reach % 512 == 0 else 128
    for b in range(reach // block):
        cells = host[:, b * block : (b + 1) * block]
        row = (cells // cz) % cr
        mask = iota((cr, block), 0) == row
        spread = jnp.where(mask[None], source[:nf, b * block : (b + 1) * block][:, None, :], 0.0)
        upper, lower = parts_of(spread.reshape(nf * cr, block), 2)
        ahot = hots[:, b * block : (b + 1) * block]
        part = across(upper, ahot) + across(lower, ahot)
        if b == 0:
            total[...] = part
        else:
            total[...] += part


def list_hots(lists, section, slots, lhot):
    width = lists.shape[-1]
    for d in range(2):
        names = lists[0, 0, section, d : d + 1, :].astype(F32)
        column = jnp.broadcast_to(names, (width, width)).T
        for b in range(slots // width):
            at = iota((width, width), 1).astype(F32) + float(b * width)
            lhot[d * width : (d + 1) * width, b * width : (b + 1) * width] = hot(column == at)


def gather(parcels, lhot):
    parts = jnp.concatenate(parts_of(parcels, 3), axis=0)
    taken = across(parts, lhot)
    return taken[:ROWS] + taken[ROWS : 2 * ROWS] + taken[2 * ROWS :]


def gone_from(lhot):
    ones = jnp.ones((8, lhot.shape[0]), BF16)
    return jnp.dot(ones, lhot, preferred_element_type=F32)[0:1]


def packs_of(taken, lists, section, span, slots):
    width = lists.shape[-1]
    packs = []
    for d in range(2):
        valid = lists[0, 0, section, d : d + 1, :] < slots
        pack = taken[:, d * width : (d + 1) * width]
        cell = pack[HOST : HOST + 1].astype(jnp.int32) % span
        cell = jnp.where(valid, cell.astype(F32), -1.0)
        row = iota(pack.shape, 0)
        pack = jnp.where(row == HOST, cell, jnp.where(valid & (row < HOST), pack, 0.0))
        packs.append(pack)
    left, right = packs
    flip = odd("azim") == 1
    return jnp.where(flip, left, right), jnp.where(flip, right, left)


def send_rows(gas, near, far):
    cr = gas.shape[2]
    flip = odd("radax") == 1
    for f in range(gas.shape[0]):
        low, high = gas[f, :, 0, :], gas[f, :, cr - 1, :]
        near[f] = jnp.where(flip, low, high)
        far[f] = jnp.where(flip, high, low)


def probe_one_kernel(
    count, gas, transport, chemistry, evap, source_map, lists, mass, state, host_in,
    near, far, parcels, on, off, table, hots, source, cells, probed, lhot,
):
    nf, ca, cr, cz = gas.shape
    slots = probed.shape[1]
    send_rows(gas, near, far)
    fill_table(table, transport, chemistry, evap, source_map)
    host = host_in[0]
    live = (iota((1, slots), 1) < count[...]).astype(F32)
    attr = jnp.concatenate([mass[0]] + [state[k, 0] for k in range(state.shape[0])], axis=0)
    source[:nf] = parcel_work(gas, host, attr, live, table, parcels, cells, hots, probed)
    list_hots(lists, 0, slots, lhot)
    on[...], off[...] = packs_of(gather(parcels[:, :slots], lhot[...]), lists, 0, cr * cz, slots)
    parcels[LIVE : LIVE + 1, :slots] = jnp.where(gone_from(lhot[...]) > 0.5, 0.0, live)


def field_one_kernel(spare, gas, table, parcels, hots, source, out, total, tanh):
    nf, ca, cr, cz = gas.shape
    slots = hots.shape[1]
    for g in range(nf):
        tanh[g] = jnp.tanh(gas[g])
    host = parcels[HOST : HOST + 1, :slots].astype(jnp.int32)
    deposit_all(source, host, hots, gas.shape, slots - spare, total)
    for f, a, terms in inner_terms(gas, table, tanh):
        out[f, a] = gas[f, a] + DT * (terms + total[f * cr : (f + 1) * cr, a * cz : (a + 1) * cz])


def probe_two_kernel(
    gas, table, lists, old, near, far, parcels, hots, source, taken, lhot, cells, probed
):
    slots = probed.shape[1]
    send_rows(gas, near, far)
    host = old[HOST : HOST + 1, :slots].astype(jnp.int32)
    source[: gas.shape[0]] = parcel_work(
        gas, host, old[0:HOST, :slots], old[LIVE : LIVE + 1, :slots], table, parcels, cells, hots, probed
    )
    list_hots(lists, 1, slots, lhot)
    taken[...] = gather(parcels[:, :slots], lhot[...])
    parcels[GONE : GONE + 1, :slots] = gone_from(lhot[...])


def field_two_kernel(spare, gas, table, old_gas, parcels, hots, source, out, total, tanh):
    nf, ca, cr, cz = gas.shape
    slots = hots.shape[1]
    for g in range(nf):
        tanh[g] = jnp.tanh(gas[g])
    host = parcels[HOST : HOST + 1, :slots].astype(jnp.int32)
    deposit_all(source, host, hots, gas.shape, slots - spare, total)
    for f, a, terms in inner_terms(gas, table, tanh):
        terms += total[f * cr : (f + 1) * cr, a * cz : (a + 1) * cz]
        out[f, a] = 0.5 * (old_gas[f, a] + gas[f, a] + DT * terms)


def parcel_work(gas, host, attr, live, table, parcels, cells, hots, probed):
    slots = probed.shape[1]
    probe_all(gas, host, cells, hots, probed)
    rows, source = react(probed[...], attr, live, table, gas.shape[0])
    parcels[...] = jnp.zeros_like(parcels)
    parcels[0:ROWS, :slots] = jnp.concatenate(
        rows + [host.astype(F32), live, jnp.zeros((ROWS - LIVE - 1, slots), F32)], axis=0
    )
    return source


def edge_terms(scale, table, out, on, off, near, far):
    nf, ca, cr, cz = out.shape
    flip_a, flip_r = odd("azim") == 1, odd("radax") == 1
    for f in range(nf):
        got_on, got_off = on[f * cr : (f + 1) * cr], off[f * cr : (f + 1) * cr]
        east = jnp.where(flip_a, got_off, got_on)
        west = jnp.where(flip_a, got_on, got_off)
        out[f, 0] += (scale * spread(table, WEST, f, cr)) * west
        out[f, ca - 1] += (scale * spread(table, EAST, f, cr)) * east
        north = jnp.where(flip_r, far[f], near[f])
        south = jnp.where(flip_r, near[f], far[f])
        nu = scale * spread(table, NU, f, ca)
        out[f, :, 0, :] += nu * south
        out[f, :, cr - 1, :] += nu * north


def edge_kernel(table, base, on, off, near, far, pack_on, pack_off, out, send_on, send_off):
    nf, ca, cr, cz = out.shape
    out[...] = base[...]
    edge_terms(DT, table, out, on, off, near, far)
    flip = odd("azim") == 1
    for f in range(nf):
        low, high = out[f, 0], out[f, ca - 1]
        send_on[f * cr : (f + 1) * cr] = jnp.where(flip, low, high)
        send_off[f * cr : (f + 1) * cr] = jnp.where(flip, high, low)
    send_on[nf * cr :] = pack_on[...]
    send_off[nf * cr :] = pack_off[...]


def put(parcels, pack, start, live):
    width = pack.shape[1]
    row = iota(pack.shape, 0)
    pack = jnp.where(row == LIVE, live, pack)
    shift = start % width
    first = pl.multiple_of((start // width) * width, width)
    pack = pltpu.roll(pack, shift, 1)
    lane = iota(pack.shape, 1)
    taken = pack[LIVE : LIVE + 1] > 0.5
    here = parcels[:, pl.ds(first, width)]
    parcels[:, pl.ds(first, width)] = jnp.where(taken & (lane >= shift) & (row != GONE), pack, here)
    second = pl.multiple_of(first + width, width)
    here = parcels[:, pl.ds(second, width)]
    parcels[:, pl.ds(second, width)] = jnp.where(taken & (lane < shift) & (row != GONE), pack, here)


def sides(on, off):
    flip = odd("azim") == 1
    return jnp.where(flip, on, off), jnp.where(flip, off, on)


def scalar(ref):
    return jnp.sum(ref[...].astype(F32)).astype(jnp.int32)


def arrive_kernel(
    count, gas, table, lists, on, off, old, taken, lhot, parcels, send_on, send_off, sources, used, cells
):
    nf, ca, cr, cz = gas.shape
    slots = lhot.shape[1]
    base = nf * cr
    packs = sides(on[base:], off[base:])
    parcels[...] = old[...]
    start = scalar(count)
    for side in range(2):
        layer = side * (ca - 1)
        pack = packs[side]
        cell = pack[HOST : HOST + 1].astype(jnp.int32)
        live = (cell >= 0).astype(F32)
        for f in range(nf):
            upper, lower = parts_of(gas[f, layer], 2)
            cells[f * cr : (f + 1) * cr, :cz] = upper
            cells[f * cr : (f + 1) * cr, cz:] = lower
        zhot = hot(iota((cz, cell.shape[1]), 0) == cell % cz)
        found = jnp.dot(cells[:, :cz], zhot, preferred_element_type=F32)
        found += jnp.dot(cells[:, cz:], zhot, preferred_element_type=F32)
        mask = iota((cr, cell.shape[1]), 0) == cell // cz
        found = jnp.where(mask[None], found.reshape(nf, cr, cell.shape[1]), 0.0)
        probed = jnp.sum(found, axis=1)
        rows, source = react(probed, pack[0:HOST], live, table, nf)
        sources[side, :nf] = source
        sources[side, nf : nf + 1] = pack[HOST : HOST + 1]
        home = (cell + layer * cr * cz).astype(F32)
        moved = jnp.concatenate(rows + [home, live, jnp.zeros((ROWS - LIVE - 1, cell.shape[1]), F32)], 0)
        put(parcels, moved, start, live)
        start = start + jnp.sum(live).astype(jnp.int32)
    used[...] = jnp.broadcast_to(start, (1, 1))
    width = lists.shape[-1]
    first = pl.multiple_of(scalar(count), width)
    window = pl.ds(first, 2 * width)
    again = gather(parcels[:, window], lhot[:, window])
    names = jnp.concatenate([lists[0, 0, 1, d : d + 1, :] for d in range(2)], axis=1)
    inside = (names >= first) & (names < first + 2 * width)
    both = jnp.where(inside, again, taken[...])
    send_on[...], send_off[...] = packs_of(both, lists, 1, cr * cz, slots)
    gone = parcels[GONE : GONE + 1, :slots] > 0.5
    parcels[LIVE : LIVE + 1, :slots] = jnp.where(gone, 0.0, parcels[LIVE : LIVE + 1, :slots])


def finish_kernel(table, base, on, off, near, far, sources, out):
    nf, ca, cr, cz = out.shape
    out[...] = base[...]
    edge_terms(0.5 * DT, table, out, on, off, near, far)
    for side in range(2):
        layer = side * (ca - 1)
        cell = sources[side, nf : nf + 1].astype(jnp.int32)
        mask = iota((cr, cell.shape[1]), 0) == cell // cz
        laid = jnp.where(mask[None], sources[side, :nf][:, None, :], 0.0)
        upper, lower = parts_of(laid.reshape(nf * cr, cell.shape[1]), 2)
        zhot = hot(iota((cz, cell.shape[1]), 0) == cell % cz)
        total = across(upper, zhot) + across(lower, zhot)
        for f in range(nf):
            out[f, layer] += (0.5 * DT) * total[f * cr : (f + 1) * cr]


def place_kernel(far_offset, count, on, off, old, mass, state, host, used, parcels):
    slots = mass.shape[-1]
    parcels[...] = old[...]
    packs = sides(on[...], off[...])
    start = scalar(count)
    for side in range(2):
        pack = packs[side]
        live = (pack[HOST : HOST + 1] >= 0.0).astype(F32)
        row = iota(pack.shape, 0)
        pack = jnp.where(row == HOST, pack + float(side * far_offset), pack)
        put(parcels, pack, start, live)
        start = start + jnp.sum(live).astype(jnp.int32)
    used[...] = jnp.broadcast_to(start, (1, 1))
    live = parcels[LIVE : LIVE + 1, :slots] > 0.5
    mass[0] = jnp.where(live, parcels[0:1, :slots], 0.0)
    for k in range(state.shape[0]):
        state[k, 0] = jnp.where(live, parcels[k + 1 : k + 2, :slots], 0.0)
    host[0] = jnp.where(live, parcels[HOST : HOST + 1, :slots].astype(jnp.int32), -1)


def swap(array, axis, phase, wrap):
    size = lax.axis_size(axis)
    pairs = []
    for i in range(phase, size if wrap else size - 1, 2):
        j = (i + 1) % size
        pairs += [(i, j), (j, i)]
    return lax.ppermute(array, axis, pairs)


def on_device(
    gas, transport, chemistry, evap, source_map, mass, state, host, count, crossing
):
    nf, ca, cr, cz = gas.shape
    slots = mass.shape[-1]
    width = crossing.shape[-1]
    padded = slots + 2 * width
    ring, pack = shape((nf, ca, cz)), shape((ROWS, width))
    one = shape((1, 1), jnp.int32)
    grid, slotted = shape(gas.shape), shape((ROWS, padded))
    small = (gas, transport, chemistry, evap.reshape(1, nf), source_map.T, mass, state, host, crossing)
    on, off, *small = call(
        pack_kernel,
        [shape((nf, cr, cz)), shape((nf, cr, cz))] + [shape(v.shape, v.dtype) for v in small],
        [HBM] * (1 + len(small)),
        [VMEM] * (2 + len(small)),
        tuple(pltpu.with_memory_space_constraint(v, pltpu.HBM) for v in (gas,) + small),
        scratch=[pltpu.SemaphoreType.DMA((2 + len(small),))],
        moved=2_000_000,
    )
    gas, transport, chemistry, evap, source_map, mass, state, host, crossing = small
    off = swap(off.reshape(nf * cr, cz), "azim", 1, True)
    on = swap(on.reshape(nf * cr, cz), "azim", 0, True)

    hots, lhot = shape((ca * cz, slots), BF16), shape((2 * width, slots), BF16)
    source = shape((ROWS, slots))
    probe_scratch = [pltpu.VMEM((nf * cr, 2 * ca * cz), BF16), pltpu.VMEM((ROWS, slots), F32)]
    field_scratch = [pltpu.VMEM((nf * cr, ca * cz), F32), pltpu.VMEM(gas.shape, F32)]
    heavy = dict(flops=3_000_000_000, moved=2_000_000, trans=300_000)
    near, far, parcels, pack_on, pack_off, table, cell_hots, sources = call(
        probe_one_kernel,
        [ring, ring, slotted, pack, pack, shape((SOURCE + source_map.shape[0] + nf, ROWS, LANES)), hots, source],
        [VMEM] * 10,
        [VMEM] * 8,
        (count, gas, transport, chemistry, evap, source_map, crossing, mass, state, host),
        scratch=probe_scratch + [pltpu.VMEM(lhot.shape, BF16)],
        **heavy,
    )
    near = swap(near, "radax", 0, False)
    far = swap(far, "radax", 1, False)
    base = call(
        functools.partial(field_one_kernel, 4 * width),
        grid,
        [VMEM] * 5,
        VMEM,
        (gas, table, parcels, cell_hots, sources),
        scratch=field_scratch,
        flops=1_000_000,
        moved=10_000,
    )
    longer = shape((nf * cr + ROWS, cz))
    section_one, on, off = call(
        edge_kernel,
        [grid, longer, longer],
        [VMEM] * 8,
        [VMEM] * 3,
        (table, base, on, off, near, far, pack_on, pack_off),
        aliases={1: 0},
        moved=3_000_000,
    )
    off = swap(off, "azim", 1, True)
    on = swap(on, "azim", 0, True)
    near, far, parcels, cell_hots, sources, taken, named = call(
        probe_two_kernel,
        [ring, ring, slotted, hots, source, shape((ROWS, 2 * width)), lhot],
        [VMEM] * 4,
        [VMEM] * 7,
        (section_one, table, crossing, parcels),
        scratch=probe_scratch,
        **heavy,
    )
    near = swap(near, "radax", 0, False)
    far = swap(far, "radax", 1, False)
    base = call(
        functools.partial(field_two_kernel, 4 * width),
        grid,
        [VMEM] * 6,
        VMEM,
        (section_one, table, gas, parcels, cell_hots, sources),
        scratch=field_scratch,
        flops=1_000_000,
        moved=10_000,
    )
    parcels, pack_on, pack_off, sources, count = call(
        arrive_kernel,
        [slotted, pack, pack, shape((2, ROWS, width)), one],
        [VMEM] * 9,
        [VMEM] * 5,
        (count, section_one, table, crossing, on, off, parcels, taken, named),
        scratch=[pltpu.VMEM((nf * cr, 2 * cz), BF16)],
        flops=100_000_000,
        moved=2_000_000,
    )
    pack_off = swap(pack_off, "azim", 1, True)
    pack_on = swap(pack_on, "azim", 0, True)
    gas_next = call(
        finish_kernel,
        shape(gas.shape),
        [VMEM] * 7,
        VMEM,
        (table, base, on, off, near, far, sources),
        flops=100_000_000,
        moved=3_000_000,
    )
    mass_next, state_next, host_next, count_next = call(
        functools.partial(place_kernel, (ca - 1) * cr * cz),
        [shape(mass.shape), shape(state.shape), shape(host.shape, jnp.int32), one],
        [VMEM] * 4,
        [VMEM] * 4,
        (count, pack_on, pack_off, parcels),
        scratch=[pltpu.VMEM((ROWS, padded), F32)],
        moved=500_000,
    )
    return gas_next, mass_next, state_next, host_next, count_next


def solution(mesh):
    in_specs = (
        P(None, "azim", "radax", None),
        P(),
        P(),
        P(),
        P(),
        P("azim", "radax", None),
        P(None, "azim", "radax", None),
        P("azim", "radax", None),
        P("azim", "radax"),
        P("azim", "radax", None, None, None),
    )
    out_specs = (
        P(None, "azim", "radax", None),
        P("azim", "radax", None),
        P(None, "azim", "radax", None),
        P("azim", "radax", None),
        P("azim", "radax"),
    )
    return jax.shard_map(
        on_device, mesh=mesh, in_specs=in_specs, out_specs=out_specs, check_vma=False
    )
```

time: 39.2 us -> 33.3 us (0.85)
  local copies, waits for them, and re-layouts: 2.57 us -> 0 us
  Pallas kernels: 19 us -> 16.6 us
  waiting for transfers between devices: 1.67 us -> 0.9 us
    unnamed x23 -> x0, local copies, waits for them, and re-layouts: 2.57 us -> none
    pallas_call x7 -> x9, Pallas kernels: 19 us -> 16.6 us  [call(): pl.pallas_call(kernel, out_shape=outs, in_specs=ins, out_specs=out_specs,...]
    ppermute x10, waiting for transfers between devices: 1.67 us -> 0.9 us  [swap(): return lax.ppermute(array, axis, pairs)]
  transfers between devices with their start and end apart: 10 -> 10, of which waited for: 2 -> 1; matrix products, arithmetic and copies ran while one was open for 0% -> 0% of each run, Pallas kernels for 40% -> 40%
where the time goes in v2:
time: 33.3 us; the launch traced here: 33.1 us
  Pallas kernels  16.6 us (50%)
  starting transfers between devices  14.1 us (42%)
  between operations  1.4 us (4%)
  waiting for transfers between devices  0.9 us (3%)
    pallas_call x9, Pallas kernels, call(): pl.pallas_call(kernel, out_shape=outs, in_specs=ins, out_specs=out_specs,...  16.6 us
    ppermute x10, starting transfers between devices, swap(): return lax.ppermute(array, axis, pairs)  14.1 us
    ppermute x10, waiting for transfers between devices, swap(): return lax.ppermute(array, axis, pairs)  0.9 us
  transfers between devices with their start and end apart: 10, of which 1 were waited for; matrix products, arithmetic and copies ran while one was open for 0% of the time, Pallas kernels for 40%

profile of v2, /device:TPU:0, one launch (start us, length us, event | category | flops | bytes accessed | tf_op | source)
XLA Modules:
  0.0 33.1 jit_solution(4927502829235013403)
XLA Ops:
  0.6 1.5 %shard_map.137 = (f32[14,32,128]{2,1,0:T(8,128)S(1)}, f32[14,32,128]{2,1,0:T(8,128)S(1)}, f32[14,4,32,128]{3,2,1,0:T(8,128)S(1)}, f32[3,14]{1,0:T(4,128)S(1)}, f...) custom-call(f32[14,4,32,128]{3,2,1,0:T(8,128)} %refs_0_.1, ...), custom_call_target="tpu_custom_call" | custom-call | bytes 2000000 | tf_op jit(solution)/shard_map/pallas_call | solution.py:48
  2.2 0.5 %collective-permute-start = (f32[448,128]{1,0:T(8,128)S(1)}, f32[448,128]{1,0:T(8,128)S(1)}, u32[]{:S(2)}, u32[]{:S(2)}) collective-permute-start(f32[448,128]{1,0:T(8,128)S(1)} %bitcast.5), channel_id=1, source_target_pairs={{0,4},{4,0},{8,12},{12,8},{16,20},{20,16},{24,28},{28,24},{1,5},{5... | collective-permute-start | bytes 688136 | tf_op jit(solution)/shard_map/ppermute | solution.py:445
  2.7 3.6 %collective-permute-start.1 = (f32[448,128]{1,0:T(8,128)S(1)}, f32[448,128]{1,0:T(8,128)S(1)}, u32[]{:S(2)}, u32[]{:S(2)}) collective-permute-start(f32[448,128]{1,0:T(8,128)S(1)} %bitcast.4), channel_id=1, source_target_pairs={{4,8},{8,4},{12,16},{16,12},{20,24},{24,20},{28,0},{0,28},{5,9},{9... | collective-permute-start | bytes 688136 | tf_op jit(solution)/shard_map/ppermute | solution.py:445
  6.9 2.8 %shard_map.138 = (f32[14,4,128]{2,1,0:T(4,128)S(1)}, f32[14,4,128]{2,1,0:T(4,128)S(1)}, f32[16,2304]{1,0:T(8,128)S(1)}, f32[16,128]{1,0:T(8,128)S(1)}, f32[16,12...) custom-call(s32[1,1]{1,0:T(1,128)S(6)} %copy.17.count, ...), custom_call_target="tpu_custom_call" | custom-call | flops 3000000000 | bytes 2000000 | tf_op jit(solution)/shard_map/pallas_call | solution.py:48
  9.8 1.6 %collective-permute-start.2 = (f32[14,4,128]{2,1,0:T(4,128)S(1)}, f32[14,4,128]{2,1,0:T(4,128)S(1)}, u32[]{:S(2)}, u32[]{:S(2)}) collective-permute-start(f32[14,4,128]{2,1,0:T(4,128)S(1)} %get-tuple-element.58), channel_id=1, source_target_pairs={{0,1},{1,0},{2,3},{3,2},{4,5},{5,4},{6,7},{7,6},{8,9},{9,8},{10,11... | collective-permute-start | bytes 86024 | tf_op jit(solution)/shard_map/ppermute | solution.py:445
  11.4 0.7 %collective-permute-start.3 = (f32[14,4,128]{2,1,0:T(4,128)S(1)}, f32[14,4,128]{2,1,0:T(4,128)S(1)}, u32[]{:S(2)}, u32[]{:S(2)}) collective-permute-start(f32[14,4,128]{2,1,0:T(4,128)S(1)} %get-tuple-element.59), channel_id=1, source_target_pairs={{1,2},{2,1},{5,6},{6,5},{9,10},{10,9},{13,14},{14,13},{17,18},{18,... | collective-permute-start | bytes 86024 | tf_op jit(solution)/shard_map/ppermute | solution.py:445
  12.1 2.7 %shard_map.139.base = f32[14,4,32,128]{3,2,1,0:T(8,128)S(1)} custom-call(f32[14,4,32,128]{3,2,1,0:T(8,128)S(1)} %get-tuple-element.43.gas.old_gas, f32[28,16,128]{2,1,0:T(8,128)S(1)} %get-tuple-element.52.table, f32[16,2304]{1,0:T(8,128)S(1)} %get-tuple-element.53.parcels.old, bf16[512,2048]{1,0:T(8,128)(2,1)S(1)} %get-tuple-element.54.hots, ...), custom_call_target="tpu_custom_call" | custom-call | flops 1000000 | bytes 10000 | tf_op jit(solution)/shard_map/pallas_call | solution.py:48
  14.8 0.0 collective-permute-done.2.near
  14.8 0.0 collective-permute-done.3.far
  14.8 0.0 collective-permute-done.on
  14.8 0.0 collective-permute-done.1.off
  14.8 0.3 shard_map.140
  15.1 0.1 collective-permute-start.4
  15.2 0.6 %collective-permute-start.5 = (f32[464,128]{1,0:T(8,128)S(1)}, f32[464,128]{1,0:T(8,128)S(1)}, u32[]{:S(2)}, u32[]{:S(2)}) collective-permute-start(f32[464,128]{1,0:T(8,128)S(1)} %get-tuple-element.67), channel_id=1, source_target_pairs={{4,8},{8,4},{12,16},{16,12},{20,24},{24,20},{28,0},{0,28},{5,9},{9... | collective-permute-start | bytes 712712 | tf_op jit(solution)/shard_map/ppermute | solution.py:445
  15.8 2.8 %shard_map.141 = (f32[14,4,128]{2,1,0:T(4,128)S(1)}, f32[14,4,128]{2,1,0:T(4,128)S(1)}, f32[16,2304]{1,0:T(8,128)S(1)}, bf16[512,2048]{1,0:T(8,128)(2,1)S(1)}, f...) custom-call(f32[14,4,32,128]{3,2,1,0:T(8,128)S(1)} %get-tuple-element.62.gas, ...), custom_call_target="tpu_custom_call" | custom-call | flops 3000000000 | bytes 2000000 | tf_op jit(solution)/shard_map/pallas_call | solution.py:48
  18.6 4.4 %collective-permute-start.6 = (f32[14,4,128]{2,1,0:T(4,128)S(1)}, f32[14,4,128]{2,1,0:T(4,128)S(1)}, u32[]{:S(2)}, u32[]{:S(2)}) collective-permute-start(f32[14,4,128]{2,1,0:T(4,128)S(1)} %get-tuple-element.68), channel_id=1, source_target_pairs={{0,1},{1,0},{2,3},{3,2},{4,5},{5,4},{6,7},{7,6},{8,9},{9,8},{10,11... | collective-permute-start | bytes 86024 | tf_op jit(solution)/shard_map/ppermute | solution.py:445
  23.1 0.8 %collective-permute-start.7 = (f32[14,4,128]{2,1,0:T(4,128)S(1)}, f32[14,4,128]{2,1,0:T(4,128)S(1)}, u32[]{:S(2)}, u32[]{:S(2)}) collective-permute-start(f32[14,4,128]{2,1,0:T(4,128)S(1)} %get-tuple-element.69), channel_id=1, source_target_pairs={{1,2},{2,1},{5,6},{6,5},{9,10},{10,9},{13,14},{14,13},{17,18},{18,... | collective-permute-start | bytes 86024 | tf_op jit(solution)/shard_map/ppermute | solution.py:445
  23.9 2.8 %shard_map.142.base = f32[14,4,32,128]{3,2,1,0:T(8,128)S(1)} custom-call(f32[14,4,32,128]{3,2,1,0:T(8,128)S(1)} %get-tuple-element.62.gas, f32[28,16,128]{2,1,0:T(8,128)S(1)} %get-tuple-element.52.table, f32[14,4,32,128]{3,2,1,0:T(8,128)S(1)} %get-tuple-element.43.gas.old_gas, f32[16,2304]{1,0:T(8,128)S(1)} %get-tuple-element.63.parcels.old, ...), custom_call_target="tpu_custom_call" | custom-call | flops 1000000 | bytes 10000 | tf_op jit(solution)/shard_map/pallas_call | solution.py:48
  26.7 0.0 collective-permute-done.4.on
  26.7 0.0 collective-permute-done.5.off
  26.7 0.9 %shard_map.143 = (f32[16,2304]{1,0:T(8,128)S(1)}, f32[16,128]{1,0:T(8,128)S(1)}, f32[16,128]{1,0:T(8,128)S(1)}, f32[2,16,128]{2,1,0:T(8,128)S(1)}, s32[1,1]{1,0:T(1,128)}) custom-call(s32[1,1]{1,0:T(1,128)S(6)} %copy.17.count, f32[14,4,32,128]{3,2,1,0:T(8,128)S(1)} %get-tuple-element.62.gas, f32[28,16,128]{2,1,0:T(8,128)S(1)} %get-tuple-element.52.table, ...), custom_call_target="tpu_custom_call" | custom-call | flops 100000000 | bytes 2000000 | tf_op jit(solution)/shard_map/pallas_call | solution.py:48
  27.6 0.0 collective-permute-start.8
  27.6 1.8 %collective-permute-start.9 = (f32[16,128]{1,0:T(8,128)S(1)}, f32[16,128]{1,0:T(8,128)S(1)}, u32[]{:S(2)}, u32[]{:S(2)}) collective-permute-start(f32[16,128]{1,0:T(8,128)S(1)} %get-tuple-element.75), channel_id=1, source_target_pairs={{4,8},{8,4},{12,16},{16,12},{20,24},{24,20},{28,0},{0,28},{5,9},{9... | collective-permute-start | bytes 24584 | tf_op jit(solution)/shard_map/ppermute | solution.py:445
  29.4 0.0 collective-permute-done.6.near
  29.4 0.0 collective-permute-done.7.far
  29.4 1.3 %shard_map.144 = f32[14,4,32,128]{3,2,1,0:T(8,128)} custom-call(f32[28,16,128]{2,1,0:T(8,128)S(1)} %get-tuple-element.52.table, f32[14,4,32,128]{3,2,1,0:T(8,128)S(1)} %shard_map.142.base, f32[464,128]{1,0:T(8,128)S(1)} %collective-permute-done.4.on, f32[464,128]{1,0:T(8,128)S(1)} %collective-permute-done.5.off, ...), custom_call_target="tpu_custom_call" | custom-call | flops 100000000 | bytes 3000000 | tf_op jit(solution)/shard_map/pallas_call | solution.py:48
  30.7 0.0 collective-permute-done.8.on
  30.7 0.9 %collective-permute-done.9.off = f32[16,128]{1,0:T(8,128)S(1)} collective-permute-done((f32[16,128]{1,0:T(8,128)S(1)}, f32[16,128]{1,0:T(8,128)S(1)}, u32[]{:S(2)}, u32[]{:S(2)}) %collective-permute-start.9) | collective-permute-done | bytes 8224 | tf_op jit(solution)/shard_map/ppermute | solution.py:445
  31.6 1.5 %shard_map.145 = (f32[1,1,2048]{2,1,0:T(1,128)}, f32[7,1,1,2048]{3,2,1,0:T(1,128)}, s32[1,1,2048]{2,1,0:T(1,128)}, s32[1,1]{1,0:T(1,128)}) custom-call(s32[1,1]{1,0:T(1,128)} %get-tuple-element.73.count, f32[16,128]{1,0:T(8,128)S(1)} %collective-permute-done.8.on, f32[16,128]{1,0:T(8,128)S(1)} %collective-permute-done.9.off, ...), custom_call_target="tpu_custom_call" | custom-call | bytes 500000 | tf_op jit(solution)/shard_map/pallas_call | solution.py:48
Async XLA Ops:
  2.2 12.6 %collective-permute-start = (f32[448,128]{1,0:T(8,128)S(1)}, f32[448,128]{1,0:T(8,128)S(1)}, u32[]{:S(2)}, u32[]{:S(2)}) collective-permute-start(f32[448,128]{1,0:T(8,128)S(1)} %bitcast.5), channel_id=1, source_target_pairs={{0,4},{4,0},{8,12},{12,8},{16,20},{20,16},{24,28},{28,24},{1,5},{5... | collective-permute-start | bytes 688136 | tf_op jit(solution)/shard_map/ppermute | solution.py:445
  2.7 12.1 %collective-permute-start.1 = (f32[448,128]{1,0:T(8,128)S(1)}, f32[448,128]{1,0:T(8,128)S(1)}, u32[]{:S(2)}, u32[]{:S(2)}) collective-permute-start(f32[448,128]{1,0:T(8,128)S(1)} %bitcast.4), channel_id=1, source_target_pairs={{4,8},{8,4},{12,16},{16,12},{20,24},{24,20},{28,0},{0,28},{5,9},{9... | collective-permute-start | bytes 688136 | tf_op jit(solution)/shard_map/ppermute | solution.py:445
  9.8 5.0 %collective-permute-start.2 = (f32[14,4,128]{2,1,0:T(4,128)S(1)}, f32[14,4,128]{2,1,0:T(4,128)S(1)}, u32[]{:S(2)}, u32[]{:S(2)}) collective-permute-start(f32[14,4,128]{2,1,0:T(4,128)S(1)} %get-tuple-element.58), channel_id=1, source_target_pairs={{0,1},{1,0},{2,3},{3,2},{4,5},{5,4},{6,7},{7,6},{8,9},{9,8},{10,11... | collective-permute-start | bytes 86024 | tf_op jit(solution)/shard_map/ppermute | solution.py:445
  11.4 3.4 %collective-permute-start.3 = (f32[14,4,128]{2,1,0:T(4,128)S(1)}, f32[14,4,128]{2,1,0:T(4,128)S(1)}, u32[]{:S(2)}, u32[]{:S(2)}) collective-permute-start(f32[14,4,128]{2,1,0:T(4,128)S(1)} %get-tuple-element.59), channel_id=1, source_target_pairs={{1,2},{2,1},{5,6},{6,5},{9,10},{10,9},{13,14},{14,13},{17,18},{18,... | collective-permute-start | bytes 86024 | tf_op jit(solution)/shard_map/ppermute | solution.py:445
  15.1 11.6 %collective-permute-start.4 = (f32[464,128]{1,0:T(8,128)S(1)}, f32[464,128]{1,0:T(8,128)S(1)}, u32[]{:S(2)}, u32[]{:S(2)}) collective-permute-start(f32[464,128]{1,0:T(8,128)S(1)} %get-tuple-element.66), channel_id=1, source_target_pairs={{0,4},{4,0},{8,12},{12,8},{16,20},{20,16},{24,28},{28,24},{1,5},{5... | collective-permute-start | bytes 712712 | tf_op jit(solution)/shard_map/ppermute | solution.py:445
  15.2 11.5 %collective-permute-start.5 = (f32[464,128]{1,0:T(8,128)S(1)}, f32[464,128]{1,0:T(8,128)S(1)}, u32[]{:S(2)}, u32[]{:S(2)}) collective-permute-start(f32[464,128]{1,0:T(8,128)S(1)} %get-tuple-element.67), channel_id=1, source_target_pairs={{4,8},{8,4},{12,16},{16,12},{20,24},{24,20},{28,0},{0,28},{5,9},{9... | collective-permute-start | bytes 712712 | tf_op jit(solution)/shard_map/ppermute | solution.py:445
  18.6 10.8 %collective-permute-start.6 = (f32[14,4,128]{2,1,0:T(4,128)S(1)}, f32[14,4,128]{2,1,0:T(4,128)S(1)}, u32[]{:S(2)}, u32[]{:S(2)}) collective-permute-start(f32[14,4,128]{2,1,0:T(4,128)S(1)} %get-tuple-element.68), channel_id=1, source_target_pairs={{0,1},{1,0},{2,3},{3,2},{4,5},{5,4},{6,7},{7,6},{8,9},{9,8},{10,11... | collective-permute-start | bytes 86024 | tf_op jit(solution)/shard_map/ppermute | solution.py:445
  23.1 6.3 %collective-permute-start.7 = (f32[14,4,128]{2,1,0:T(4,128)S(1)}, f32[14,4,128]{2,1,0:T(4,128)S(1)}, u32[]{:S(2)}, u32[]{:S(2)}) collective-permute-start(f32[14,4,128]{2,1,0:T(4,128)S(1)} %get-tuple-element.69), channel_id=1, source_target_pairs={{1,2},{2,1},{5,6},{6,5},{9,10},{10,9},{13,14},{14,13},{17,18},{18,... | collective-permute-start | bytes 86024 | tf_op jit(solution)/shard_map/ppermute | solution.py:445
  27.6 3.1 %collective-permute-start.8 = (f32[16,128]{1,0:T(8,128)S(1)}, f32[16,128]{1,0:T(8,128)S(1)}, u32[]{:S(2)}, u32[]{:S(2)}) collective-permute-start(f32[16,128]{1,0:T(8,128)S(1)} %get-tuple-element.74), channel_id=1, source_target_pairs={{0,4},{4,0},{8,12},{12,8},{16,20},{20,16},{24,28},{28,24},{1,5},{5... | collective-permute-start | bytes 24584 | tf_op jit(solution)/shard_map/ppermute | solution.py:445
  27.6 4.0 %collective-permute-start.9 = (f32[16,128]{1,0:T(8,128)S(1)}, f32[16,128]{1,0:T(8,128)S(1)}, u32[]{:S(2)}, u32[]{:S(2)}) collective-permute-start(f32[16,128]{1,0:T(8,128)S(1)} %get-tuple-element.75), channel_id=1, source_target_pairs={{4,8},{8,4},{12,16},{16,12},{20,24},{24,20},{28,0},{0,28},{5,9},{9... | collective-permute-start | bytes 24584 | tf_op jit(solution)/shard_map/ppermute | solution.py:445

commit v3 on v2

--- a/solution.py
+++ b/solution.py
@@ -304,6 +304,8 @@
 
 def edge_terms(scale, table, out, on, off, near, far):
     nf, ca, cr, cz = out.shape
+    block = lax.axis_index("radax")
+    inner, outer = block == 0, block == lax.axis_size("radax") - 1
     flip_a, flip_r = odd("azim") == 1, odd("radax") == 1
     for f in range(nf):
         got_on, got_off = on[f * cr : (f + 1) * cr], off[f * cr : (f + 1) * cr]
@@ -311,14 +313,14 @@
         west = jnp.where(flip_a, got_on, got_off)
         out[f, 0] += (scale * spread(table, WEST, f, cr)) * west
         out[f, ca - 1] += (scale * spread(table, EAST, f, cr)) * east
-        north = jnp.where(flip_r, far[f], near[f])
-        south = jnp.where(flip_r, near[f], far[f])
+        north = jnp.where(outer, 0.0, jnp.where(flip_r, far[f], near[f]))
+        south = jnp.where(inner, 0.0, jnp.where(flip_r, near[f], far[f]))
         nu = scale * spread(table, NU, f, ca)
         out[f, :, 0, :] += nu * south
         out[f, :, cr - 1, :] += nu * north
 
 
-def edge_kernel(table, base, on, off, near, far, pack_on, pack_off, out, send_on, send_off):
+def edge_kernel(table, base, off, on, far, near, pack_on, pack_off, out, send_on, send_off):
     nf, ca, cr, cz = out.shape
     out[...] = base[...]
     edge_terms(DT, table, out, on, off, near, far)
@@ -400,7 +402,7 @@
     parcels[LIVE : LIVE + 1, :slots] = jnp.where(gone, 0.0, parcels[LIVE : LIVE + 1, :slots])
 
 
-def finish_kernel(table, base, on, off, near, far, sources, out):
+def finish_kernel(table, base, off, on, near, far, sources, out):
     nf, ca, cr, cz = out.shape
     out[...] = base[...]
     edge_terms(0.5 * DT, table, out, on, off, near, far)
@@ -416,7 +418,7 @@
             out[f, layer] += (0.5 * DT) * total[f * cr : (f + 1) * cr]
 
 
-def place_kernel(far_offset, count, on, off, old, mass, state, host, used, parcels):
+def place_kernel(far_offset, count, off, on, old, mass, state, host, used, parcels):
     slots = mass.shape[-1]
     parcels[...] = old[...]
     packs = sides(on[...], off[...])
@@ -436,13 +438,24 @@
     host[0] = jnp.where(live, parcels[HOST : HOST + 1, :slots].astype(jnp.int32), -1)
 
 
-def swap(array, axis, phase, wrap):
+def swap(array, axis, phase):
     size = lax.axis_size(axis)
     pairs = []
-    for i in range(phase, size if wrap else size - 1, 2):
+    for i in range(phase, size + phase, 2):
         j = (i + 1) % size
         pairs += [(i, j), (j, i)]
     return lax.ppermute(array, axis, pairs)
+
+
+def swap_rows(array, phase):
+    sectors, blocks = lax.axis_size("azim"), lax.axis_size("radax")
+    pairs = []
+    for i in range(sectors):
+        for j in range(blocks):
+            other = j + 1 if (j - phase) % 2 == 0 else j - 1
+            target = (i, other) if 0 <= other < blocks else (i ^ 1, j)
+            pairs.append((i * blocks + j, target[0] * blocks + target[1]))
+    return lax.ppermute(array, ("azim", "radax"), pairs)
 
 
 def on_device(
@@ -466,8 +479,8 @@
         moved=2_000_000,
     )
     gas, transport, chemistry, evap, source_map, mass, state, host, crossing = small
-    off = swap(off.reshape(nf * cr, cz), "azim", 1, True)
-    on = swap(on.reshape(nf * cr, cz), "azim", 0, True)
+    off = swap(off.reshape(nf * cr, cz), "azim", 1)
+    on = swap(on.reshape(nf * cr, cz), "azim", 0)
 
     hots, lhot = shape((ca * cz, slots), BF16), shape((2 * width, slots), BF16)
     source = shape((ROWS, slots))
@@ -483,8 +496,8 @@
         scratch=probe_scratch + [pltpu.VMEM(lhot.shape, BF16)],
         **heavy,
     )
-    near = swap(near, "radax", 0, False)
-    far = swap(far, "radax", 1, False)
+    near = swap_rows(near, 0)
+    far = swap_rows(far, 1)
     base = call(
         functools.partial(field_one_kernel, 4 * width),
         grid,
@@ -501,12 +514,12 @@
         [grid, longer, longer],
         [VMEM] * 8,
         [VMEM] * 3,
-        (table, base, on, off, near, far, pack_on, pack_off),
+        (table, base, off, on, far, near, pack_on, pack_off),
         aliases={1: 0},
         moved=3_000_000,
     )
-    off = swap(off, "azim", 1, True)
-    on = swap(on, "azim", 0, True)
+    off = swap(off, "azim", 1)
+    on = swap(on, "azim", 0)
     near, far, parcels, cell_hots, sources, taken, named = call(
         probe_two_kernel,
         [ring, ring, slotted, hots, source, shape((ROWS, 2 * width)), lhot],
@@ -516,8 +529,8 @@
         scratch=probe_scratch,
         **heavy,
     )
-    near = swap(near, "radax", 0, False)
-    far = swap(far, "radax", 1, False)
+    near = swap_rows(near, 0)
+    far = swap_rows(far, 1)
     base = call(
         functools.partial(field_two_kernel, 4 * width),
         grid,
@@ -538,14 +551,14 @@
         flops=100_000_000,
         moved=2_000_000,
     )
-    pack_off = swap(pack_off, "azim", 1, True)
-    pack_on = swap(pack_on, "azim", 0, True)
+    pack_off = swap(pack_off, "azim", 1)
+    pack_on = swap(pack_on, "azim", 0)
     gas_next = call(
         finish_kernel,
         shape(gas.shape),
         [VMEM] * 7,
         VMEM,
-        (table, base, on, off, near, far, sources),
+        (table, base, off, on, near, far, sources),
         flops=100_000_000,
         moved=3_000_000,
     )
@@ -554,7 +567,7 @@
         [shape(mass.shape), shape(state.shape), shape(host.shape, jnp.int32), one],
         [VMEM] * 4,
         [VMEM] * 4,
-        (count, pack_on, pack_off, parcels),
+        (count, pack_off, pack_on, parcels),
         scratch=[pltpu.VMEM((ROWS, padded), F32)],
         moved=500_000,
     )

time: 33.3 us -> 30.3 us (0.910)
  starting transfers between devices: 14.1 us -> 10.7 us
  waiting for transfers between devices: 0.9 us -> 1.44 us
    ppermute x10 -> x6, starting transfers between devices: 14.1 us -> 6.34 us  [swap(): return lax.ppermute(array, axis, pairs)]
    ppermute x0 -> x4, starting transfers between devices: none -> 4.4 us  [swap_rows(): return lax.ppermute(array, ('azim', 'radax'), pairs)]
    ppermute x10 -> x6, waiting for transfers between devices: 0.9 us -> 1.43 us  [swap(): return lax.ppermute(array, axis, pairs)]
  transfers between devices with their start and end apart: 10 -> 10, of which waited for: 1 -> 2; matrix products, arithmetic and copies ran while one was open for 0% -> 0% of each run, Pallas kernels for 40% -> 44%
where the time goes in v3:
time: 30.3 us; the launch traced here: 30.2 us
  Pallas kernels  16.6 us (55%)
  starting transfers between devices  10.7 us (35%)
  waiting for transfers between devices  1.44 us (5%)
  between operations  1.36 us (4%)
    pallas_call x9, Pallas kernels, call(): pl.pallas_call(kernel, out_shape=outs, in_specs=ins, out_specs=out_specs,...  16.6 us
    ppermute x6, starting transfers between devices, swap(): return lax.ppermute(array, axis, pairs)  6.34 us
    ppermute x4, starting transfers between devices, swap_rows(): return lax.ppermute(array, ('azim', 'radax'), pairs)  4.4 us
    ppermute x6, waiting for transfers between devices, swap(): return lax.ppermute(array, axis, pairs)  1.43 us
  transfers between devices with their start and end apart: 10, of which 2 were waited for; matrix products, arithmetic and copies ran while one was open for 0% of the time, Pallas kernels for 44%

profile of v3, /device:TPU:0, one launch (start us, length us, event | category | flops | bytes accessed | tf_op | source)
XLA Modules:
  0.0 30.2 jit_solution(1789641489848817030)
XLA Ops:
  0.6 1.5 %shard_map.137 = (f32[14,32,128]{2,1,0:T(8,128)S(1)}, f32[14,32,128]{2,1,0:T(8,128)S(1)}, f32[14,4,32,128]{3,2,1,0:T(8,128)S(1)}, f32[3,14]{1,0:T(4,128)S(1)}, f...) custom-call(f32[14,4,32,128]{3,2,1,0:T(8,128)} %refs_0_.1, ...), custom_call_target="tpu_custom_call" | custom-call | bytes 2000000 | tf_op jit(solution)/shard_map/pallas_call | solution.py:48
  2.2 3.4 %collective-permute-start = (f32[448,128]{1,0:T(8,128)S(1)}, f32[448,128]{1,0:T(8,128)S(1)}, u32[]{:S(2)}, u32[]{:S(2)}) collective-permute-start(f32[448,128]{1,0:T(8,128)S(1)} %bitcast.5), channel_id=1, source_target_pairs={{4,8},{8,4},{12,16},{16,12},{20,24},{24,20},{28,0},{0,28},{5,9},{9... | collective-permute-start | bytes 688136 | tf_op jit(solution)/shard_map/ppermute | solution.py:447
  5.6 0.0 collective-permute-start.1
  6.2 2.8 %shard_map.138 = (f32[14,4,128]{2,1,0:T(4,128)S(1)}, f32[14,4,128]{2,1,0:T(4,128)S(1)}, f32[16,2304]{1,0:T(8,128)S(1)}, f32[16,128]{1,0:T(8,128)S(1)}, f32[16,12...) custom-call(s32[1,1]{1,0:T(1,128)S(6)} %copy.17.count, ...), custom_call_target="tpu_custom_call" | custom-call | flops 3000000000 | bytes 2000000 | tf_op jit(solution)/shard_map/pallas_call | solution.py:48
  9.1 0.6 %collective-permute-start.2 = (f32[14,4,128]{2,1,0:T(4,128)S(1)}, f32[14,4,128]{2,1,0:T(4,128)S(1)}, u32[]{:S(2)}, u32[]{:S(2)}) collective-permute-start(f32[14,4,128]{2,1,0:T(4,128)S(1)} %get-tuple-element.58), channel_id=1, source_target_pairs={{0,4},{1,2},{2,1},{3,7},{4,0},{5,6},{6,5},{7,3},{8,12},{9,10},{10,... | collective-permute-start | bytes 86024 | tf_op jit(solution)/shard_map/ppermute | solution.py:458
  9.7 2.6 %collective-permute-start.3 = (f32[14,4,128]{2,1,0:T(4,128)S(1)}, f32[14,4,128]{2,1,0:T(4,128)S(1)}, u32[]{:S(2)}, u32[]{:S(2)}) collective-permute-start(f32[14,4,128]{2,1,0:T(4,128)S(1)} %get-tuple-element.59), channel_id=1, source_target_pairs={{0,1},{1,0},{2,3},{3,2},{4,5},{5,4},{6,7},{7,6},{8,9},{9,8},{10,11... | collective-permute-start | bytes 86024 | tf_op jit(solution)/shard_map/ppermute | solution.py:458
  12.3 2.7 %shard_map.139.base = f32[14,4,32,128]{3,2,1,0:T(8,128)S(1)} custom-call(f32[14,4,32,128]{3,2,1,0:T(8,128)S(1)} %get-tuple-element.43.gas.old_gas, f32[28,16,128]{2,1,0:T(8,128)S(1)} %get-tuple-element.52.table, f32[16,2304]{1,0:T(8,128)S(1)} %get-tuple-element.53.parcels.old, bf16[512,2048]{1,0:T(8,128)(2,1)S(1)} %get-tuple-element.54.hots, ...), custom_call_target="tpu_custom_call" | custom-call | flops 1000000 | bytes 10000 | tf_op jit(solution)/shard_map/pallas_call | solution.py:48
  15.0 0.0 collective-permute-done.2.far
  15.0 0.0 collective-permute-done.3.near
  15.0 0.0 collective-permute-done.off
  15.0 0.0 collective-permute-done.1.on
  15.0 0.3 shard_map.140
  15.3 0.3 collective-permute-start.4
  15.6 1.1 %collective-permute-start.5 = (f32[464,128]{1,0:T(8,128)S(1)}, f32[464,128]{1,0:T(8,128)S(1)}, u32[]{:S(2)}, u32[]{:S(2)}) collective-permute-start(f32[464,128]{1,0:T(8,128)S(1)} %get-tuple-element.67), channel_id=1, source_target_pairs={{0,4},{4,0},{8,12},{12,8},{16,20},{20,16},{24,28},{28,24},{1,5},{5... | collective-permute-start | bytes 712712 | tf_op jit(solution)/shard_map/ppermute | solution.py:447
  16.7 2.8 %shard_map.141 = (f32[14,4,128]{2,1,0:T(4,128)S(1)}, f32[14,4,128]{2,1,0:T(4,128)S(1)}, f32[16,2304]{1,0:T(8,128)S(1)}, bf16[512,2048]{1,0:T(8,128)(2,1)S(1)}, f...) custom-call(f32[14,4,32,128]{3,2,1,0:T(8,128)S(1)} %get-tuple-element.62.gas, ...), custom_call_target="tpu_custom_call" | custom-call | flops 3000000000 | bytes 2000000 | tf_op jit(solution)/shard_map/pallas_call | solution.py:48
  19.5 1.2 %collective-permute-start.6 = (f32[14,4,128]{2,1,0:T(4,128)S(1)}, f32[14,4,128]{2,1,0:T(4,128)S(1)}, u32[]{:S(2)}, u32[]{:S(2)}) collective-permute-start(f32[14,4,128]{2,1,0:T(4,128)S(1)} %get-tuple-element.68), channel_id=1, source_target_pairs={{0,1},{1,0},{2,3},{3,2},{4,5},{5,4},{6,7},{7,6},{8,9},{9,8},{10,11... | collective-permute-start | bytes 86024 | tf_op jit(solution)/shard_map/ppermute | solution.py:458
  20.7 0.0 collective-permute-start.7
  20.7 2.8 %shard_map.142.base = f32[14,4,32,128]{3,2,1,0:T(8,128)S(1)} custom-call(f32[14,4,32,128]{3,2,1,0:T(8,128)S(1)} %get-tuple-element.62.gas, f32[28,16,128]{2,1,0:T(8,128)S(1)} %get-tuple-element.52.table, f32[14,4,32,128]{3,2,1,0:T(8,128)S(1)} %get-tuple-element.43.gas.old_gas, f32[16,2304]{1,0:T(8,128)S(1)} %get-tuple-element.63.parcels.old, ...), custom_call_target="tpu_custom_call" | custom-call | flops 1000000 | bytes 10000 | tf_op jit(solution)/shard_map/pallas_call | solution.py:48
  23.5 0.3 %collective-permute-done.4.off = f32[464,128]{1,0:T(8,128)S(1)} collective-permute-done((f32[464,128]{1,0:T(8,128)S(1)}, f32[464,128]{1,0:T(8,128)S(1)}, u32[]{:S(2)}, u32[]{:S(2)}) %collective-permute-start.4) | collective-permute-done | bytes 237600 | tf_op jit(solution)/shard_map/ppermute | solution.py:447
  23.8 0.0 collective-permute-done.5.on
  23.8 0.9 %shard_map.143 = (f32[16,2304]{1,0:T(8,128)S(1)}, f32[16,128]{1,0:T(8,128)S(1)}, f32[16,128]{1,0:T(8,128)S(1)}, f32[2,16,128]{2,1,0:T(8,128)S(1)}, s32[1,1]{1,0:T(1,128)}) custom-call(s32[1,1]{1,0:T(1,128)S(6)} %copy.17.count, f32[14,4,32,128]{3,2,1,0:T(8,128)S(1)} %get-tuple-element.62.gas, f32[28,16,128]{2,1,0:T(8,128)S(1)} %get-tuple-element.52.table, ...), custom_call_target="tpu_custom_call" | custom-call | flops 100000000 | bytes 2000000 | tf_op jit(solution)/shard_map/pallas_call | solution.py:48
  24.7 1.5 %collective-permute-start.8 = (f32[16,128]{1,0:T(8,128)S(1)}, f32[16,128]{1,0:T(8,128)S(1)}, u32[]{:S(2)}, u32[]{:S(2)}) collective-permute-start(f32[16,128]{1,0:T(8,128)S(1)} %get-tuple-element.74), channel_id=1, source_target_pairs={{4,8},{8,4},{12,16},{16,12},{20,24},{24,20},{28,0},{0,28},{5,9},{9... | collective-permute-start | bytes 24584 | tf_op jit(solution)/shard_map/ppermute | solution.py:447
  26.2 0.0 collective-permute-start.9
  26.2 0.0 collective-permute-done.6.near
  26.2 0.0 collective-permute-done.7.far
  26.2 1.3 %shard_map.144 = f32[14,4,32,128]{3,2,1,0:T(8,128)} custom-call(f32[28,16,128]{2,1,0:T(8,128)S(1)} %get-tuple-element.52.table, f32[14,4,32,128]{3,2,1,0:T(8,128)S(1)} %shard_map.142.base, f32[464,128]{1,0:T(8,128)S(1)} %collective-permute-done.4.off, f32[464,128]{1,0:T(8,128)S(1)} %collective-permute-done.5.on, ...), custom_call_target="tpu_custom_call" | custom-call | flops 100000000 | bytes 3000000 | tf_op jit(solution)/shard_map/pallas_call | solution.py:48
  27.6 1.1 %collective-permute-done.8.off = f32[16,128]{1,0:T(8,128)S(1)} collective-permute-done((f32[16,128]{1,0:T(8,128)S(1)}, f32[16,128]{1,0:T(8,128)S(1)}, u32[]{:S(2)}, u32[]{:S(2)}) %collective-permute-start.8) | collective-permute-done | bytes 8224 | tf_op jit(solution)/shard_map/ppermute | solution.py:447
  28.7 0.0 collective-permute-done.9.on
  28.7 1.5 %shard_map.145 = (f32[1,1,2048]{2,1,0:T(1,128)}, f32[7,1,1,2048]{3,2,1,0:T(1,128)}, s32[1,1,2048]{2,1,0:T(1,128)}, s32[1,1]{1,0:T(1,128)}) custom-call(s32[1,1]{1,0:T(1,128)} %get-tuple-element.73.count, f32[16,128]{1,0:T(8,128)S(1)} %collective-permute-done.8.off, f32[16,128]{1,0:T(8,128)S(1)} %collective-permute-done.9.on, ...), custom_call_target="tpu_custom_call" | custom-call | bytes 500000 | tf_op jit(solution)/shard_map/pallas_call | solution.py:48
Async XLA Ops:
  2.2 12.8 %collective-permute-start = (f32[448,128]{1,0:T(8,128)S(1)}, f32[448,128]{1,0:T(8,128)S(1)}, u32[]{:S(2)}, u32[]{:S(2)}) collective-permute-start(f32[448,128]{1,0:T(8,128)S(1)} %bitcast.5), channel_id=1, source_target_pairs={{4,8},{8,4},{12,16},{16,12},{20,24},{24,20},{28,0},{0,28},{5,9},{9... | collective-permute-start | bytes 688136 | tf_op jit(solution)/shard_map/ppermute | solution.py:447
  5.6 9.4 %collective-permute-start.1 = (f32[448,128]{1,0:T(8,128)S(1)}, f32[448,128]{1,0:T(8,128)S(1)}, u32[]{:S(2)}, u32[]{:S(2)}) collective-permute-start(f32[448,128]{1,0:T(8,128)S(1)} %bitcast.4), channel_id=1, source_target_pairs={{0,4},{4,0},{8,12},{12,8},{16,20},{20,16},{24,28},{28,24},{1,5},{5... | collective-permute-start | bytes 688136 | tf_op jit(solution)/shard_map/ppermute | solution.py:447
  9.1 5.9 %collective-permute-start.2 = (f32[14,4,128]{2,1,0:T(4,128)S(1)}, f32[14,4,128]{2,1,0:T(4,128)S(1)}, u32[]{:S(2)}, u32[]{:S(2)}) collective-permute-start(f32[14,4,128]{2,1,0:T(4,128)S(1)} %get-tuple-element.58), channel_id=1, source_target_pairs={{0,4},{1,2},{2,1},{3,7},{4,0},{5,6},{6,5},{7,3},{8,12},{9,10},{10,... | collective-permute-start | bytes 86024 | tf_op jit(solution)/shard_map/ppermute | solution.py:458
  9.7 5.4 %collective-permute-start.3 = (f32[14,4,128]{2,1,0:T(4,128)S(1)}, f32[14,4,128]{2,1,0:T(4,128)S(1)}, u32[]{:S(2)}, u32[]{:S(2)}) collective-permute-start(f32[14,4,128]{2,1,0:T(4,128)S(1)} %get-tuple-element.59), channel_id=1, source_target_pairs={{0,1},{1,0},{2,3},{3,2},{4,5},{5,4},{6,7},{7,6},{8,9},{9,8},{10,11... | collective-permute-start | bytes 86024 | tf_op jit(solution)/shard_map/ppermute | solution.py:458
  15.3 8.4 %collective-permute-start.4 = (f32[464,128]{1,0:T(8,128)S(1)}, f32[464,128]{1,0:T(8,128)S(1)}, u32[]{:S(2)}, u32[]{:S(2)}) collective-permute-start(f32[464,128]{1,0:T(8,128)S(1)} %get-tuple-element.66), channel_id=1, source_target_pairs={{4,8},{8,4},{12,16},{16,12},{20,24},{24,20},{28,0},{0,28},{5,9},{9... | collective-permute-start | bytes 712712 | tf_op jit(solution)/shard_map/ppermute | solution.py:447
  15.6 8.2 %collective-permute-start.5 = (f32[464,128]{1,0:T(8,128)S(1)}, f32[464,128]{1,0:T(8,128)S(1)}, u32[]{:S(2)}, u32[]{:S(2)}) collective-permute-start(f32[464,128]{1,0:T(8,128)S(1)} %get-tuple-element.67), channel_id=1, source_target_pairs={{0,4},{4,0},{8,12},{12,8},{16,20},{20,16},{24,28},{28,24},{1,5},{5... | collective-permute-start | bytes 712712 | tf_op jit(solution)/shard_map/ppermute | solution.py:447
  19.5 6.7 %collective-permute-start.6 = (f32[14,4,128]{2,1,0:T(4,128)S(1)}, f32[14,4,128]{2,1,0:T(4,128)S(1)}, u32[]{:S(2)}, u32[]{:S(2)}) collective-permute-start(f32[14,4,128]{2,1,0:T(4,128)S(1)} %get-tuple-element.68), channel_id=1, source_target_pairs={{0,1},{1,0},{2,3},{3,2},{4,5},{5,4},{6,7},{7,6},{8,9},{9,8},{10,11... | collective-permute-start | bytes 86024 | tf_op jit(solution)/shard_map/ppermute | solution.py:458
  20.7 5.5 %collective-permute-start.7 = (f32[14,4,128]{2,1,0:T(4,128)S(1)}, f32[14,4,128]{2,1,0:T(4,128)S(1)}, u32[]{:S(2)}, u32[]{:S(2)}) collective-permute-start(f32[14,4,128]{2,1,0:T(4,128)S(1)} %get-tuple-element.69), channel_id=1, source_target_pairs={{0,4},{1,2},{2,1},{3,7},{4,0},{5,6},{6,5},{7,3},{8,12},{9,10},{10,... | collective-permute-start | bytes 86024 | tf_op jit(solution)/shard_map/ppermute | solution.py:458
  24.7 4.0 %collective-permute-start.8 = (f32[16,128]{1,0:T(8,128)S(1)}, f32[16,128]{1,0:T(8,128)S(1)}, u32[]{:S(2)}, u32[]{:S(2)}) collective-permute-start(f32[16,128]{1,0:T(8,128)S(1)} %get-tuple-element.74), channel_id=1, source_target_pairs={{4,8},{8,4},{12,16},{16,12},{20,24},{24,20},{28,0},{0,28},{5,9},{9... | collective-permute-start | bytes 24584 | tf_op jit(solution)/shard_map/ppermute | solution.py:447
  26.2 2.4 %collective-permute-start.9 = (f32[16,128]{1,0:T(8,128)S(1)}, f32[16,128]{1,0:T(8,128)S(1)}, u32[]{:S(2)}, u32[]{:S(2)}) collective-permute-start(f32[16,128]{1,0:T(8,128)S(1)} %get-tuple-element.75), channel_id=1, source_target_pairs={{0,4},{4,0},{8,12},{12,8},{16,20},{20,16},{24,28},{28,24},{1,5},{5... | collective-permute-start | bytes 24584 | tf_op jit(solution)/shard_map/ppermute | solution.py:447

commit v4 on v3

--- a/solution.py
+++ b/solution.py
@@ -239,13 +239,14 @@
 
 def probe_one_kernel(
     count, gas, transport, chemistry, evap, source_map, lists, mass, state, host_in,
-    near, far, parcels, on, off, table, hots, source, cells, probed, lhot,
+    near, far, parcels, on, off, table, hots, source, used, cells, probed, lhot,
 ):
     nf, ca, cr, cz = gas.shape
     slots = probed.shape[1]
     send_rows(gas, near, far)
     fill_table(table, transport, chemistry, evap, source_map)
     host = host_in[0]
+    used[...] = jnp.broadcast_to(count[...].astype(F32), used.shape)
     live = (iota((1, slots), 1) < count[...]).astype(F32)
     attr = jnp.concatenate([mass[0]] + [state[k, 0] for k in range(state.shape[0])], axis=0)
     source[:nf] = parcel_work(gas, host, attr, live, table, parcels, cells, hots, probed)
@@ -355,7 +356,7 @@
 
 
 def scalar(ref):
-    return jnp.sum(ref[...].astype(F32)).astype(jnp.int32)
+    return jnp.max(ref[0:1]).astype(jnp.int32)
 
 
 def arrive_kernel(
@@ -389,7 +390,7 @@
         moved = jnp.concatenate(rows + [home, live, jnp.zeros((ROWS - LIVE - 1, cell.shape[1]), F32)], 0)
         put(parcels, moved, start, live)
         start = start + jnp.sum(live).astype(jnp.int32)
-    used[...] = jnp.broadcast_to(start, (1, 1))
+    used[...] = jnp.broadcast_to(start.astype(F32), used.shape)
     width = lists.shape[-1]
     first = pl.multiple_of(scalar(count), width)
     window = pl.ds(first, 2 * width)
@@ -466,9 +467,9 @@
     width = crossing.shape[-1]
     padded = slots + 2 * width
     ring, pack = shape((nf, ca, cz)), shape((ROWS, width))
-    one = shape((1, 1), jnp.int32)
+    tile = shape((8, LANES))
     grid, slotted = shape(gas.shape), shape((ROWS, padded))
-    small = (gas, transport, chemistry, evap.reshape(1, nf), source_map.T, mass, state, host, crossing)
+    small = (transport, chemistry, evap.reshape(1, nf), source_map.T, mass, state, host, crossing)
     on, off, *small = call(
         pack_kernel,
         [shape((nf, cr, cz)), shape((nf, cr, cz))] + [shape(v.shape, v.dtype) for v in small],
@@ -476,9 +477,10 @@
         [VMEM] * (2 + len(small)),
         tuple(pltpu.with_memory_space_constraint(v, pltpu.HBM) for v in (gas,) + small),
         scratch=[pltpu.SemaphoreType.DMA((2 + len(small),))],
+        flops=5_000_000_000,
         moved=2_000_000,
     )
-    gas, transport, chemistry, evap, source_map, mass, state, host, crossing = small
+    transport, chemistry, evap, source_map, mass, state, host, crossing = small
     off = swap(off.reshape(nf * cr, cz), "azim", 1)
     on = swap(on.reshape(nf * cr, cz), "azim", 0)
 
@@ -487,11 +489,11 @@
     probe_scratch = [pltpu.VMEM((nf * cr, 2 * ca * cz), BF16), pltpu.VMEM((ROWS, slots), F32)]
     field_scratch = [pltpu.VMEM((nf * cr, ca * cz), F32), pltpu.VMEM(gas.shape, F32)]
     heavy = dict(flops=3_000_000_000, moved=2_000_000, trans=300_000)
-    near, far, parcels, pack_on, pack_off, table, cell_hots, sources = call(
+    near, far, parcels, pack_on, pack_off, table, cell_hots, sources, used = call(
         probe_one_kernel,
-        [ring, ring, slotted, pack, pack, shape((SOURCE + source_map.shape[0] + nf, ROWS, LANES)), hots, source],
+        [ring, ring, slotted, pack, pack, shape((SOURCE + source_map.shape[0] + nf, ROWS, LANES)), hots, source, tile],
         [VMEM] * 10,
-        [VMEM] * 8,
+        [VMEM] * 9,
         (count, gas, transport, chemistry, evap, source_map, crossing, mass, state, host),
         scratch=probe_scratch + [pltpu.VMEM(lhot.shape, BF16)],
         **heavy,
@@ -541,12 +543,12 @@
         flops=1_000_000,
         moved=10_000,
     )
-    parcels, pack_on, pack_off, sources, count = call(
+    parcels, pack_on, pack_off, sources, used_now = call(
         arrive_kernel,
-        [slotted, pack, pack, shape((2, ROWS, width)), one],
+        [slotted, pack, pack, shape((2, ROWS, width)), tile],
         [VMEM] * 9,
         [VMEM] * 5,
-        (count, section_one, table, crossing, on, off, parcels, taken, named),
+        (used, section_one, table, crossing, on, off, parcels, taken, named),
         scratch=[pltpu.VMEM((nf * cr, 2 * cz), BF16)],
         flops=100_000_000,
         moved=2_000_000,
@@ -564,10 +566,10 @@
     )
     mass_next, state_next, host_next, count_next = call(
         functools.partial(place_kernel, (ca - 1) * cr * cz),
-        [shape(mass.shape), shape(state.shape), shape(host.shape, jnp.int32), one],
+        [shape(mass.shape), shape(state.shape), shape(host.shape, jnp.int32), shape((1, 1), jnp.int32)],
         [VMEM] * 4,
         [VMEM] * 4,
-        (count, pack_off, pack_on, parcels),
+        (used_now, pack_off, pack_on, parcels),
         scratch=[pltpu.VMEM((ROWS, padded), F32)],
         moved=500_000,
     )

time: 30.3 us -> 29.2 us (0.964)
  Pallas kernels: 16.6 us -> 15.4 us
    pallas_call x9, Pallas kernels: 16.6 us -> 15.4 us  [call(): pl.pallas_call(kernel, out_shape=outs, in_specs=ins, out_specs=out_specs,...]
  transfers between devices with their start and end apart: 10 -> 10, of which waited for: 2 -> 2; matrix products, arithmetic and copies ran while one was open for 0% -> 0% of each run, Pallas kernels for 44% -> 45%
where the time goes in v4:
time: 29.2 us; the launch traced here: 29 us
  Pallas kernels  15.4 us (53%)
  starting transfers between devices  10.8 us (37%)
  waiting for transfers between devices  1.45 us (5%)
  between operations  1.39 us (5%)
    pallas_call x9, Pallas kernels, call(): pl.pallas_call(kernel, out_shape=outs, in_specs=ins, out_specs=out_specs,...  15.4 us
    ppermute x6, starting transfers between devices, swap(): return lax.ppermute(array, axis, pairs)  6.39 us
    ppermute x4, starting transfers between devices, swap_rows(): return lax.ppermute(array, ('azim', 'radax'), pairs)  4.4 us
    ppermute x6, waiting for transfers between devices, swap(): return lax.ppermute(array, axis, pairs)  1.44 us
  transfers between devices with their start and end apart: 10, of which 2 were waited for; matrix products, arithmetic and copies ran while one was open for 0% of the time, Pallas kernels for 45%

profile of v4, /device:TPU:0, one launch (start us, length us, event | category | flops | bytes accessed | tf_op | source)
XLA Modules:
  0.0 29.0 jit_solution(15583435669670287060)
XLA Ops:
  0.6 0.0 copy-start
  0.6 1.3 %shard_map.137 = (f32[14,32,128]{2,1,0:T(8,128)S(1)}, f32[14,32,128]{2,1,0:T(8,128)S(1)}, f32[3,14]{1,0:T(4,128)S(1)}, f32[14,14]{1,0:T(8,128)S(1)}, f32[1,14]{1...) custom-call(f32[14,4,32,128]{3,2,1,0:T(8,128)} %old_gas.1, ...), custom_call_target="tpu_custom_call" | custom-call | flops 5000000000 | bytes 2000000 | tf_op jit(solution)/shard_map/pallas_call | solution.py:48
  2.0 3.4 %collective-permute-start = (f32[448,128]{1,0:T(8,128)S(1)}, f32[448,128]{1,0:T(8,128)S(1)}, u32[]{:S(2)}, u32[]{:S(2)}) collective-permute-start(f32[448,128]{1,0:T(8,128)S(1)} %bitcast.5), channel_id=1, source_target_pairs={{4,8},{8,4},{12,16},{16,12},{20,24},{24,20},{28,0},{0,28},{5,9},{9... | collective-permute-start | bytes 688136 | tf_op jit(solution)/shard_map/ppermute | solution.py:448
  5.4 0.0 collective-permute-start.1
  6.0 0.0 copy-done
  6.0 2.8 %shard_map.138 = (f32[14,4,128]{2,1,0:T(4,128)S(1)}, f32[14,4,128]{2,1,0:T(4,128)S(1)}, f32[16,2304]{1,0:T(8,128)S(1)}, f32[16,128]{1,0:T(8,128)S(1)}, f32[16,12...) custom-call(s32[1,1]{1,0:T(1,128)S(6)} %copy.17.count, ...), custom_call_target="tpu_custom_call" | custom-call | flops 3000000000 | bytes 2000000 | tf_op jit(solution)/shard_map/pallas_call | solution.py:48
  8.8 0.6 %collective-permute-start.2 = (f32[14,4,128]{2,1,0:T(4,128)S(1)}, f32[14,4,128]{2,1,0:T(4,128)S(1)}, u32[]{:S(2)}, u32[]{:S(2)}) collective-permute-start(f32[14,4,128]{2,1,0:T(4,128)S(1)} %get-tuple-element.57), channel_id=1, source_target_pairs={{0,4},{1,2},{2,1},{3,7},{4,0},{5,6},{6,5},{7,3},{8,12},{9,10},{10,... | collective-permute-start | bytes 86024 | tf_op jit(solution)/shard_map/ppermute | solution.py:459
  9.4 2.6 %collective-permute-start.3 = (f32[14,4,128]{2,1,0:T(4,128)S(1)}, f32[14,4,128]{2,1,0:T(4,128)S(1)}, u32[]{:S(2)}, u32[]{:S(2)}) collective-permute-start(f32[14,4,128]{2,1,0:T(4,128)S(1)} %get-tuple-element.58), channel_id=1, source_target_pairs={{0,1},{1,0},{2,3},{3,2},{4,5},{5,4},{6,7},{7,6},{8,9},{9,8},{10,11... | collective-permute-start | bytes 86024 | tf_op jit(solution)/shard_map/ppermute | solution.py:459
  12.1 2.7 %shard_map.139.base = f32[14,4,32,128]{3,2,1,0:T(8,128)S(1)} custom-call(f32[14,4,32,128]{3,2,1,0:T(8,128)S(1)} %copy-done, f32[28,16,128]{2,1,0:T(8,128)S(1)} %get-tuple-element.51.table, f32[16,2304]{1,0:T(8,128)S(1)} %get-tuple-element.52.parcels.old, bf16[512,2048]{1,0:T(8,128)(2,1)S(1)} %get-tuple-element.53.hots, f32[16,2048]{1,0:T(8,128)S(1)} %get-tuple-element.54.source), custom_call_target="tpu_custom_call" | custom-call | flops 1000000 | bytes 10000 | tf_op jit(solution)/shard_map/pallas_call | solution.py:48
  14.8 0.0 collective-permute-done.2.far
  14.8 0.0 collective-permute-done.3.near
  14.8 0.0 collective-permute-done.off
  14.8 0.0 collective-permute-done.1.on
  14.8 0.3 %shard_map.140 = (f32[14,4,32,128]{3,2,1,0:T(8,128)S(1)}, f32[464,128]{1,0:T(8,128)S(1)}, f32[464,128]{1,0:T(8,128)S(1)}) custom-call(f32[28,16,128]{2,1,0:T(8,128)S(1)} %get-tuple-element.51.table, f32[14,4,32,128]{3,2,1,0:T(8,128)S(1)} %shard_map.139.base, f32[448,128]{1,0:T(8,128)S(1)} %collective-permute-done.off, ...), custom_call_target="tpu_custom_call", output_to_operand_aliasing={{0}: (1, {})} | custom-call | bytes 3000000 | tf_op jit(solution)/shard_map/pallas_call | solution.py:48
  15.1 0.3 collective-permute-start.4
  15.4 1.1 %collective-permute-start.5 = (f32[464,128]{1,0:T(8,128)S(1)}, f32[464,128]{1,0:T(8,128)S(1)}, u32[]{:S(2)}, u32[]{:S(2)}) collective-permute-start(f32[464,128]{1,0:T(8,128)S(1)} %get-tuple-element.66), channel_id=1, source_target_pairs={{0,4},{4,0},{8,12},{12,8},{16,20},{20,16},{24,28},{28,24},{1,5},{5... | collective-permute-start | bytes 712712 | tf_op jit(solution)/shard_map/ppermute | solution.py:448
  16.5 2.8 %shard_map.141 = (f32[14,4,128]{2,1,0:T(4,128)S(1)}, f32[14,4,128]{2,1,0:T(4,128)S(1)}, f32[16,2304]{1,0:T(8,128)S(1)}, bf16[512,2048]{1,0:T(8,128)(2,1)S(1)}, f...) custom-call(f32[14,4,32,128]{3,2,1,0:T(8,128)S(1)} %get-tuple-element.61.gas, ...), custom_call_target="tpu_custom_call" | custom-call | flops 3000000000 | bytes 2000000 | tf_op jit(solution)/shard_map/pallas_call | solution.py:48
  19.3 1.2 %collective-permute-start.6 = (f32[14,4,128]{2,1,0:T(4,128)S(1)}, f32[14,4,128]{2,1,0:T(4,128)S(1)}, u32[]{:S(2)}, u32[]{:S(2)}) collective-permute-start(f32[14,4,128]{2,1,0:T(4,128)S(1)} %get-tuple-element.67), channel_id=1, source_target_pairs={{0,1},{1,0},{2,3},{3,2},{4,5},{5,4},{6,7},{7,6},{8,9},{9,8},{10,11... | collective-permute-start | bytes 86024 | tf_op jit(solution)/shard_map/ppermute | solution.py:459
  20.5 0.0 collective-permute-start.7
  20.5 2.8 %shard_map.142.base = f32[14,4,32,128]{3,2,1,0:T(8,128)S(1)} custom-call(f32[14,4,32,128]{3,2,1,0:T(8,128)S(1)} %get-tuple-element.61.gas, f32[28,16,128]{2,1,0:T(8,128)S(1)} %get-tuple-element.51.table, f32[14,4,32,128]{3,2,1,0:T(8,128)S(1)} %copy-done, f32[16,2304]{1,0:T(8,128)S(1)} %get-tuple-element.62.parcels.old, ...), custom_call_target="tpu_custom_call" | custom-call | flops 1000000 | bytes 10000 | tf_op jit(solution)/shard_map/pallas_call | solution.py:48
  23.2 0.3 %collective-permute-done.4.off = f32[464,128]{1,0:T(8,128)S(1)} collective-permute-done((f32[464,128]{1,0:T(8,128)S(1)}, f32[464,128]{1,0:T(8,128)S(1)}, u32[]{:S(2)}, u32[]{:S(2)}) %collective-permute-start.4) | collective-permute-done | bytes 237600 | tf_op jit(solution)/shard_map/ppermute | solution.py:448
  23.5 0.0 collective-permute-done.5.on
  23.5 0.6 %shard_map.143 = (f32[16,2304]{1,0:T(8,128)S(1)}, f32[16,128]{1,0:T(8,128)S(1)}, f32[16,128]{1,0:T(8,128)S(1)}, f32[2,16,128]{2,1,0:T(8,128)S(1)}, f32[8,128]{1,0:T(8,128)S(1)}) custom-call(f32[8,128]{1,0:T(8,128)S(1)} %get-tuple-element.69.count, f32[14,4,32,128]{3,2,1,0:T(8,128)S(1)} %get-tuple-element.61.gas, f32[28,16,128]{2,1,0:T(8,128)S(1)} %get-tuple-element.51.table, ...), custom_call_target="tpu_custom_call" | custom-call | flops 100000000 | bytes 2000000 | tf_op jit(solution)/shard_map/pallas_call | solution.py:48
  24.1 1.6 %collective-permute-start.8 = (f32[16,128]{1,0:T(8,128)S(1)}, f32[16,128]{1,0:T(8,128)S(1)}, u32[]{:S(2)}, u32[]{:S(2)}) collective-permute-start(f32[16,128]{1,0:T(8,128)S(1)} %get-tuple-element.74), channel_id=1, source_target_pairs={{4,8},{8,4},{12,16},{16,12},{20,24},{24,20},{28,0},{0,28},{5,9},{9... | collective-permute-start | bytes 24584 | tf_op jit(solution)/shard_map/ppermute | solution.py:448
  25.7 0.0 collective-permute-start.9
  25.8 0.0 collective-permute-done.6.near
  25.8 0.0 collective-permute-done.7.far
  25.8 1.3 %shard_map.144 = f32[14,4,32,128]{3,2,1,0:T(8,128)} custom-call(f32[28,16,128]{2,1,0:T(8,128)S(1)} %get-tuple-element.51.table, f32[14,4,32,128]{3,2,1,0:T(8,128)S(1)} %shard_map.142.base, f32[464,128]{1,0:T(8,128)S(1)} %collective-permute-done.4.off, f32[464,128]{1,0:T(8,128)S(1)} %collective-permute-done.5.on, ...), custom_call_target="tpu_custom_call" | custom-call | flops 100000000 | bytes 3000000 | tf_op jit(solution)/shard_map/pallas_call | solution.py:48
  27.1 1.1 %collective-permute-done.8.off = f32[16,128]{1,0:T(8,128)S(1)} collective-permute-done((f32[16,128]{1,0:T(8,128)S(1)}, f32[16,128]{1,0:T(8,128)S(1)}, u32[]{:S(2)}, u32[]{:S(2)}) %collective-permute-start.8) | collective-permute-done | bytes 8224 | tf_op jit(solution)/shard_map/ppermute | solution.py:448
  28.2 0.0 collective-permute-done.9.on
  28.2 0.9 %shard_map.145 = (f32[1,1,2048]{2,1,0:T(1,128)}, f32[7,1,1,2048]{3,2,1,0:T(1,128)}, s32[1,1,2048]{2,1,0:T(1,128)}, s32[1,1]{1,0:T(1,128)}) custom-call(f32[8,128]{1,0:T(8,128)S(1)} %get-tuple-element.73.count, f32[16,128]{1,0:T(8,128)S(1)} %collective-permute-done.8.off, f32[16,128]{1,0:T(8,128)S(1)} %collective-permute-done.9.on, ...), custom_call_target="tpu_custom_call" | custom-call | bytes 500000 | tf_op jit(solution)/shard_map/pallas_call | solution.py:48
Async XLA Ops:
  0.6 5.4 %copy-start = (f32[14,4,32,128]{3,2,1,0:T(8,128)S(1)}, f32[14,4,32,128]{3,2,1,0:T(8,128)}, u32[]{:S(2)}) copy-start(f32[14,4,32,128]{3,2,1,0:T(8,128)} %old_gas.1) | copy-start | bytes 2752516
  2.0 12.8 %collective-permute-start = (f32[448,128]{1,0:T(8,128)S(1)}, f32[448,128]{1,0:T(8,128)S(1)}, u32[]{:S(2)}, u32[]{:S(2)}) collective-permute-start(f32[448,128]{1,0:T(8,128)S(1)} %bitcast.5), channel_id=1, source_target_pairs={{4,8},{8,4},{12,16},{16,12},{20,24},{24,20},{28,0},{0,28},{5,9},{9... | collective-permute-start | bytes 688136 | tf_op jit(solution)/shard_map/ppermute | solution.py:448
  5.4 9.4 %collective-permute-start.1 = (f32[448,128]{1,0:T(8,128)S(1)}, f32[448,128]{1,0:T(8,128)S(1)}, u32[]{:S(2)}, u32[]{:S(2)}) collective-permute-start(f32[448,128]{1,0:T(8,128)S(1)} %bitcast.4), channel_id=1, source_target_pairs={{0,4},{4,0},{8,12},{12,8},{16,20},{20,16},{24,28},{28,24},{1,5},{5... | collective-permute-start | bytes 688136 | tf_op jit(solution)/shard_map/ppermute | solution.py:448
  8.8 5.9 %collective-permute-start.2 = (f32[14,4,128]{2,1,0:T(4,128)S(1)}, f32[14,4,128]{2,1,0:T(4,128)S(1)}, u32[]{:S(2)}, u32[]{:S(2)}) collective-permute-start(f32[14,4,128]{2,1,0:T(4,128)S(1)} %get-tuple-element.57), channel_id=1, source_target_pairs={{0,4},{1,2},{2,1},{3,7},{4,0},{5,6},{6,5},{7,3},{8,12},{9,10},{10,... | collective-permute-start | bytes 86024 | tf_op jit(solution)/shard_map/ppermute | solution.py:459
  9.4 5.4 %collective-permute-start.3 = (f32[14,4,128]{2,1,0:T(4,128)S(1)}, f32[14,4,128]{2,1,0:T(4,128)S(1)}, u32[]{:S(2)}, u32[]{:S(2)}) collective-permute-start(f32[14,4,128]{2,1,0:T(4,128)S(1)} %get-tuple-element.58), channel_id=1, source_target_pairs={{0,1},{1,0},{2,3},{3,2},{4,5},{5,4},{6,7},{7,6},{8,9},{9,8},{10,11... | collective-permute-start | bytes 86024 | tf_op jit(solution)/shard_map/ppermute | solution.py:459
  15.1 8.4 %collective-permute-start.4 = (f32[464,128]{1,0:T(8,128)S(1)}, f32[464,128]{1,0:T(8,128)S(1)}, u32[]{:S(2)}, u32[]{:S(2)}) collective-permute-start(f32[464,128]{1,0:T(8,128)S(1)} %get-tuple-element.65), channel_id=1, source_target_pairs={{4,8},{8,4},{12,16},{16,12},{20,24},{24,20},{28,0},{0,28},{5,9},{9... | collective-permute-start | bytes 712712 | tf_op jit(solution)/shard_map/ppermute | solution.py:448
  15.4 8.2 %collective-permute-start.5 = (f32[464,128]{1,0:T(8,128)S(1)}, f32[464,128]{1,0:T(8,128)S(1)}, u32[]{:S(2)}, u32[]{:S(2)}) collective-permute-start(f32[464,128]{1,0:T(8,128)S(1)} %get-tuple-element.66), channel_id=1, source_target_pairs={{0,4},{4,0},{8,12},{12,8},{16,20},{20,16},{24,28},{28,24},{1,5},{5... | collective-permute-start | bytes 712712 | tf_op jit(solution)/shard_map/ppermute | solution.py:448
  19.3 6.5 %collective-permute-start.6 = (f32[14,4,128]{2,1,0:T(4,128)S(1)}, f32[14,4,128]{2,1,0:T(4,128)S(1)}, u32[]{:S(2)}, u32[]{:S(2)}) collective-permute-start(f32[14,4,128]{2,1,0:T(4,128)S(1)} %get-tuple-element.67), channel_id=1, source_target_pairs={{0,1},{1,0},{2,3},{3,2},{4,5},{5,4},{6,7},{7,6},{8,9},{9,8},{10,11... | collective-permute-start | bytes 86024 | tf_op jit(solution)/shard_map/ppermute | solution.py:459
  20.5 5.3 %collective-permute-start.7 = (f32[14,4,128]{2,1,0:T(4,128)S(1)}, f32[14,4,128]{2,1,0:T(4,128)S(1)}, u32[]{:S(2)}, u32[]{:S(2)}) collective-permute-start(f32[14,4,128]{2,1,0:T(4,128)S(1)} %get-tuple-element.68), channel_id=1, source_target_pairs={{0,4},{1,2},{2,1},{3,7},{4,0},{5,6},{6,5},{7,3},{8,12},{9,10},{10,... | collective-permute-start | bytes 86024 | tf_op jit(solution)/shard_map/ppermute | solution.py:459
  24.1 4.0 %collective-permute-start.8 = (f32[16,128]{1,0:T(8,128)S(1)}, f32[16,128]{1,0:T(8,128)S(1)}, u32[]{:S(2)}, u32[]{:S(2)}) collective-permute-start(f32[16,128]{1,0:T(8,128)S(1)} %get-tuple-element.74), channel_id=1, source_target_pairs={{4,8},{8,4},{12,16},{16,12},{20,24},{24,20},{28,0},{0,28},{5,9},{9... | collective-permute-start | bytes 24584 | tf_op jit(solution)/shard_map/ppermute | solution.py:448
  25.7 2.4 %collective-permute-start.9 = (f32[16,128]{1,0:T(8,128)S(1)}, f32[16,128]{1,0:T(8,128)S(1)}, u32[]{:S(2)}, u32[]{:S(2)}) collective-permute-start(f32[16,128]{1,0:T(8,128)S(1)} %get-tuple-element.75), channel_id=1, source_target_pairs={{0,4},{4,0},{8,12},{12,8},{16,20},{20,16},{24,28},{28,24},{1,5},{5... | collective-permute-start | bytes 24584 | tf_op jit(solution)/shard_map/ppermute | solution.py:448

commit v5 on v4

--- a/solution.py
+++ b/solution.py
@@ -104,15 +104,18 @@
     return jnp.broadcast_to(table[k, f : f + 1], (rows, LANES))
 
 
-def inner_terms(gas, table, tanh):
+def inner_terms(gas, table, tanh, layers):
     nf, ca, cr, cz = gas.shape
     lane = iota((cr, cz), 1)
     row = iota((cr, cz), 0)
     chem = table.shape[0] - nf
+    for g in range(nf):
+        for a in layers:
+            tanh[g, a] = jnp.tanh(gas[g, a])
     for f in range(nf):
         nu, upper, lower, east, west = (spread(table, k, f, cr) for k in (NU, UPPER, LOWER, EAST, WEST))
-        totals = []
-        for a in range(ca):
+        totals = {}
+        for a in layers:
             here = gas[f, a]
             total = nu * (
                 jnp.where(row == cr - 1, 0.0, pltpu.roll(here, cr - 1, 0))
@@ -125,12 +128,12 @@
                 total += east * gas[f, a + 1]
             if a > 0:
                 total += west * gas[f, a - 1]
-            totals.append(total)
+            totals[a] = total
         for g in range(nf):
             rate = spread(table, chem + g, f, cr)
-            for a in range(ca):
+            for a in layers:
                 totals[a] += rate * tanh[g, a]
-        for a in range(ca):
+        for a in layers:
             yield f, a, totals[a]
 
 
@@ -145,7 +148,8 @@
             table[f * cr : (f + 1) * cr, width + a * cz : width + (a + 1) * cz] = lower
     span = cr * cz
     block = 256
-    for b in range(slots // block):
+
+    def probe(b):
         cells = host[:, b * block : (b + 1) * block]
         column = (cells // span) * cz + cells % cz
         row = (cells // cz) % cr
@@ -156,6 +160,9 @@
         mask = iota((cr, block), 0) == row
         found = jnp.where(mask[None], found.reshape(nf, cr, block), 0.0)
         probed[:nf, b * block : (b + 1) * block] = jnp.sum(found, axis=1)
+
+    for b in range(slots // block):
+        probe(b)
 
 
 def react(probed, attr, live, table, nf):
@@ -175,16 +182,18 @@
 
 def deposit_all(source, host, hots, shapes, reach, total):
     nf, ca, cr, cz = shapes
-    width = ca * cz
     block = 512 if reach % 512 == 0 else 128
     for b in range(reach // block):
         cells = host[:, b * block : (b + 1) * block]
         row = (cells // cz) % cr
         mask = iota((cr, block), 0) == row
-        spread = jnp.where(mask[None], source[:nf, b * block : (b + 1) * block][:, None, :], 0.0)
-        upper, lower = parts_of(spread.reshape(nf * cr, block), 2)
         ahot = hots[:, b * block : (b + 1) * block]
-        part = across(upper, ahot) + across(lower, ahot)
+        part = None
+        for piece in parts_of(source[:nf, b * block : (b + 1) * block], 2):
+            piece = piece.astype(F32)
+            laid = [jnp.where(mask, piece[f : f + 1], 0.0).astype(BF16) for f in range(nf)]
+            one = across(jnp.concatenate(laid, axis=0), ahot)
+            part = one if part is None else part + one
         if b == 0:
             total[...] = part
         else:
@@ -228,6 +237,10 @@
     return jnp.where(flip, left, right), jnp.where(flip, right, left)
 
 
+def rows_kernel(gas, after, near, far):
+    send_rows(gas, near, far)
+
+
 def send_rows(gas, near, far):
     cr = gas.shape[2]
     flip = odd("radax") == 1
@@ -239,11 +252,10 @@
 
 def probe_one_kernel(
     count, gas, transport, chemistry, evap, source_map, lists, mass, state, host_in,
-    near, far, parcels, on, off, table, hots, source, used, cells, probed, lhot,
+    parcels, on, off, table, hots, source, used, cells, probed, lhot,
 ):
     nf, ca, cr, cz = gas.shape
     slots = probed.shape[1]
-    send_rows(gas, near, far)
     fill_table(table, transport, chemistry, evap, source_map)
     host = host_in[0]
     used[...] = jnp.broadcast_to(count[...].astype(F32), used.shape)
@@ -255,15 +267,57 @@
     parcels[LIVE : LIVE + 1, :slots] = jnp.where(gone_from(lhot[...]) > 0.5, 0.0, live)
 
 
-def field_one_kernel(spare, gas, table, parcels, hots, source, out, total, tanh):
-    nf, ca, cr, cz = gas.shape
-    slots = hots.shape[1]
-    for g in range(nf):
-        tanh[g] = jnp.tanh(gas[g])
-    host = parcels[HOST : HOST + 1, :slots].astype(jnp.int32)
-    deposit_all(source, host, hots, gas.shape, slots - spare, total)
-    for f, a, terms in inner_terms(gas, table, tanh):
-        out[f, a] = gas[f, a] + DT * (terms + total[f * cr : (f + 1) * cr, a * cz : (a + 1) * cz])
+def field_one_kernel(reach, gas, table, parcels, hots, source, out, total, tanh):
+    nf, ca, cr, cz = gas.shape
+    host = parcels[HOST : HOST + 1, :reach].astype(jnp.int32)
+    deposit_all(source, host, hots, gas.shape, reach, total)
+    for f, a, terms in inner_terms(gas, table, tanh, (0, ca - 1)):
+        terms += total[f * cr : (f + 1) * cr, a * cz : (a + 1) * cz]
+        out[f, min(a, 1)] = gas[f, a] + DT * terms
+
+
+def radial_halos(near, far, f):
+    block = lax.axis_index("radax")
+    flip = odd("radax") == 1
+    north = jnp.where(flip, far[f], near[f])
+    south = jnp.where(flip, near[f], far[f])
+    return jnp.where(block == 0, 0.0, south), jnp.where(block == lax.axis_size("radax") - 1, 0.0, north)
+
+
+def edge_kernel(table, outer, far, near, pack_on, pack_off, send_on, send_off):
+    nf, _, cr, cz = outer.shape
+    ca = near.shape[1]
+    flip = odd("azim") == 1
+    row = iota((cr, cz), 0)
+    for f in range(nf):
+        south, north = radial_halos(near, far, f)
+        nu = DT * spread(table, NU, f, cr)
+        low, high = (
+            outer[f, k]
+            + nu
+            * (
+                jnp.where(row == 0, jnp.broadcast_to(south[a : a + 1], (cr, cz)), 0.0)
+                + jnp.where(row == cr - 1, jnp.broadcast_to(north[a : a + 1], (cr, cz)), 0.0)
+            )
+            for k, a in ((0, 0), (1, ca - 1))
+        )
+        send_on[f * cr : (f + 1) * cr] = jnp.where(flip, low, high)
+        send_off[f * cr : (f + 1) * cr] = jnp.where(flip, high, low)
+    send_on[nf * cr :] = pack_on[...]
+    send_off[nf * cr :] = pack_off[...]
+
+
+def join_kernel(gas, table, outer, total, off, on, far, near, out, tanh):
+    nf, ca, cr, cz = gas.shape
+    for f in range(nf):
+        out[f, 0] = outer[f, 0]
+        out[f, ca - 1] = outer[f, 1]
+    for f, a, terms in inner_terms(gas, table, tanh, range(1, ca - 1)):
+        terms += total[f * cr : (f + 1) * cr, a * cz : (a + 1) * cz]
+        out[f, a] = gas[f, a] + DT * terms
+    for f in range(nf):
+        west, east = sides(on[f * cr : (f + 1) * cr], off[f * cr : (f + 1) * cr])
+        edge_terms(DT, table, out, f, west, east, near, far)
 
 
 def probe_two_kernel(
@@ -272,22 +326,20 @@
     slots = probed.shape[1]
     send_rows(gas, near, far)
     host = old[HOST : HOST + 1, :slots].astype(jnp.int32)
+    live = old[LIVE : LIVE + 1, :slots]
     source[: gas.shape[0]] = parcel_work(
-        gas, host, old[0:HOST, :slots], old[LIVE : LIVE + 1, :slots], table, parcels, cells, hots, probed
+        gas, host, old[0:HOST, :slots], live, table, parcels, cells, hots, probed
     )
     list_hots(lists, 1, slots, lhot)
     taken[...] = gather(parcels[:, :slots], lhot[...])
     parcels[GONE : GONE + 1, :slots] = gone_from(lhot[...])
 
 
-def field_two_kernel(spare, gas, table, old_gas, parcels, hots, source, out, total, tanh):
-    nf, ca, cr, cz = gas.shape
-    slots = hots.shape[1]
-    for g in range(nf):
-        tanh[g] = jnp.tanh(gas[g])
-    host = parcels[HOST : HOST + 1, :slots].astype(jnp.int32)
-    deposit_all(source, host, hots, gas.shape, slots - spare, total)
-    for f, a, terms in inner_terms(gas, table, tanh):
+def field_two_kernel(reach, gas, table, old_gas, parcels, hots, source, out, total, tanh):
+    nf, ca, cr, cz = gas.shape
+    host = parcels[HOST : HOST + 1, :reach].astype(jnp.int32)
+    deposit_all(source, host, hots, gas.shape, reach, total)
+    for f, a, terms in inner_terms(gas, table, tanh, range(ca)):
         terms += total[f * cr : (f + 1) * cr, a * cz : (a + 1) * cz]
         out[f, a] = 0.5 * (old_gas[f, a] + gas[f, a] + DT * terms)
 
@@ -303,35 +355,14 @@
     return source
 
 
-def edge_terms(scale, table, out, on, off, near, far):
-    nf, ca, cr, cz = out.shape
-    block = lax.axis_index("radax")
-    inner, outer = block == 0, block == lax.axis_size("radax") - 1
-    flip_a, flip_r = odd("azim") == 1, odd("radax") == 1
-    for f in range(nf):
-        got_on, got_off = on[f * cr : (f + 1) * cr], off[f * cr : (f + 1) * cr]
-        east = jnp.where(flip_a, got_off, got_on)
-        west = jnp.where(flip_a, got_on, got_off)
-        out[f, 0] += (scale * spread(table, WEST, f, cr)) * west
-        out[f, ca - 1] += (scale * spread(table, EAST, f, cr)) * east
-        north = jnp.where(outer, 0.0, jnp.where(flip_r, far[f], near[f]))
-        south = jnp.where(inner, 0.0, jnp.where(flip_r, near[f], far[f]))
-        nu = scale * spread(table, NU, f, ca)
-        out[f, :, 0, :] += nu * south
-        out[f, :, cr - 1, :] += nu * north
-
-
-def edge_kernel(table, base, off, on, far, near, pack_on, pack_off, out, send_on, send_off):
-    nf, ca, cr, cz = out.shape
-    out[...] = base[...]
-    edge_terms(DT, table, out, on, off, near, far)
-    flip = odd("azim") == 1
-    for f in range(nf):
-        low, high = out[f, 0], out[f, ca - 1]
-        send_on[f * cr : (f + 1) * cr] = jnp.where(flip, low, high)
-        send_off[f * cr : (f + 1) * cr] = jnp.where(flip, high, low)
-    send_on[nf * cr :] = pack_on[...]
-    send_off[nf * cr :] = pack_off[...]
+def edge_terms(scale, table, out, f, west, east, near, far):
+    ca, cr = out.shape[1], out.shape[2]
+    out[f, 0] += (scale * spread(table, WEST, f, cr)) * west
+    out[f, ca - 1] += (scale * spread(table, EAST, f, cr)) * east
+    south, north = radial_halos(near, far, f)
+    nu = scale * spread(table, NU, f, ca)
+    out[f, :, 0, :] += nu * south
+    out[f, :, cr - 1, :] += nu * north
 
 
 def put(parcels, pack, start, live):
@@ -403,10 +434,14 @@
     parcels[LIVE : LIVE + 1, :slots] = jnp.where(gone, 0.0, parcels[LIVE : LIVE + 1, :slots])
 
 
-def finish_kernel(table, base, off, on, near, far, sources, out):
+def finish_kernel(table, base, gas, off, on, near, far, sources, out):
     nf, ca, cr, cz = out.shape
     out[...] = base[...]
-    edge_terms(0.5 * DT, table, out, on, off, near, far)
+    for f in range(nf):
+        west, east = sides(on[f * cr : (f + 1) * cr], off[f * cr : (f + 1) * cr])
+        west += (DT * spread(table, EAST, f, cr)) * gas[f, 0]
+        east += (DT * spread(table, WEST, f, cr)) * gas[f, ca - 1]
+        edge_terms(0.5 * DT, table, out, f, west, east, near, far)
     for side in range(2):
         layer = side * (ca - 1)
         cell = sources[side, nf : nf + 1].astype(jnp.int32)
@@ -484,44 +519,54 @@
     off = swap(off.reshape(nf * cr, cz), "azim", 1)
     on = swap(on.reshape(nf * cr, cz), "azim", 0)
 
+    near, far = call(rows_kernel, [ring, ring], [VMEM] * 2, [VMEM] * 2, (gas, transport), moved=100_000)
+    near = swap_rows(near, 0)
+    far = swap_rows(far, 1)
     hots, lhot = shape((ca * cz, slots), BF16), shape((2 * width, slots), BF16)
     source = shape((ROWS, slots))
     probe_scratch = [pltpu.VMEM((nf * cr, 2 * ca * cz), BF16), pltpu.VMEM((ROWS, slots), F32)]
-    field_scratch = [pltpu.VMEM((nf * cr, ca * cz), F32), pltpu.VMEM(gas.shape, F32)]
+    tanh_scratch = pltpu.VMEM(gas.shape, F32)
+    total = shape((nf * cr, ca * cz))
     heavy = dict(flops=3_000_000_000, moved=2_000_000, trans=300_000)
-    near, far, parcels, pack_on, pack_off, table, cell_hots, sources, used = call(
+    light = dict(flops=1_000_000, moved=10_000)
+    parcels, pack_on, pack_off, table, cell_hots, sources, used = call(
         probe_one_kernel,
-        [ring, ring, slotted, pack, pack, shape((SOURCE + source_map.shape[0] + nf, ROWS, LANES)), hots, source, tile],
+        [slotted, pack, pack, shape((SOURCE + source_map.shape[0] + nf, ROWS, LANES)), hots, source, tile],
         [VMEM] * 10,
-        [VMEM] * 9,
+        [VMEM] * 7,
         (count, gas, transport, chemistry, evap, source_map, crossing, mass, state, host),
         scratch=probe_scratch + [pltpu.VMEM(lhot.shape, BF16)],
         **heavy,
     )
-    near = swap_rows(near, 0)
-    far = swap_rows(far, 1)
-    base = call(
-        functools.partial(field_one_kernel, 4 * width),
+    outer, total = call(
+        functools.partial(field_one_kernel, slots - 4 * width),
+        [shape((nf, 2, cr, cz)), total],
+        [VMEM] * 5,
+        [VMEM] * 2,
+        (gas, table, parcels, cell_hots, sources),
+        scratch=[tanh_scratch],
+        **light,
+    )
+    longer = shape((nf * cr + ROWS, cz))
+    send_on, send_off = call(
+        edge_kernel,
+        [longer, longer],
+        [VMEM] * 6,
+        [VMEM] * 2,
+        (table, outer, far, near, pack_on, pack_off),
+        **light,
+    )
+    section_one = call(
+        join_kernel,
         grid,
-        [VMEM] * 5,
+        [VMEM] * 8,
         VMEM,
-        (gas, table, parcels, cell_hots, sources),
-        scratch=field_scratch,
-        flops=1_000_000,
-        moved=10_000,
-    )
-    longer = shape((nf * cr + ROWS, cz))
-    section_one, on, off = call(
-        edge_kernel,
-        [grid, longer, longer],
-        [VMEM] * 8,
-        [VMEM] * 3,
-        (table, base, off, on, far, near, pack_on, pack_off),
-        aliases={1: 0},
-        moved=3_000_000,
-    )
-    off = swap(off, "azim", 1)
-    on = swap(on, "azim", 0)
+        (gas, table, outer, total, off, on, far, near),
+        scratch=[tanh_scratch],
+        **heavy,
+    )
+    off = swap(send_off, "azim", 1)
+    on = swap(send_on, "azim", 0)
     near, far, parcels, cell_hots, sources, taken, named = call(
         probe_two_kernel,
         [ring, ring, slotted, hots, source, shape((ROWS, 2 * width)), lhot],
@@ -529,19 +574,18 @@
         [VMEM] * 7,
         (section_one, table, crossing, parcels),
         scratch=probe_scratch,
-        **heavy,
+        **light,
     )
     near = swap_rows(near, 0)
     far = swap_rows(far, 1)
     base = call(
-        functools.partial(field_two_kernel, 4 * width),
+        functools.partial(field_two_kernel, slots - 4 * width),
         grid,
         [VMEM] * 6,
         VMEM,
         (section_one, table, gas, parcels, cell_hots, sources),
-        scratch=field_scratch,
-        flops=1_000_000,
-        moved=10_000,
+        scratch=[pltpu.VMEM(total.shape, F32), tanh_scratch],
+        **light,
     )
     parcels, pack_on, pack_off, sources, used_now = call(
         arrive_kernel,
@@ -558,9 +602,9 @@
     gas_next = call(
         finish_kernel,
         shape(gas.shape),
-        [VMEM] * 7,
+        [VMEM] * 8,
         VMEM,
-        (table, base, off, on, near, far, sources),
+        (table, base, gas, off, on, near, far, sources),
         flops=100_000_000,
         moved=3_000_000,
     )

time: 29.2 us -> 28.8 us (0.986)
  starting transfers between devices: 10.8 us -> 9.3 us
  waiting for transfers between devices: 1.45 us -> 1.98 us
  Pallas kernels: 15.4 us -> 15.7 us
    ppermute x6, starting transfers between devices: 6.39 us -> 4.51 us  [swap(): return lax.ppermute(array, axis, pairs)]
    ppermute x6, waiting for transfers between devices: 1.44 us -> 1.97 us  [swap(): return lax.ppermute(array, axis, pairs)]
    ppermute x4, starting transfers between devices: 4.4 us -> 4.79 us  [swap_rows(): return lax.ppermute(array, ('azim', 'radax'), pairs)]
    pallas_call x9 -> x11, Pallas kernels: 15.4 us -> 15.7 us  [call(): pl.pallas_call(kernel, out_shape=outs, in_specs=ins, out_specs=out_specs,...]
  transfers between devices with their start and end apart: 10 -> 10, of which waited for: 2 -> 2; matrix products, arithmetic and copies ran while one was open for 0% -> 0% of each run, Pallas kernels for 45% -> 47%
where the time goes in v5:
time: 28.8 us; the launch traced here: 28.6 us
  Pallas kernels  15.7 us (55%)
  starting transfers between devices  9.3 us (32%)
  waiting for transfers between devices  1.98 us (7%)
  between operations  1.39 us (5%)
    pallas_call x11, Pallas kernels, call(): pl.pallas_call(kernel, out_shape=outs, in_specs=ins, out_specs=out_specs,...  15.7 us
    ppermute x4, starting transfers between devices, swap_rows(): return lax.ppermute(array, ('azim', 'radax'), pairs)  4.79 us
    ppermute x6, starting transfers between devices, swap(): return lax.ppermute(array, axis, pairs)  4.51 us
    ppermute x6, waiting for transfers between devices, swap(): return lax.ppermute(array, axis, pairs)  1.97 us
  transfers between devices with their start and end apart: 10, of which 2 were waited for; matrix products, arithmetic and copies ran while one was open for 0% of the time, Pallas kernels for 47%

profile of v5, /device:TPU:0, one launch (start us, length us, event | category | flops | bytes accessed | tf_op | source)
XLA Modules:
  0.0 28.6 jit_solution(13769605282711939731)
XLA Ops:
  0.6 0.0 copy-start
  0.6 1.3 %shard_map.137 = (f32[14,32,128]{2,1,0:T(8,128)S(1)}, f32[14,32,128]{2,1,0:T(8,128)S(1)}, f32[3,14]{1,0:T(4,128)S(1)}, f32[14,14]{1,0:T(8,128)S(1)}, f32[1,14]{1...) custom-call(f32[14,4,32,128]{3,2,1,0:T(8,128)} %gas.11, ...), custom_call_target="tpu_custom_call" | custom-call | flops 5000000000 | bytes 2000000 | tf_op jit(solution)/shard_map/pallas_call | solution.py:48
  2.0 0.2 copy-done
  2.2 0.5 %collective-permute-start.2 = (f32[14,4,128]{2,1,0:T(4,128)S(1)}, f32[14,4,128]{2,1,0:T(4,128)S(1)}, u32[]{:S(2)}, u32[]{:S(2)}) collective-permute-start(f32[14,4,128]{2,1,0:T(4,128)S(1)} %get-tuple-element.60), channel_id=1, source_target_pairs={{0,4},{1,2},{2,1},{3,7},{4,0},{5,6},{6,5},{7,3},{8,12},{9,10},{10,... | collective-permute-start | bytes 86024 | tf_op jit(solution)/shard_map/ppermute | solution.py:494
  2.7 4.1 %collective-permute-start.3 = (f32[14,4,128]{2,1,0:T(4,128)S(1)}, f32[14,4,128]{2,1,0:T(4,128)S(1)}, u32[]{:S(2)}, u32[]{:S(2)}) collective-permute-start(f32[14,4,128]{2,1,0:T(4,128)S(1)} %get-tuple-element.61), channel_id=1, source_target_pairs={{0,1},{1,0},{2,3},{3,2},{4,5},{5,4},{6,7},{7,6},{8,9},{9,8},{10,11... | collective-permute-start | bytes 86024 | tf_op jit(solution)/shard_map/ppermute | solution.py:494
  6.9 1.3 %collective-permute-start = (f32[448,128]{1,0:T(8,128)S(1)}, f32[448,128]{1,0:T(8,128)S(1)}, u32[]{:S(2)}, u32[]{:S(2)}) collective-permute-start(f32[448,128]{1,0:T(8,128)S(1)} %bitcast.5), channel_id=1, source_target_pairs={{4,8},{8,4},{12,16},{16,12},{20,24},{24,20},{28,0},{0,28},{5,9},{9... | collective-permute-start | bytes 688136 | tf_op jit(solution)/shard_map/ppermute | solution.py:483
  8.2 0.3 collective-permute-start.1
  9.1 2.8 %shard_map.138 = (f32[16,2304]{1,0:T(8,128)S(1)}, f32[16,128]{1,0:T(8,128)S(1)}, f32[16,128]{1,0:T(8,128)S(1)}, f32[28,16,128]{2,1,0:T(8,128)S(1)}, bf16[512,204...) custom-call(s32[1,1]{1,0:T(1,128)S(6)} %copy.15.count, f32[14,4,32,128]{3,2,1,0:T(8,128)S(1)} %copy-done, ...), custom_call_target="tpu_custom_call" | custom-call | flops 3000000000 | bytes 2000000 | tf_op jit(solution)/shard_map/pallas_call | solution.py:48
  11.9 2.2 %shard_map.139 = (f32[14,2,32,128]{3,2,1,0:T(8,128)S(1)}, f32[448,512]{1,0:T(8,128)S(1)}) custom-call(f32[14,4,32,128]{3,2,1,0:T(8,128)S(1)} %copy-done, f32[28,16,128]{2,1,0:T(8,128)S(1)} %get-tuple-element.52.table, f32[16,2304]{1,0:T(8,128)S(1)} %get-tuple-element.53.parcels.old, bf16[512,2048]{1,0:T(8,128)(2,1)S(1)} %get-tuple-element.54.hots, ...), custom_call_target="tpu_custom_call" | custom-call | flops 1000000 | bytes 10000 | tf_op jit(solution)/shard_map/pallas_call | solution.py:48
  14.2 0.0 collective-permute-done.2.far
  14.2 0.0 collective-permute-done.3.near
  14.2 0.1 shard_map.144
  14.3 1.1 %collective-permute-start.4 = (f32[464,128]{1,0:T(8,128)S(1)}, f32[464,128]{1,0:T(8,128)S(1)}, u32[]{:S(2)}, u32[]{:S(2)}) collective-permute-start(f32[464,128]{1,0:T(8,128)S(1)} %get-tuple-element.67), channel_id=1, source_target_pairs={{4,8},{8,4},{12,16},{16,12},{20,24},{24,20},{28,0},{0,28},{5,9},{9... | collective-permute-start | bytes 712712 | tf_op jit(solution)/shard_map/ppermute | solution.py:483
  15.4 0.6 %collective-permute-start.5 = (f32[464,128]{1,0:T(8,128)S(1)}, f32[464,128]{1,0:T(8,128)S(1)}, u32[]{:S(2)}, u32[]{:S(2)}) collective-permute-start(f32[464,128]{1,0:T(8,128)S(1)} %get-tuple-element.68), channel_id=1, source_target_pairs={{0,4},{4,0},{8,12},{12,8},{16,20},{20,16},{24,28},{28,24},{1,5},{5... | collective-permute-start | bytes 712712 | tf_op jit(solution)/shard_map/ppermute | solution.py:483
  16.0 0.0 collective-permute-done.off
  16.0 0.0 collective-permute-done.1.on
  16.0 1.0 %shard_map.141.gas = f32[14,4,32,128]{3,2,1,0:T(8,128)S(1)} custom-call(f32[14,4,32,128]{3,2,1,0:T(8,128)S(1)} %copy-done, f32[28,16,128]{2,1,0:T(8,128)S(1)} %get-tuple-element.52.table, f32[14,2,32,128]{3,2,1,0:T(8,128)S(1)} %get-tuple-element.56.outer, f32[448,512]{1,0:T(8,128)S(1)} %get-tuple-element.57.total, f32[448,128]{1,0:T(8,128)S(1)} %collective-permute-done.off, ...), custom_call_target="tpu_custom_call" | custom-call | flops 3000000000 | bytes 2000000 | tf_op jit(solution)/shard_map/pallas_call | solution.py:48
  17.0 2.8 %shard_map.142 = (f32[14,4,128]{2,1,0:T(4,128)S(1)}, f32[14,4,128]{2,1,0:T(4,128)S(1)}, f32[16,2304]{1,0:T(8,128)S(1)}, bf16[512,2048]{1,0:T(8,128)(2,1)S(1)}, f...) custom-call(f32[14,4,32,128]{3,2,1,0:T(8,128)S(1)} %shard_map.141.gas, ...), custom_call_target="tpu_custom_call" | custom-call | flops 1000000 | bytes 10000 | tf_op jit(solution)/shard_map/pallas_call | solution.py:48
  19.8 0.1 collective-permute-start.6
  19.8 0.1 collective-permute-start.7
  19.9 2.6 %shard_map.143.base = f32[14,4,32,128]{3,2,1,0:T(8,128)S(1)} custom-call(f32[14,4,32,128]{3,2,1,0:T(8,128)S(1)} %shard_map.141.gas, f32[28,16,128]{2,1,0:T(8,128)S(1)} %get-tuple-element.52.table, f32[14,4,32,128]{3,2,1,0:T(8,128)S(1)} %copy-done, f32[16,2304]{1,0:T(8,128)S(1)} %get-tuple-element.62.parcels.old, ...), custom_call_target="tpu_custom_call" | custom-call | flops 1000000 | bytes 10000 | tf_op jit(solution)/shard_map/pallas_call | solution.py:48
  22.6 0.5 %collective-permute-done.4.off = f32[464,128]{1,0:T(8,128)S(1)} collective-permute-done((f32[464,128]{1,0:T(8,128)S(1)}, f32[464,128]{1,0:T(8,128)S(1)}, u32[]{:S(2)}, u32[]{:S(2)}) %collective-permute-start.4) | collective-permute-done | bytes 237600 | tf_op jit(solution)/shard_map/ppermute | solution.py:483
  23.1 0.0 collective-permute-done.5.on
  23.1 0.6 %shard_map.145 = (f32[16,2304]{1,0:T(8,128)S(1)}, f32[16,128]{1,0:T(8,128)S(1)}, f32[16,128]{1,0:T(8,128)S(1)}, f32[2,16,128]{2,1,0:T(8,128)S(1)}, f32[8,128]{1,0:T(8,128)S(1)}) custom-call(f32[8,128]{1,0:T(8,128)S(1)} %get-tuple-element.71.count, f32[14,4,32,128]{3,2,1,0:T(8,128)S(1)} %shard_map.141.gas, f32[28,16,128]{2,1,0:T(8,128)S(1)} %get-tuple-element.52.table, ...), custom_call_target="tpu_custom_call" | custom-call | flops 100000000 | bytes 2000000 | tf_op jit(solution)/shard_map/pallas_call | solution.py:48
  23.7 1.2 %collective-permute-start.8 = (f32[16,128]{1,0:T(8,128)S(1)}, f32[16,128]{1,0:T(8,128)S(1)}, u32[]{:S(2)}, u32[]{:S(2)}) collective-permute-start(f32[16,128]{1,0:T(8,128)S(1)} %get-tuple-element.76), channel_id=1, source_target_pairs={{4,8},{8,4},{12,16},{16,12},{20,24},{24,20},{28,0},{0,28},{5,9},{9... | collective-permute-start | bytes 24584 | tf_op jit(solution)/shard_map/ppermute | solution.py:483
  24.9 0.0 collective-permute-start.9
  24.9 0.0 collective-permute-done.6.near
  24.9 0.0 collective-permute-done.7.far
  24.9 1.4 %shard_map.146 = f32[14,4,32,128]{3,2,1,0:T(8,128)} custom-call(f32[28,16,128]{2,1,0:T(8,128)S(1)} %get-tuple-element.52.table, f32[14,4,32,128]{3,2,1,0:T(8,128)S(1)} %shard_map.143.base, f32[14,4,32,128]{3,2,1,0:T(8,128)S(1)} %copy-done, f32[464,128]{1,0:T(8,128)S(1)} %collective-permute-done.4.off, f32[464,128]{1,0:T(8,128)S(1)} %collective-permute-done.5.on, ...), custom_call_target="tpu_custom_call" | custom-call | flops 100000000 | bytes 3000000 | tf_op jit(solution)/shard_map/pallas_call | solution.py:48
  26.3 1.4 %collective-permute-done.8.off = f32[16,128]{1,0:T(8,128)S(1)} collective-permute-done((f32[16,128]{1,0:T(8,128)S(1)}, f32[16,128]{1,0:T(8,128)S(1)}, u32[]{:S(2)}, u32[]{:S(2)}) %collective-permute-start.8) | collective-permute-done | bytes 8224 | tf_op jit(solution)/shard_map/ppermute | solution.py:483
  27.7 0.0 collective-permute-done.9.on
  27.7 0.9 %shard_map.147 = (f32[1,1,2048]{2,1,0:T(1,128)}, f32[7,1,1,2048]{3,2,1,0:T(1,128)}, s32[1,1,2048]{2,1,0:T(1,128)}, s32[1,1]{1,0:T(1,128)}) custom-call(f32[8,128]{1,0:T(8,128)S(1)} %get-tuple-element.75.count, f32[16,128]{1,0:T(8,128)S(1)} %collective-permute-done.8.off, f32[16,128]{1,0:T(8,128)S(1)} %collective-permute-done.9.on, ...), custom_call_target="tpu_custom_call" | custom-call | bytes 500000 | tf_op jit(solution)/shard_map/pallas_call | solution.py:48
  (1 shorter events, 0.0 us)
Async XLA Ops:
  0.6 1.5 %copy-start = (f32[14,4,32,128]{3,2,1,0:T(8,128)S(1)}, f32[14,4,32,128]{3,2,1,0:T(8,128)}, u32[]{:S(2)}) copy-start(f32[14,4,32,128]{3,2,1,0:T(8,128)} %gas.11) | copy-start | bytes 2752516
  2.2 12.0 %collective-permute-start.2 = (f32[14,4,128]{2,1,0:T(4,128)S(1)}, f32[14,4,128]{2,1,0:T(4,128)S(1)}, u32[]{:S(2)}, u32[]{:S(2)}) collective-permute-start(f32[14,4,128]{2,1,0:T(4,128)S(1)} %get-tuple-element.60), channel_id=1, source_target_pairs={{0,4},{1,2},{2,1},{3,7},{4,0},{5,6},{6,5},{7,3},{8,12},{9,10},{10,... | collective-permute-start | bytes 86024 | tf_op jit(solution)/shard_map/ppermute | solution.py:494
  2.7 11.5 %collective-permute-start.3 = (f32[14,4,128]{2,1,0:T(4,128)S(1)}, f32[14,4,128]{2,1,0:T(4,128)S(1)}, u32[]{:S(2)}, u32[]{:S(2)}) collective-permute-start(f32[14,4,128]{2,1,0:T(4,128)S(1)} %get-tuple-element.61), channel_id=1, source_target_pairs={{0,1},{1,0},{2,3},{3,2},{4,5},{5,4},{6,7},{7,6},{8,9},{9,8},{10,11... | collective-permute-start | bytes 86024 | tf_op jit(solution)/shard_map/ppermute | solution.py:494
  6.9 9.1 %collective-permute-start = (f32[448,128]{1,0:T(8,128)S(1)}, f32[448,128]{1,0:T(8,128)S(1)}, u32[]{:S(2)}, u32[]{:S(2)}) collective-permute-start(f32[448,128]{1,0:T(8,128)S(1)} %bitcast.5), channel_id=1, source_target_pairs={{4,8},{8,4},{12,16},{16,12},{20,24},{24,20},{28,0},{0,28},{5,9},{9... | collective-permute-start | bytes 688136 | tf_op jit(solution)/shard_map/ppermute | solution.py:483
  8.2 7.8 %collective-permute-start.1 = (f32[448,128]{1,0:T(8,128)S(1)}, f32[448,128]{1,0:T(8,128)S(1)}, u32[]{:S(2)}, u32[]{:S(2)}) collective-permute-start(f32[448,128]{1,0:T(8,128)S(1)} %bitcast.4), channel_id=1, source_target_pairs={{0,4},{4,0},{8,12},{12,8},{16,20},{20,16},{24,28},{28,24},{1,5},{5... | collective-permute-start | bytes 688136 | tf_op jit(solution)/shard_map/ppermute | solution.py:483
  14.3 8.8 %collective-permute-start.4 = (f32[464,128]{1,0:T(8,128)S(1)}, f32[464,128]{1,0:T(8,128)S(1)}, u32[]{:S(2)}, u32[]{:S(2)}) collective-permute-start(f32[464,128]{1,0:T(8,128)S(1)} %get-tuple-element.67), channel_id=1, source_target_pairs={{4,8},{8,4},{12,16},{16,12},{20,24},{24,20},{28,0},{0,28},{5,9},{9... | collective-permute-start | bytes 712712 | tf_op jit(solution)/shard_map/ppermute | solution.py:483
  15.4 7.7 %collective-permute-start.5 = (f32[464,128]{1,0:T(8,128)S(1)}, f32[464,128]{1,0:T(8,128)S(1)}, u32[]{:S(2)}, u32[]{:S(2)}) collective-permute-start(f32[464,128]{1,0:T(8,128)S(1)} %get-tuple-element.68), channel_id=1, source_target_pairs={{0,4},{4,0},{8,12},{12,8},{16,20},{20,16},{24,28},{28,24},{1,5},{5... | collective-permute-start | bytes 712712 | tf_op jit(solution)/shard_map/ppermute | solution.py:483
  19.8 5.2 %collective-permute-start.6 = (f32[14,4,128]{2,1,0:T(4,128)S(1)}, f32[14,4,128]{2,1,0:T(4,128)S(1)}, u32[]{:S(2)}, u32[]{:S(2)}) collective-permute-start(f32[14,4,128]{2,1,0:T(4,128)S(1)} %get-tuple-element.69), channel_id=1, source_target_pairs={{0,1},{1,0},{2,3},{3,2},{4,5},{5,4},{6,7},{7,6},{8,9},{9,8},{10,11... | collective-permute-start | bytes 86024 | tf_op jit(solution)/shard_map/ppermute | solution.py:494
  19.8 5.1 %collective-permute-start.7 = (f32[14,4,128]{2,1,0:T(4,128)S(1)}, f32[14,4,128]{2,1,0:T(4,128)S(1)}, u32[]{:S(2)}, u32[]{:S(2)}) collective-permute-start(f32[14,4,128]{2,1,0:T(4,128)S(1)} %get-tuple-element.70), channel_id=1, source_target_pairs={{0,4},{1,2},{2,1},{3,7},{4,0},{5,6},{6,5},{7,3},{8,12},{9,10},{10,... | collective-permute-start | bytes 86024 | tf_op jit(solution)/shard_map/ppermute | solution.py:494
  23.7 4.0 %collective-permute-start.8 = (f32[16,128]{1,0:T(8,128)S(1)}, f32[16,128]{1,0:T(8,128)S(1)}, u32[]{:S(2)}, u32[]{:S(2)}) collective-permute-start(f32[16,128]{1,0:T(8,128)S(1)} %get-tuple-element.76), channel_id=1, source_target_pairs={{4,8},{8,4},{12,16},{16,12},{20,24},{24,20},{28,0},{0,28},{5,9},{9... | collective-permute-start | bytes 24584 | tf_op jit(solution)/shard_map/ppermute | solution.py:483
  24.9 2.8 %collective-permute-start.9 = (f32[16,128]{1,0:T(8,128)S(1)}, f32[16,128]{1,0:T(8,128)S(1)}, u32[]{:S(2)}, u32[]{:S(2)}) collective-permute-start(f32[16,128]{1,0:T(8,128)S(1)} %get-tuple-element.77), channel_id=1, source_target_pairs={{0,4},{4,0},{8,12},{12,8},{16,20},{20,16},{24,28},{28,24},{1,5},{5... | collective-permute-start | bytes 24584 | tf_op jit(solution)/shard_map/ppermute | solution.py:483

commit v6 on v5

--- a/solution.py
+++ b/solution.py
@@ -65,14 +65,10 @@
     return lax.axis_index(axis) % 2
 
 
-def pack_kernel(gas, *refs):
-    small = (len(refs) - 3) // 2
-    sources, (on, off), targets = refs[:small], refs[small : small + 2], refs[small + 2 : -1]
-    sems = refs[-1]
+def pack_kernel(gas, off, on, sems):
     last = gas.shape[1] - 1
     flip = odd("azim")
     pairs = [(gas.at[:, last * flip], off), (gas.at[:, last * (1 - flip)], on)]
-    pairs += list(zip(sources, targets))
     copies = [pltpu.make_async_copy(src, dst, sems.at[k]) for k, (src, dst) in enumerate(pairs)]
     for copy in copies:
         copy.start()
@@ -339,9 +335,11 @@
     nf, ca, cr, cz = gas.shape
     host = parcels[HOST : HOST + 1, :reach].astype(jnp.int32)
     deposit_all(source, host, hots, gas.shape, reach, total)
-    for f, a, terms in inner_terms(gas, table, tanh, range(ca)):
+    for f, a, terms in inner_terms(gas, table, tanh, range(ca - 1)):
         terms += total[f * cr : (f + 1) * cr, a * cz : (a + 1) * cz]
         out[f, a] = 0.5 * (old_gas[f, a] + gas[f, a] + DT * terms)
+    for f in range(nf):
+        out[f, ca - 1] = total[f * cr : (f + 1) * cr, (ca - 1) * cz :]
 
 
 def parcel_work(gas, host, attr, live, table, parcels, cells, hots, probed):
@@ -434,9 +432,11 @@
     parcels[LIVE : LIVE + 1, :slots] = jnp.where(gone, 0.0, parcels[LIVE : LIVE + 1, :slots])
 
 
-def finish_kernel(table, base, gas, off, on, near, far, sources, out):
+def finish_kernel(table, base, gas, off, on, near, far, sources, middle, out, tanh):
     nf, ca, cr, cz = out.shape
-    out[...] = base[...]
+    out[:, : ca - 1] = base[:, : ca - 1]
+    for f, a, terms in inner_terms(middle, table, tanh, (ca - 1,)):
+        out[f, a] = 0.5 * (gas[f, a] + middle[f, a] + DT * (terms + base[f, a]))
     for f in range(nf):
         west, east = sides(on[f * cr : (f + 1) * cr], off[f * cr : (f + 1) * cr])
         west += (DT * spread(table, EAST, f, cr)) * gas[f, 0]
@@ -504,22 +504,22 @@
     ring, pack = shape((nf, ca, cz)), shape((ROWS, width))
     tile = shape((8, LANES))
     grid, slotted = shape(gas.shape), shape((ROWS, padded))
-    small = (transport, chemistry, evap.reshape(1, nf), source_map.T, mass, state, host, crossing)
-    on, off, *small = call(
+    evap, source_map = evap.reshape(1, nf), source_map.T
+    off, on = call(
         pack_kernel,
-        [shape((nf, cr, cz)), shape((nf, cr, cz))] + [shape(v.shape, v.dtype) for v in small],
-        [HBM] * (1 + len(small)),
-        [VMEM] * (2 + len(small)),
-        tuple(pltpu.with_memory_space_constraint(v, pltpu.HBM) for v in (gas,) + small),
-        scratch=[pltpu.SemaphoreType.DMA((2 + len(small),))],
+        [shape((nf, cr, cz)), shape((nf, cr, cz))],
+        [HBM],
+        [VMEM] * 2,
+        (pltpu.with_memory_space_constraint(gas, pltpu.HBM),),
+        scratch=[pltpu.SemaphoreType.DMA((2,))],
         flops=5_000_000_000,
         moved=2_000_000,
     )
-    transport, chemistry, evap, source_map, mass, state, host, crossing = small
+    packed = off
     off = swap(off.reshape(nf * cr, cz), "azim", 1)
     on = swap(on.reshape(nf * cr, cz), "azim", 0)
 
-    near, far = call(rows_kernel, [ring, ring], [VMEM] * 2, [VMEM] * 2, (gas, transport), moved=100_000)
+    near, far = call(rows_kernel, [ring, ring], [VMEM] * 2, [VMEM] * 2, (gas, packed), moved=100_000)
     near = swap_rows(near, 0)
     far = swap_rows(far, 1)
     hots, lhot = shape((ca * cz, slots), BF16), shape((2 * width, slots), BF16)
@@ -602,9 +602,10 @@
     gas_next = call(
         finish_kernel,
         shape(gas.shape),
-        [VMEM] * 8,
+        [VMEM] * 9,
         VMEM,
-        (table, base, gas, off, on, near, far, sources),
+        (table, base, gas, off, on, near, far, sources, section_one),
+        scratch=[tanh_scratch],
         flops=100_000_000,
         moved=3_000_000,
     )

time: 28.8 us -> 28.7 us (level)
  transfers between devices with their start and end apart: 10 -> 10, of which waited for: 2 -> 2; matrix products, arithmetic and copies ran while one was open for 0% -> 0% of each run, Pallas kernels for 47% -> 48%
where the time goes in v6:
time: 28.7 us; the launch traced here: 28.5 us
  Pallas kernels  15.7 us (55%)
  starting transfers between devices  9.29 us (32%)
  waiting for transfers between devices  1.85 us (6%)
  between operations  1.52 us (5%)
    pallas_call x11, Pallas kernels, call(): pl.pallas_call(kernel, out_shape=outs, in_specs=ins, out_specs=out_specs,...  15.7 us
    ppermute x4, starting transfers between devices, swap_rows(): return lax.ppermute(array, ('azim', 'radax'), pairs)  4.79 us
    ppermute x6, starting transfers between devices, swap(): return lax.ppermute(array, axis, pairs)  4.51 us
    ppermute x6, waiting for transfers between devices, swap(): return lax.ppermute(array, axis, pairs)  1.84 us
  transfers between devices with their start and end apart: 10, of which 2 were waited for; matrix products, arithmetic and copies ran while one was open for 0% of the time, Pallas kernels for 48%

profile of v6, /device:TPU:0, one launch (start us, length us, event | category | flops | bytes accessed | tf_op | source)
XLA Modules:
  0.0 28.5 jit_solution(14951169722066303910)
XLA Ops:
  0.6 0.0 copy-start
  0.6 0.0 copy-start.8
  0.7 0.0 copy-start.6
  0.7 0.0 copy-start.7
  0.7 0.0 copy-start.3
  0.7 0.0 copy-start.4
  0.7 0.0 copy-start.2
  0.7 0.0 copy-start.5
  0.7 0.0 copy-start.1
  0.7 1.1 %shard_map.139 = (f32[14,32,128]{2,1,0:T(8,128)S(1)}, f32[14,32,128]{2,1,0:T(8,128)S(1)}) custom-call(f32[14,4,32,128]{3,2,1,0:T(8,128)} %gas.11), custom_call_target="tpu_custom_call" | custom-call | flops 5000000000 | bytes 2000000 | tf_op jit(solution)/shard_map/pallas_call | solution.py:48
  1.9 0.2 copy-done
  2.1 0.5 %collective-permute-start.2 = (f32[14,4,128]{2,1,0:T(4,128)S(1)}, f32[14,4,128]{2,1,0:T(4,128)S(1)}, u32[]{:S(2)}, u32[]{:S(2)}) collective-permute-start(f32[14,4,128]{2,1,0:T(4,128)S(1)} %get-tuple-element.44), channel_id=1, source_target_pairs={{0,4},{1,2},{2,1},{3,7},{4,0},{5,6},{6,5},{7,3},{8,12},{9,10},{10,... | collective-permute-start | bytes 86024 | tf_op jit(solution)/shard_map/ppermute | solution.py:494
  2.6 4.1 %collective-permute-start.3 = (f32[14,4,128]{2,1,0:T(4,128)S(1)}, f32[14,4,128]{2,1,0:T(4,128)S(1)}, u32[]{:S(2)}, u32[]{:S(2)}) collective-permute-start(f32[14,4,128]{2,1,0:T(4,128)S(1)} %get-tuple-element.45), channel_id=1, source_target_pairs={{0,1},{1,0},{2,3},{3,2},{4,5},{5,4},{6,7},{7,6},{8,9},{9,8},{10,11... | collective-permute-start | bytes 86024 | tf_op jit(solution)/shard_map/ppermute | solution.py:494
  6.8 1.3 %collective-permute-start = (f32[448,128]{1,0:T(8,128)S(1)}, f32[448,128]{1,0:T(8,128)S(1)}, u32[]{:S(2)}, u32[]{:S(2)}) collective-permute-start(f32[448,128]{1,0:T(8,128)S(1)} %bitcast.4), channel_id=1, source_target_pairs={{4,8},{8,4},{12,16},{16,12},{20,24},{24,20},{28,0},{0,28},{5,9},{9... | collective-permute-start | bytes 688136 | tf_op jit(solution)/shard_map/ppermute | solution.py:483
  8.1 0.3 collective-permute-start.1
  9.0 0.0 copy-done.8
  9.0 0.0 copy-done.6
  9.0 0.0 copy-done.7
  9.0 0.0 copy-done.3
  9.1 0.0 copy-done.4
  9.1 0.0 copy-done.2
  9.1 0.0 copy-done.5
  9.1 0.0 copy-done.1
  9.1 2.8 %shard_map.137 = (f32[16,2304]{1,0:T(8,128)S(1)}, f32[16,128]{1,0:T(8,128)S(1)}, f32[16,128]{1,0:T(8,128)S(1)}, f32[28,16,128]{2,1,0:T(8,128)S(1)}, bf16[512,204...) custom-call(s32[1,1]{1,0:T(1,128)S(6)} %copy.15.count, f32[14,4,32,128]{3,2,1,0:T(8,128)S(1)} %copy-done, ...), custom_call_target="tpu_custom_call" | custom-call | flops 3000000000 | bytes 2000000 | tf_op jit(solution)/shard_map/pallas_call | solution.py:48
  11.9 2.2 %shard_map.138 = (f32[14,2,32,128]{3,2,1,0:T(8,128)S(1)}, f32[448,512]{1,0:T(8,128)S(1)}) custom-call(f32[14,4,32,128]{3,2,1,0:T(8,128)S(1)} %copy-done, f32[28,16,128]{2,1,0:T(8,128)S(1)} %get-tuple-element.36.table, f32[16,2304]{1,0:T(8,128)S(1)} %get-tuple-element.37.parcels.old, bf16[512,2048]{1,0:T(8,128)(2,1)S(1)} %get-tuple-element.38.hots, ...), custom_call_target="tpu_custom_call" | custom-call | flops 1000000 | bytes 10000 | tf_op jit(solution)/shard_map/pallas_call | solution.py:48
  14.1 0.0 collective-permute-done.2.far
  14.1 0.0 collective-permute-done.3.near
  14.1 0.1 shard_map.144
  14.2 1.1 %collective-permute-start.4 = (f32[464,128]{1,0:T(8,128)S(1)}, f32[464,128]{1,0:T(8,128)S(1)}, u32[]{:S(2)}, u32[]{:S(2)}) collective-permute-start(f32[464,128]{1,0:T(8,128)S(1)} %get-tuple-element.51), channel_id=1, source_target_pairs={{4,8},{8,4},{12,16},{16,12},{20,24},{24,20},{28,0},{0,28},{5,9},{9... | collective-permute-start | bytes 712712 | tf_op jit(solution)/shard_map/ppermute | solution.py:483
  15.3 0.6 %collective-permute-start.5 = (f32[464,128]{1,0:T(8,128)S(1)}, f32[464,128]{1,0:T(8,128)S(1)}, u32[]{:S(2)}, u32[]{:S(2)}) collective-permute-start(f32[464,128]{1,0:T(8,128)S(1)} %get-tuple-element.52), channel_id=1, source_target_pairs={{0,4},{4,0},{8,12},{12,8},{16,20},{20,16},{24,28},{28,24},{1,5},{5... | collective-permute-start | bytes 712712 | tf_op jit(solution)/shard_map/ppermute | solution.py:483
  15.9 0.0 collective-permute-done.off
  15.9 0.0 collective-permute-done.1.on
  15.9 1.0 %shard_map.141.gas.middle = f32[14,4,32,128]{3,2,1,0:T(8,128)S(1)} custom-call(f32[14,4,32,128]{3,2,1,0:T(8,128)S(1)} %copy-done, f32[28,16,128]{2,1,0:T(8,128)S(1)} %get-tuple-element.36.table, f32[14,2,32,128]{3,2,1,0:T(8,128)S(1)} %get-tuple-element.40.outer, f32[448,512]{1,0:T(8,128)S(1)} %get-tuple-element.41.total, ...), custom_call_target="tpu_custom_call" | custom-call | flops 3000000000 | bytes 2000000 | tf_op jit(solution)/shard_map/pallas_call | solution.py:48
  17.0 2.8 %shard_map.142 = (f32[14,4,128]{2,1,0:T(4,128)S(1)}, f32[14,4,128]{2,1,0:T(4,128)S(1)}, f32[16,2304]{1,0:T(8,128)S(1)}, bf16[512,2048]{1,0:T(8,128)(2,1)S(1)}, f...) custom-call(f32[14,4,32,128]{3,2,1,0:T(8,128)S(1)} %shard_map.141.gas.middle, ...), custom_call_target="tpu_custom_call" | custom-call | flops 1000000 | bytes 10000 | tf_op jit(solution)/shard_map/pallas_call | solution.py:48
  19.7 0.1 collective-permute-start.6
  19.8 0.1 collective-permute-start.7
  19.9 2.4 %shard_map.143.base = f32[14,4,32,128]{3,2,1,0:T(8,128)S(1)} custom-call(f32[14,4,32,128]{3,2,1,0:T(8,128)S(1)} %shard_map.141.gas.middle, f32[28,16,128]{2,1,0:T(8,128)S(1)} %get-tuple-element.36.table, f32[14,4,32,128]{3,2,1,0:T(8,128)S(1)} %copy-done, f32[16,2304]{1,0:T(8,128)S(1)} %get-tuple-element.46.parcels.old, ...), custom_call_target="tpu_custom_call" | custom-call | flops 1000000 | bytes 10000 | tf_op jit(solution)/shard_map/pallas_call | solution.py:48
  22.2 0.8 %collective-permute-done.4.off = f32[464,128]{1,0:T(8,128)S(1)} collective-permute-done((f32[464,128]{1,0:T(8,128)S(1)}, f32[464,128]{1,0:T(8,128)S(1)}, u32[]{:S(2)}, u32[]{:S(2)}) %collective-permute-start.4) | collective-permute-done | bytes 237600 | tf_op jit(solution)/shard_map/ppermute | solution.py:483
  23.0 0.0 collective-permute-done.5.on
  23.0 0.6 %shard_map.145 = (f32[16,2304]{1,0:T(8,128)S(1)}, f32[16,128]{1,0:T(8,128)S(1)}, f32[16,128]{1,0:T(8,128)S(1)}, f32[2,16,128]{2,1,0:T(8,128)S(1)}, f32[8,128]{1,0:T(8,128)S(1)}) custom-call(f32[8,128]{1,0:T(8,128)S(1)} %get-tuple-element.55.count, f32[14,4,32,128]{3,2,1,0:T(8,128)S(1)} %shard_map.141.gas.middle, f32[28,16,128]{2,1,0:T(8,128)S(1)} %get-tuple-element.36.table, ...), custom_call_target="tpu_custom_call" | custom-call | flops 100000000 | bytes 2000000 | tf_op jit(solution)/shard_map/pallas_call | solution.py:48
  23.6 1.2 %collective-permute-start.8 = (f32[16,128]{1,0:T(8,128)S(1)}, f32[16,128]{1,0:T(8,128)S(1)}, u32[]{:S(2)}, u32[]{:S(2)}) collective-permute-start(f32[16,128]{1,0:T(8,128)S(1)} %get-tuple-element.60), channel_id=1, source_target_pairs={{4,8},{8,4},{12,16},{16,12},{20,24},{24,20},{28,0},{0,28},{5,9},{9... | collective-permute-start | bytes 24584 | tf_op jit(solution)/shard_map/ppermute | solution.py:483
  24.9 0.0 collective-permute-start.9
  24.9 0.0 collective-permute-done.6.near
  24.9 0.0 collective-permute-done.7.far
  24.9 1.8 %shard_map.146 = f32[14,4,32,128]{3,2,1,0:T(8,128)} custom-call(f32[28,16,128]{2,1,0:T(8,128)S(1)} %get-tuple-element.36.table, f32[14,4,32,128]{3,2,1,0:T(8,128)S(1)} %shard_map.143.base, f32[14,4,32,128]{3,2,1,0:T(8,128)S(1)} %copy-done, f32[464,128]{1,0:T(8,128)S(1)} %collective-permute-done.4.off, f32[464,128]{1,0:T(8,128)S(1)} %collective-permute-done.5.on, ...), custom_call_target="tpu_custom_call" | custom-call | flops 100000000 | bytes 3000000 | tf_op jit(solution)/shard_map/pallas_call | solution.py:48
  26.7 1.0 %collective-permute-done.8.off = f32[16,128]{1,0:T(8,128)S(1)} collective-permute-done((f32[16,128]{1,0:T(8,128)S(1)}, f32[16,128]{1,0:T(8,128)S(1)}, u32[]{:S(2)}, u32[]{:S(2)}) %collective-permute-start.8) | collective-permute-done | bytes 8224 | tf_op jit(solution)/shard_map/ppermute | solution.py:483
  27.7 0.0 collective-permute-done.9.on
  27.7 0.9 %shard_map.147 = (f32[1,1,2048]{2,1,0:T(1,128)}, f32[7,1,1,2048]{3,2,1,0:T(1,128)}, s32[1,1,2048]{2,1,0:T(1,128)}, s32[1,1]{1,0:T(1,128)}) custom-call(f32[8,128]{1,0:T(8,128)S(1)} %get-tuple-element.59.count, f32[16,128]{1,0:T(8,128)S(1)} %collective-permute-done.8.off, f32[16,128]{1,0:T(8,128)S(1)} %collective-permute-done.9.on, ...), custom_call_target="tpu_custom_call" | custom-call | bytes 500000 | tf_op jit(solution)/shard_map/pallas_call | solution.py:48
  (1 shorter events, 0.0 us)
Async XLA Ops:
  0.6 1.4 %copy-start = (f32[14,4,32,128]{3,2,1,0:T(8,128)S(1)}, f32[14,4,32,128]{3,2,1,0:T(8,128)}, u32[]{:S(2)}) copy-start(f32[14,4,32,128]{3,2,1,0:T(8,128)} %gas.11) | copy-start | bytes 2752516
  0.6 8.4 %copy-start.8 = (f32[14]{0:T(128)S(1)}, f32[14]{0:T(128)}, u32[]{:S(2)}) copy-start(f32[14]{0:T(128)} %param.13) | copy-start | bytes 172
  0.7 8.4 %copy-start.6 = (f32[14,8]{0,1:T(8,128)S(1)}, f32[14,8]{0,1:T(8,128)}, u32[]{:S(2)}) copy-start(f32[14,8]{0,1:T(8,128)} %param.14) | copy-start | bytes 1348
  0.7 8.4 %copy-start.7 = (f32[3,14]{1,0:T(4,128)S(1)}, f32[3,14]{1,0:T(4,128)}, u32[]{:S(2)}) copy-start(f32[3,14]{1,0:T(4,128)} %transport.1) | copy-start | bytes 508
  0.7 8.4 %copy-start.3 = (f32[14,14]{1,0:T(8,128)S(1)}, f32[14,14]{1,0:T(8,128)}, u32[]{:S(2)}) copy-start(f32[14,14]{1,0:T(8,128)} %chemistry.1) | copy-start | bytes 2356
  0.7 8.4 %copy-start.4 = (f32[1,1,2048]{2,1,0:T(1,128)S(1)}, f32[1,1,2048]{2,1,0:T(1,128)}, u32[]{:S(2)}) copy-start(f32[1,1,2048]{2,1,0:T(1,128)} %mass.1) | copy-start | bytes 24580
  0.7 8.4 %copy-start.2 = (f32[7,1,1,2048]{3,2,1,0:T(1,128)S(1)}, f32[7,1,1,2048]{3,2,1,0:T(1,128)}, u32[]{:S(2)}) copy-start(f32[7,1,1,2048]{3,2,1,0:T(1,128)} %state.1) | copy-start | bytes 172036
  0.7 8.4 %copy-start.5 = (s32[1,1,2048]{2,1,0:T(1,128)S(1)}, s32[1,1,2048]{2,1,0:T(1,128)}, u32[]{:S(2)}) copy-start(s32[1,1,2048]{2,1,0:T(1,128)} %host_in.1) | copy-start | bytes 24580
  0.7 8.4 %copy-start.1 = (s32[1,1,2,2,128]{4,3,2,1,0:T(2,128)S(1)}, s32[1,1,2,2,128]{4,3,2,1,0:T(2,128)}, u32[]{:S(2)}) copy-start(s32[1,1,2,2,128]{4,3,2,1,0:T(2,128)} %lists.5) | copy-start | bytes 6148
  2.1 12.0 %collective-permute-start.2 = (f32[14,4,128]{2,1,0:T(4,128)S(1)}, f32[14,4,128]{2,1,0:T(4,128)S(1)}, u32[]{:S(2)}, u32[]{:S(2)}) collective-permute-start(f32[14,4,128]{2,1,0:T(4,128)S(1)} %get-tuple-element.44), channel_id=1, source_target_pairs={{0,4},{1,2},{2,1},{3,7},{4,0},{5,6},{6,5},{7,3},{8,12},{9,10},{10,... | collective-permute-start | bytes 86024 | tf_op jit(solution)/shard_map/ppermute | solution.py:494
  2.6 11.5 %collective-permute-start.3 = (f32[14,4,128]{2,1,0:T(4,128)S(1)}, f32[14,4,128]{2,1,0:T(4,128)S(1)}, u32[]{:S(2)}, u32[]{:S(2)}) collective-permute-start(f32[14,4,128]{2,1,0:T(4,128)S(1)} %get-tuple-element.45), channel_id=1, source_target_pairs={{0,1},{1,0},{2,3},{3,2},{4,5},{5,4},{6,7},{7,6},{8,9},{9,8},{10,11... | collective-permute-start | bytes 86024 | tf_op jit(solution)/shard_map/ppermute | solution.py:494
  6.8 9.2 %collective-permute-start = (f32[448,128]{1,0:T(8,128)S(1)}, f32[448,128]{1,0:T(8,128)S(1)}, u32[]{:S(2)}, u32[]{:S(2)}) collective-permute-start(f32[448,128]{1,0:T(8,128)S(1)} %bitcast.4), channel_id=1, source_target_pairs={{4,8},{8,4},{12,16},{16,12},{20,24},{24,20},{28,0},{0,28},{5,9},{9... | collective-permute-start | bytes 688136 | tf_op jit(solution)/shard_map/ppermute | solution.py:483
  8.1 7.8 %collective-permute-start.1 = (f32[448,128]{1,0:T(8,128)S(1)}, f32[448,128]{1,0:T(8,128)S(1)}, u32[]{:S(2)}, u32[]{:S(2)}) collective-permute-start(f32[448,128]{1,0:T(8,128)S(1)} %bitcast.5), channel_id=1, source_target_pairs={{0,4},{4,0},{8,12},{12,8},{16,20},{20,16},{24,28},{28,24},{1,5},{5... | collective-permute-start | bytes 688136 | tf_op jit(solution)/shard_map/ppermute | solution.py:483
  14.2 8.8 %collective-permute-start.4 = (f32[464,128]{1,0:T(8,128)S(1)}, f32[464,128]{1,0:T(8,128)S(1)}, u32[]{:S(2)}, u32[]{:S(2)}) collective-permute-start(f32[464,128]{1,0:T(8,128)S(1)} %get-tuple-element.51), channel_id=1, source_target_pairs={{4,8},{8,4},{12,16},{16,12},{20,24},{24,20},{28,0},{0,28},{5,9},{9... | collective-permute-start | bytes 712712 | tf_op jit(solution)/shard_map/ppermute | solution.py:483
  15.3 7.7 %collective-permute-start.5 = (f32[464,128]{1,0:T(8,128)S(1)}, f32[464,128]{1,0:T(8,128)S(1)}, u32[]{:S(2)}, u32[]{:S(2)}) collective-permute-start(f32[464,128]{1,0:T(8,128)S(1)} %get-tuple-element.52), channel_id=1, source_target_pairs={{0,4},{4,0},{8,12},{12,8},{16,20},{20,16},{24,28},{28,24},{1,5},{5... | collective-permute-start | bytes 712712 | tf_op jit(solution)/shard_map/ppermute | solution.py:483
  19.7 5.1 %collective-permute-start.6 = (f32[14,4,128]{2,1,0:T(4,128)S(1)}, f32[14,4,128]{2,1,0:T(4,128)S(1)}, u32[]{:S(2)}, u32[]{:S(2)}) collective-permute-start(f32[14,4,128]{2,1,0:T(4,128)S(1)} %get-tuple-element.53), channel_id=1, source_target_pairs={{0,1},{1,0},{2,3},{3,2},{4,5},{5,4},{6,7},{7,6},{8,9},{9,8},{10,11... | collective-permute-start | bytes 86024 | tf_op jit(solution)/shard_map/ppermute | solution.py:494
  19.8 5.1 %collective-permute-start.7 = (f32[14,4,128]{2,1,0:T(4,128)S(1)}, f32[14,4,128]{2,1,0:T(4,128)S(1)}, u32[]{:S(2)}, u32[]{:S(2)}) collective-permute-start(f32[14,4,128]{2,1,0:T(4,128)S(1)} %get-tuple-element.54), channel_id=1, source_target_pairs={{0,4},{1,2},{2,1},{3,7},{4,0},{5,6},{6,5},{7,3},{8,12},{9,10},{10,... | collective-permute-start | bytes 86024 | tf_op jit(solution)/shard_map/ppermute | solution.py:494
  23.6 4.0 %collective-permute-start.8 = (f32[16,128]{1,0:T(8,128)S(1)}, f32[16,128]{1,0:T(8,128)S(1)}, u32[]{:S(2)}, u32[]{:S(2)}) collective-permute-start(f32[16,128]{1,0:T(8,128)S(1)} %get-tuple-element.60), channel_id=1, source_target_pairs={{4,8},{8,4},{12,16},{16,12},{20,24},{24,20},{28,0},{0,28},{5,9},{9... | collective-permute-start | bytes 24584 | tf_op jit(solution)/shard_map/ppermute | solution.py:483
  24.9 2.8 %collective-permute-start.9 = (f32[16,128]{1,0:T(8,128)S(1)}, f32[16,128]{1,0:T(8,128)S(1)}, u32[]{:S(2)}, u32[]{:S(2)}) collective-permute-start(f32[16,128]{1,0:T(8,128)S(1)} %get-tuple-element.61), channel_id=1, source_target_pairs={{0,4},{4,0},{8,12},{12,8},{16,20},{20,16},{24,28},{28,24},{1,5},{5... | collective-permute-start | bytes 24584 | tf_op jit(solution)/shard_map/ppermute | solution.py:483
